TPU v7x, 32 devices: a whole 2x2x4 slice. The times are simulated.
32 devices in a mesh: grp: 2 (over x), seq: 16 (over z, y, core).
Axes of the slice: x: 2, y: 2, z: 4, core: 2. Of those that a mesh axis runs over, the one named last changes fastest.
Arguments:
- alignment: bfloat16 [128, 512, 768], P(('grp', 'seq')), parts along dimension 0, may hold values from -350 to 350
- depth_count: int32 [2], P('grp'), parts along dimension 0, may hold values from 16 to 64
- qkv_weight: bfloat16 [768, 2304], replicated, may hold values from -0.21650635 to 0.21650635
- pair_weight: bfloat16 [64, 12], replicated, may hold values from -1.75 to 1.75
- conv_weight: bfloat16 [4, 9, 64, 64], replicated, may hold values from -0.25 to 0.25
- head_weight: float32 [64], replicated, may hold values from -0.75 to 0.75
Outputs:
- row_mix: bfloat16 [128, 512, 768], P(('grp', 'seq')), parts along dimension 0
- contacts: float32 [1024, 512], P(('grp', 'seq')), parts along dimension 0
There are 2 independent parts, one for each index of `grp`. A program takes and returns all parts, laid end to end along the dimension named above; an argument that names none is the same for every part. Nothing has to cross between parts.
Inputs may be any that keep to these rules, and one draw needn't show every extreme that they name: Sequences of alignment from index depth_count on are padding and take no part in the scores.
All inputs are finite; a program needn't handle non-finite values.
Results may differ from a plain program's by a relative error of at most 0.014.
Values may be sent and summed in bfloat16 or wider, within the bound.
No kernel may reach another device: no remote copies, remote signals or barrier semaphores. Data moves between devices by JAX's collectives and lax.ppermute only.
A program may use at most 192 MiB of HBM per device.

v0:
```python
import functools
import math

import jax
import jax.numpy as jnp
from jax import lax
from jax.experimental import pallas as pl
from jax.experimental.pallas import tpu as pltpu
from jax.sharding import PartitionSpec as P

EPSILON = 1e-05
LINK_SCALE = 2.0**-7


def grid_of(chips):
    width = 1
    while (2 * width) ** 2 <= chips:
        width *= 2
    return chips // width, width


def head_major(values, seqs, rows, size):
    out = []
    for head in range(values.shape[1] // size):
        pieces = [
            values[seq * rows : (seq + 1) * rows, head * size : (head + 1) * size]
            for seq in range(seqs)
        ]
        out.append(jnp.concatenate(pieces, axis=1))
    return out


def norm_send_kernel(half_ref, use_ref, x_ref, wq_ref, wk_ref, normed_ref, qk_ref):
    seqs, rows, width = x_ref.shape
    size = qk_ref.shape[3] // seqs
    values = x_ref[...].reshape(seqs * rows, width).astype(jnp.float32)
    average = jnp.mean(values, axis=-1, keepdims=True)
    centered = values - average
    variance = jnp.mean(centered * centered, axis=-1, keepdims=True)
    normed = (centered * lax.rsqrt(variance + EPSILON)).astype(jnp.bfloat16)
    normed_ref[...] = normed.reshape(seqs, rows, width)
    project(use_ref, normed, wq_ref, wk_ref, qk_ref, seqs, rows, size)


def own_kernel(half_ref, use_ref, normed_ref, wq_ref, wk_ref, qk_ref):
    seqs, rows, width = normed_ref.shape
    size = qk_ref.shape[3] // seqs
    normed = normed_ref[...].reshape(seqs * rows, width)
    project(use_ref, normed, wq_ref, wk_ref, qk_ref, seqs, rows, size)


def project(use_ref, normed, wq_ref, wk_ref, qk_ref, seqs, rows, size):
    q = jnp.dot(normed, wq_ref[...], preferred_element_type=jnp.float32).astype(jnp.bfloat16)
    for head, block in enumerate(head_major(q, seqs, rows, size)):
        lane = lax.broadcasted_iota(jnp.int32, block.shape, 1)
        qk_ref[0, head] = jnp.where(lane < use_ref[0] * size, block, jnp.zeros_like(block))
    k = jnp.dot(normed, wk_ref[...], preferred_element_type=jnp.float32).astype(jnp.bfloat16)
    for head, block in enumerate(head_major(k, seqs, rows, size)):
        qk_ref[1, head] = block


def value_kernel(normed_ref, w_ref, v_ref):
    seqs, rows, width = normed_ref.shape
    size = v_ref.shape[2] // seqs
    normed = normed_ref[...].reshape(seqs * rows, width)
    v = jnp.dot(normed, w_ref[...], preferred_element_type=jnp.float32).astype(jnp.bfloat16)
    for head, block in enumerate(head_major(v, seqs, rows, size)):
        v_ref[head] = block


def score_kernel(order_ref, scale_ref, own_ref, other_ref, s_ref):
    chips, _, rows, _ = s_ref.shape
    total = None
    for ref in (own_ref, other_ref):
        q = jnp.concatenate(
            [
                ref[0, 0, pl.ds(pl.multiple_of(order_ref[chip] * rows, rows), rows), :]
                for chip in range(chips)
            ],
            axis=0,
        )
        part = lax.dot_general(
            q, ref[1, 0], (((1,), (1,)), ((), ())), preferred_element_type=jnp.float32
        )
        total = part if total is None else total + part
    total = total * scale_ref[0]
    s_ref[...] = total.reshape(chips, 1, rows, total.shape[1])


def mix_kernel(p_ref, v_ref, o_ref):
    seqs = o_ref.shape[0]
    size = v_ref.shape[2] // seqs
    mixed = []
    for head in range(v_ref.shape[0]):
        probs = p_ref[0, :, head]
        probs = probs.reshape(probs.shape[0] * probs.shape[1], probs.shape[2])
        mixed.append(
            jnp.dot(probs, v_ref[head], preferred_element_type=jnp.float32).astype(jnp.bfloat16)
        )
    for seq in range(seqs):
        o_ref[seq] = jnp.concatenate(
            [block[:, seq * size : (seq + 1) * size] for block in mixed], axis=1
        )


def cost(flops, moved):
    return pl.CostEstimate(flops=int(flops), bytes_accessed=int(moved), transcendentals=0)


def projections(alignment, qkv_weight, half, use, head_count):
    seqs, residues, features = alignment.shape
    heads = head_count // 2
    size = features // head_count
    rows = 128 if residues % 128 == 0 else residues
    cols = heads * size
    steps = residues // rows
    bf16 = jnp.bfloat16
    x_spec = pl.BlockSpec((seqs, rows, features), lambda i, *_: (0, i, 0))
    qk_spec = pl.BlockSpec((2, heads, rows, seqs * size), lambda i, *_: (0, 0, i, 0))
    qk_shape = jax.ShapeDtypeStruct((2, heads, residues, seqs * size), bf16)
    params = pltpu.CompilerParams(vmem_limit_bytes=48 << 20)

    def weight_specs(pick):
        return [
            pl.BlockSpec((features, cols), lambda i, half, use: (0, pick(half[0]))),
            pl.BlockSpec((features, cols), lambda i, half, use: (0, 2 + pick(half[0]))),
        ]

    flops = 4 * seqs * residues * features * cols
    moved = 2 * (seqs * residues * features + 2 * features * cols + 2 * seqs * residues * cols)
    normed, sent = pl.pallas_call(
        norm_send_kernel,
        out_shape=(jax.ShapeDtypeStruct(alignment.shape, bf16), qk_shape),
        grid_spec=pltpu.PrefetchScalarGridSpec(
            num_scalar_prefetch=2,
            grid=(steps,),
            in_specs=[x_spec] + weight_specs(lambda half: 1 - half),
            out_specs=[x_spec, qk_spec],
        ),
        compiler_params=params,
        cost_estimate=cost(flops, moved + 2 * alignment.size),
        name="norm_send",
    )(half, use, alignment, qkv_weight, qkv_weight)
    own = pl.pallas_call(
        own_kernel,
        out_shape=qk_shape,
        grid_spec=pltpu.PrefetchScalarGridSpec(
            num_scalar_prefetch=2,
            grid=(steps,),
            in_specs=[x_spec] + weight_specs(lambda half: half),
            out_specs=qk_spec,
        ),
        compiler_params=params,
        cost_estimate=cost(flops, moved),
        name="own_project",
    )(half, use, normed, qkv_weight, qkv_weight)
    values = pl.pallas_call(
        value_kernel,
        out_shape=jax.ShapeDtypeStruct((head_count, residues, seqs * size), bf16),
        grid=(steps,),
        in_specs=[
            pl.BlockSpec((seqs, rows, features), lambda i: (0, i, 0)),
            pl.BlockSpec((features, features), lambda i: (0, 2)),
        ],
        out_specs=pl.BlockSpec((head_count, rows, seqs * size), lambda i: (0, i, 0)),
        compiler_params=params,
        cost_estimate=cost(flops, moved),
        name="value_project",
    )(normed, qkv_weight)
    return sent, own, values


def scores_of(own, other, order, scale, chips):
    _, heads, residues, inner = own.shape
    rows = residues // chips
    spec = pl.BlockSpec((2, 1, residues, inner), lambda h, *_: (0, h, 0, 0))
    return pl.pallas_call(
        score_kernel,
        out_shape=jax.ShapeDtypeStruct((chips, heads, rows, residues), jnp.float32),
        grid_spec=pltpu.PrefetchScalarGridSpec(
            num_scalar_prefetch=1,
            grid=(heads,),
            in_specs=[pl.BlockSpec(memory_space=pltpu.SMEM), spec, spec],
            out_specs=pl.BlockSpec((chips, 1, rows, residues), lambda h, *_: (0, h, 0, 0)),
        ),
        compiler_params=pltpu.CompilerParams(vmem_limit_bytes=32 << 20),
        cost_estimate=cost(4 * heads * residues * residues * inner, 4 * own.size + 4 * heads * residues**2),
        name="scores",
    )(order, scale, own, other)


def row_mix_of(probs, values, seqs, head_count):
    _, chips, heads, rows, residues = probs.shape
    inner = values.shape[2]
    size = inner // seqs
    pairs = heads // 2
    return pl.pallas_call(
        mix_kernel,
        out_shape=jax.ShapeDtypeStruct((seqs, residues, head_count * size), jnp.bfloat16),
        grid=(2 * pairs,),
        in_specs=[
            pl.BlockSpec((1, chips, 2, rows, residues), lambda g: (g // pairs, 0, g % pairs, 0, 0)),
            pl.BlockSpec((2, residues, inner), lambda g: (g, 0, 0)),
        ],
        out_specs=pl.BlockSpec((seqs, residues, 2 * size), lambda g: (0, 0, g)),
        compiler_params=pltpu.CompilerParams(vmem_limit_bytes=32 << 20),
        cost_estimate=cost(2 * probs.size * inner, 2 * (probs.size + 2 * values.size)),
        name="row_mix",
    )(probs, values)


class Links:
    def __init__(self):
        self.devices = lax.axis_size("seq")
        self.chips = self.devices // 2
        self.tall, self.wide = grid_of(self.chips)
        index = lax.axis_index("seq")
        self.index = index
        self.core = index % 2
        self.chip = index // 2
        self.z = self.chip // self.wide
        self.y = self.chip % self.wide

    def at(self, dz, dy):
        return (self.z + dz) % self.tall * self.wide + (self.y + dy) % self.wide

    def send(self, value, dz, dy, swap=False):
        pairs = []
        for source in range(self.devices):
            chip, core = divmod(source, 2)
            z, y = divmod(chip, self.wide)
            target = (z + dz) % self.tall * self.wide + (y + dy) % self.wide
            pairs.append((source, 2 * target + (1 - core if swap else core)))
        return lax.ppermute(value, "seq", pairs)


def reduce_scatter(links, scores):
    def piece(dz, dy):
        return scores[dz * links.wide + dy]

    half = jnp.float16
    far = sorted(range(links.tall), key=lambda dz: -min(dz, links.tall - dz))
    column = {}
    for dz in far:
        column[dz] = [
            links.send(piece(dz, dy).astype(half), 0, dy) for dy in range(1, links.wide)
        ]
    total = None
    for dz in far:
        summed = piece(dz, 0)
        for arrived in column[dz]:
            summed = summed + arrived.astype(jnp.float32)
        if dz:
            summed = links.send(summed.astype(half), dz, 0).astype(jnp.float32)
        total = summed if total is None else total + summed
    return total


def all_gather(links, own):
    gathered = jnp.zeros((2, links.chips) + own.shape, own.dtype)
    far = sorted(range(links.tall), key=lambda dz: -min(dz, links.tall - dz))
    zeros = (0,) * own.ndim
    pieces = []
    for dz in far:
        pieces.append((-dz, 0, links.send(own, dz, 0) if dz else own))
    pieces = pieces[-1:] + pieces[:-1]
    pieces += [
        (dz, -dy, links.send(value, 0, dy)) for dz, _, value in pieces for dy in range(1, links.wide)
    ]
    swapped = [links.send(value, 0, 0, swap=True) for _, _, value in pieces]
    for (dz, dy, value), other in zip(pieces, swapped):
        chip = links.at(dz, dy)
        gathered = lax.dynamic_update_slice(gathered, value[None, None], (links.core, chip) + zeros)
        gathered = lax.dynamic_update_slice(gathered, other[None, None], (1 - links.core, chip) + zeros)
    return gathered


ROWS = 4
REACH = {1: (0, 1, 2, 3, 4, -1), 2: (0, 1, 2, 3, -2, -1, 4, 5)}


def taps_kernel(w_ref, near_ref, far_ref):
    size = w_ref.shape[1]
    zero = jnp.zeros((size, size), w_ref.dtype)
    for dilation, out_ref in ((1, near_ref), (2, far_ref)):
        for which in range(2):
            base = 9 * (2 * (dilation - 1) + which)
            for col in range(3):
                for slot, row in enumerate(REACH[dilation]):
                    pieces = []
                    for out_row in range(ROWS):
                        step, rest = divmod(row - out_row, dilation)
                        live = rest == 0 and -1 <= step <= 1
                        pieces.append(w_ref[base + 3 * (step + 1) + col] if live else zero)
                    out_ref[which, col, slot * size : (slot + 1) * size, :] = jnp.concatenate(
                        pieces, axis=1
                    )


def contact_kernel(
    row_ref, pf_ref, pair_ref, near_ref, far_ref, head_ref, o_ref, u_ref, v_ref, hid_ref
):
    blocks, _, residues = pf_ref.shape
    lanes = pair_ref.shape[1]
    size = lanes // ROWS
    half = lanes // 2
    bf16 = jnp.bfloat16
    position = lax.broadcasted_iota(jnp.int32, (residues, lanes), 0)
    lane_row = lax.broadcasted_iota(jnp.int32, (1, lanes), 1) // size

    def masked(m, values):
        row = row_ref[0] + ROWS * (m - 2) + lane_row
        return jnp.where((row >= 0) & (row < residues), values, 0.0)

    def spread(ref, m, values, dilation):
        ref[1, m] = values.astype(bf16)
        left = jnp.where(position >= dilation, pltpu.roll(values, dilation, 0), 0.0)
        ref[0, m] = left.astype(bf16)
        right = jnp.where(
            position < residues - dilation, pltpu.roll(values, residues - dilation, 0), 0.0
        )
        ref[2, m] = right.astype(bf16)

    def conv(ref, m, w_ref, which, dilation):
        before = jnp.maximum(m - 1, 0)
        after = jnp.minimum(m + 1, blocks - 1)
        total = None
        for col in range(3):
            low = ref[col, before, :, half:]
            high = ref[col, after, :, :half]
            if dilation == 1:
                lane = lax.broadcasted_iota(jnp.int32, low.shape, 1)
                edge = [jnp.where(lane < size, high, low)]
            else:
                edge = [low, high]
            window = jnp.concatenate([ref[col, m]] + edge, axis=1)
            part = jnp.dot(window, w_ref[which, col], preferred_element_type=jnp.float32)
            total = part if total is None else total + part
        return total

    def start(m, carry):
        hidden = lax.dot_general(
            pf_ref[m], pair_ref[...], (((0,), (0,)), ((), ())), preferred_element_type=jnp.float32
        )
        hid_ref[m] = hidden
        spread(u_ref, m, hidden, 1)
        return carry

    lax.fori_loop(0, blocks, start, 0)

    def first(m, carry):
        inner = masked(m, jnp.maximum(conv(u_ref, m, near_ref, 0, 1), 0.0))
        spread(v_ref, m, inner, 1)
        return carry

    lax.fori_loop(0, blocks, first, 0)

    def second(m, carry):
        hidden = masked(m, hid_ref[m] + conv(v_ref, m, near_ref, 1, 1))
        hid_ref[m] = hidden
        spread(u_ref, m, hidden, 2)
        return carry

    lax.fori_loop(1, blocks - 1, second, 0)

    def third(m, carry):
        inner = masked(m, jnp.maximum(conv(u_ref, m, far_ref, 0, 2), 0.0))
        spread(v_ref, m, inner, 2)
        return carry

    lax.fori_loop(1, blocks - 1, third, 0)

    group = lax.broadcasted_iota(jnp.int32, (lanes, 128), 0) // size
    slot = lax.broadcasted_iota(jnp.int32, (lanes, 128), 1)

    def last(m, logits):
        hidden = hid_ref[m] + conv(v_ref, m, far_ref, 1, 2)
        weighed = hidden * head_ref[...]
        picks = jnp.where(slot == ROWS * (m - 2) + group, 1.0, 0.0).astype(bf16)
        for _ in range(3):
            coarse = weighed.astype(bf16)
            logits = logits + jnp.dot(coarse, picks, preferred_element_type=jnp.float32)
            weighed = weighed - coarse.astype(jnp.float32)
        return logits

    logits = lax.fori_loop(2, blocks - 2, last, jnp.zeros((residues, 128), jnp.float32))
    o_ref[...] = 1.0 / (1.0 + jnp.exp(-logits.T[: o_ref.shape[0]]))


def spread_taps(conv_weight):
    kinds, taps, size, _ = conv_weight.shape
    flipped = conv_weight.transpose(0, 1, 3, 2).reshape(kinds * taps, size, size)
    return pl.pallas_call(
        taps_kernel,
        out_shape=tuple(
            jax.ShapeDtypeStruct((2, 3, len(REACH[d]) * size, ROWS * size), conv_weight.dtype)
            for d in (1, 2)
        ),
        cost_estimate=cost(0, 6 << 20),
        name="spread_taps",
    )(flipped)


def contact_head(links, probs, pair_weight, taps, head_weight):
    _, chips, heads, rows, residues = probs.shape
    own_rows = residues // links.devices
    channels = pair_weight.shape[0]
    first_row = links.index * own_rows
    margin = 2 * ROWS
    band_rows = own_rows + 2 * margin
    blocks = band_rows // ROWS
    by_row = probs.transpose(1, 3, 0, 2, 4).reshape(residues, 2 * heads, residues)
    band_probs = lax.dynamic_slice_in_dim(
        jnp.pad(by_row, ((margin, margin), (0, 0), (0, 0))), first_row, band_rows, 0
    )
    band_cols = lax.dynamic_slice_in_dim(
        jnp.pad(probs, ((0, 0), (0, 0), (0, 0), (0, 0), (margin, margin))), first_row, band_rows, 4
    )
    band_cols = band_cols.transpose(4, 0, 2, 1, 3).reshape(band_rows, 2 * heads, residues)
    pair_features = (
        (band_probs.astype(jnp.float32) + band_cols.astype(jnp.float32)) * (residues * 0.5)
    ).astype(jnp.bfloat16)
    pair_features = pair_features.reshape(blocks, ROWS * 2 * heads, residues)
    pair = jnp.kron(jnp.eye(ROWS, dtype=pair_weight.dtype), pair_weight.T)
    head = jnp.tile(head_weight, ROWS)[None]
    lanes = ROWS * channels
    vmem = pl.BlockSpec(memory_space=pltpu.VMEM)
    work = 2 * residues * lanes * lanes * (13 * blocks + 17 * (blocks - 2))
    return pl.pallas_call(
        contact_kernel,
        out_shape=jax.ShapeDtypeStruct((own_rows, residues), jnp.float32),
        in_specs=[pl.BlockSpec(memory_space=pltpu.SMEM)] + [vmem] * 5,
        out_specs=vmem,
        scratch_shapes=[
            pltpu.VMEM((3, blocks, residues, lanes), jnp.bfloat16),
            pltpu.VMEM((3, blocks, residues, lanes), jnp.bfloat16),
            pltpu.VMEM((blocks, residues, lanes), jnp.float32),
        ],
        compiler_params=pltpu.CompilerParams(vmem_limit_bytes=48 << 20),
        cost_estimate=cost(work // 4, 4 << 20),
        name="contact_head",
    )(first_row.astype(jnp.int32).reshape(1), pair_features, pair, taps[0], taps[1], head)


def local(alignment, depth_count, qkv_weight, pair_weight, conv_weight, head_weight):
    seqs, residues, features = alignment.shape
    head_count = pair_weight.shape[1]
    size = features // head_count
    links = Links()
    depth = depth_count[0]
    half = links.core.astype(jnp.int32).reshape(1)
    use = jnp.clip(depth - links.index * seqs, 0, seqs).astype(jnp.int32).reshape(1)
    sent, own, values = projections(alignment, qkv_weight, half, use, head_count)
    other = links.send(sent, 0, 0, swap=True)
    order = jnp.stack(
        [links.at(dz, dy) for dz in range(links.tall) for dy in range(links.wide)]
    ).astype(jnp.int32)
    scale = size**-0.5 / jnp.sqrt(depth.astype(jnp.float32)) * LINK_SCALE
    scores = scores_of(own, other, order, scale.reshape(1), links.chips)
    summed = reduce_scatter(links, scores) * (1.0 / LINK_SCALE)
    probabilities = jax.nn.softmax(summed, axis=-1).astype(jnp.bfloat16)
    gathered = all_gather(links, probabilities)
    row_mix = row_mix_of(gathered, values, seqs, head_count)
    contacts = contact_head(links, gathered, pair_weight, spread_taps(conv_weight), head_weight)
    return (row_mix, contacts)


def solution(mesh):
    return jax.shard_map(
        local,
        mesh=mesh,
        in_specs=(P(("grp", "seq"), None, None), P("grp"), P(), P(), P(), P()),
        out_specs=(P(("grp", "seq"), None, None), P(("grp", "seq"), None)),
        check_vma=False,
    )
```

profile of v0, /device:TPU:0, one launch (start us, length us, event | category | flops | bytes accessed | tf_op | source)
XLA Modules:
  0.0 208.2 jit_solution(6818188916623121357)
XLA Ops:
  1.3 8.1 %norm_send.1 = (bf16[4,512,768]{2,1,0:T(8,128)(2,1)S(1)}, bf16[2,6,512,256]{3,2,1,0:T(8,128)(2,1)}) custom-call(s32[1]{0:T(128)} %bitcast.10.half_ref, s32[1]{0:T(128)} %bitcast.11.use_ref, bf16[4,512,768]{2,1,0:T(8,128)(2,1)} %x_ref.1, bf16[768,2304]{1,0:T(8,128)(2,1)} %w_ref.1, bf16[768,2304]{1,0:T(8,128)(2,1)} %w_ref.1), custom_call_target="tpu_custom_call" | custom-call | flops 2415919104 | bytes 10616832 | tf_op jit(solution)/shard_map/norm_send/pallas_call | solution.py:131
  9.4 1.6 copy-done.2
  11.1 0.5 collective-permute-start
  11.6 0.1 stack.35.order_ref
  11.6 6.0 %own_project.1.own_ref = bf16[2,6,512,256]{3,2,1,0:T(8,128)(2,1)S(1)} custom-call(s32[1]{0:T(128)} %bitcast.10.half_ref, s32[1]{0:T(128)} %bitcast.11.use_ref, bf16[4,512,768]{2,1,0:T(8,128)(2,1)} %copy-done.2, bf16[768,2304]{1,0:T(8,128)(2,1)} %w_ref.1, bf16[768,2304]{1,0:T(8,128)(2,1)} %w_ref.1), custom_call_target="tpu_custom_call" | custom-call | flops 2415919104 | bytes 7471104 | tf_op jit(solution)/shard_map/own_project/pallas_call | solution.py:144
  17.6 4.2 %scores.1 = f32[8,6,64,512]{3,2,1,0:T(8,128)S(1)} custom-call(s32[8]{0:T(128)S(1)} %stack.35.order_ref, f32[1]{0:T(128)} %bitcast.9.scale_ref, bf16[2,6,512,256]{3,2,1,0:T(8,128)(2,1)S(1)} %own_project.1.own_ref, bf16[2,6,512,256]{3,2,1,0:T(8,128)(2,1)S(1)} %collective-permute-done.other_ref), custom_call_target="tpu_custom_call" | custom-call | flops 1610612736 | bytes 12582912 | tf_op jit(solution)/shard_map/scores/pallas_call | solution.py:177
  21.9 0.7 convert.8
  22.6 0.4 slice_bitcast_fusion.7
  23.1 2.6 %collective-permute-start.1 = (f16[6,64,512]{2,1,0:T(8,128)(2,1)S(1)}, f16[6,64,512]{2,1,0:T(8,128)(2,1)S(1)}, u32[]{:S(2)}, u32[]{:S(2)}) collective-permute-start(f16[6,64,512]{2,1,0:T(8,128)(2,1)S(1)} %get-tuple-element.13), channel_id=1, source_target_pairs={{0,2},{1,3},{2,0},{3,1},{4,6},{5,7},{6,4},{7,5},{8,10},{9,11},{10,... | collective-permute-start | bytes 1179656 | tf_op jit(solution)/shard_map/ppermute | solution.py:234
  25.6 0.1 collective-permute-start.5
  25.7 1.9 collective-permute-start.3
  27.7 0.1 collective-permute-start.7
  27.8 7.9 %collective-permute-done.1 = f16[6,64,512]{2,1,0:T(8,128)(2,1)S(1)} collective-permute-done((f16[6,64,512]{2,1,0:T(8,128)(2,1)S(1)}, f16[6,64,512]{2,1,0:T(8,128)(2,1)S(1)}, u32[]{:S(2)}, u32[]{:S(2)}) %collective-permute-start.1) | collective-permute-done | bytes 393248 | tf_op jit(solution)/shard_map/ppermute | solution.py:234
  35.6 8.4 %collective-permute-done.5 = f16[6,64,512]{2,1,0:T(8,128)(2,1)S(1)} collective-permute-done((f16[6,64,512]{2,1,0:T(8,128)(2,1)S(1)}, f16[6,64,512]{2,1,0:T(8,128)(2,1)S(1)}, u32[]{:S(2)}, u32[]{:S(2)}) %collective-permute-start.5) | collective-permute-done | bytes 393248 | tf_op jit(solution)/shard_map/ppermute | solution.py:234
  44.0 8.4 %collective-permute-done.3 = f16[6,64,512]{2,1,0:T(8,128)(2,1)S(1)} collective-permute-done((f16[6,64,512]{2,1,0:T(8,128)(2,1)S(1)}, f16[6,64,512]{2,1,0:T(8,128)(2,1)S(1)}, u32[]{:S(2)}, u32[]{:S(2)}) %collective-permute-start.3) | collective-permute-done | bytes 393248 | tf_op jit(solution)/shard_map/ppermute | solution.py:234
  52.5 0.4 fusion.14
  52.9 0.0 copy-start.6
  52.9 0.0 copy-start.5
  52.9 0.0 copy-start.7
  52.9 4.1 %collective-permute-start.6 = (f16[6,64,512]{2,1,0:T(8,128)(2,1)S(1)}, f16[6,64,512]{2,1,0:T(8,128)(2,1)S(1)}, u32[]{:S(2)}, u32[]{:S(2)}) collective-permute-start(f16[6,64,512]{2,1,0:T(8,128)(2,1)S(1)} %get-tuple-element.11), channel_id=1, source_target_pairs={{0,12},{1,13},{2,14},{3,15},{4,0},{5,1},{6,2},{7,3},{8,4},{9,5},{1... | collective-permute-start | bytes 1179656 | tf_op jit(solution)/shard_map/ppermute | solution.py:234
  57.0 1.0 collective-permute-start.2
  58.0 2.7 %collective-permute-done.7 = f16[6,64,512]{2,1,0:T(8,128)(2,1)S(1)} collective-permute-done((f16[6,64,512]{2,1,0:T(8,128)(2,1)S(1)}, f16[6,64,512]{2,1,0:T(8,128)(2,1)S(1)}, u32[]{:S(2)}, u32[]{:S(2)}) %collective-permute-start.7) | collective-permute-done | bytes 393248 | tf_op jit(solution)/shard_map/ppermute | solution.py:234
  60.7 5.9 %collective-permute-done.6 = f16[6,64,512]{2,1,0:T(8,128)(2,1)S(1)} collective-permute-done((f16[6,64,512]{2,1,0:T(8,128)(2,1)S(1)}, f16[6,64,512]{2,1,0:T(8,128)(2,1)S(1)}, u32[]{:S(2)}, u32[]{:S(2)}) %collective-permute-start.6) | collective-permute-done | bytes 393248 | tf_op jit(solution)/shard_map/ppermute | solution.py:234
  66.6 9.4 %collective-permute-done.4 = f16[6,64,512]{2,1,0:T(8,128)(2,1)S(1)} collective-permute-done((f16[6,64,512]{2,1,0:T(8,128)(2,1)S(1)}, f16[6,64,512]{2,1,0:T(8,128)(2,1)S(1)}, u32[]{:S(2)}, u32[]{:S(2)}) %collective-permute-start.4) | collective-permute-done | bytes 393248 | tf_op jit(solution)/shard_map/ppermute | solution.py:234
  76.0 14.2 %collective-permute-done.2 = f16[6,64,512]{2,1,0:T(8,128)(2,1)} collective-permute-done((f16[6,64,512]{2,1,0:T(8,128)(2,1)S(1)}, f16[6,64,512]{2,1,0:T(8,128)(2,1)}, u32[]{:S(2)}, u32[]{:S(2)}) %collective-permute-start.2) | collective-permute-done | bytes 393248 | tf_op jit(solution)/shard_map/ppermute | solution.py:234
  90.2 3.4 %broadcast_in_dim.57 = bf16[2,8,6,64,512]{4,3,2,1,0:T(8,128)(2,1)} broadcast(bf16[]{:T(256)} %constant.142.clone.1), dimensions={} | broadcast | bytes 6291458 | tf_op jit(solution)/shard_map/broadcast_in_dim | solution.py:260
  93.6 2.6 %bitcast_dynamic-update-slice_fusion.15 = (bf16[2,8,6,64,512]{4,3,2,1,0:T(8,128)(2,1)}, bf16[6,64,512]{2,1,0:T(8,128)(2,1)}) fusion(bf16[2,8,6,64,512]{4,3,2,1,0:T(8,128)(2,1)} %broadcast_in_dim.57, s32[]{:T(128)S(6)} %select_n.168, s32[]{:T(128)S(6)} %select_n.169, f32[8,6,64,512]{3,2,1,0:T(8,128)} %copy-done.1, ...), kind=kOutput, calls=%fused_computation.42 | output fusion | flops 2361086 | bytes 3145736 | tf_op jit(solution)/shard_map/div | solution.py:461
  96.2 0.0 collective-permute-start.9
  96.2 3.2 %collective-permute-start.11 = (bf16[6,64,512]{2,1,0:T(8,128)(2,1)}, bf16[6,64,512]{2,1,0:T(8,128)(2,1)S(1)}, u32[]{:S(2)}, u32[]{:S(2)}) collective-permute-start(bf16[6,64,512]{2,1,0:T(8,128)(2,1)} %get-tuple-element.18), channel_id=1, source_target_pairs={{0,4},{1,5},{2,6},{3,7},{4,8},{5,9},{6,10},{7,11},{8,12},{9,13},{1... | collective-permute-start | bytes 1179656 | tf_op jit(solution)/shard_map/ppermute | solution.py:234
  99.5 0.1 broadcast_multiply_fusion
  99.6 0.1 mul.92.pair_ref
  99.7 1.1 copy.12
  100.7 2.9 %spread_taps.1 = (bf16[2,3,384,256]{3,2,1,0:T(8,128)(2,1)}, bf16[2,3,512,256]{3,2,1,0:T(8,128)(2,1)}) custom-call(bf16[36,64,64]{2,1,0:T(8,128)(2,1)} %bitcast.98), custom_call_target="tpu_custom_call" | custom-call | bytes 6291456 | tf_op jit(solution)/shard_map/spread_taps/pallas_call | solution.py:393
  103.7 0.1 broadcast_in_dim_tile.3.head_ref
  103.7 5.6 %value_project.1.v_ref = bf16[12,512,256]{2,1,0:T(8,128)(2,1)S(1)} custom-call(bf16[4,512,768]{2,1,0:T(8,128)(2,1)} %copy-done.2, bf16[768,2304]{1,0:T(8,128)(2,1)} %w_ref.1), custom_call_target="tpu_custom_call" | custom-call | flops 2415919104 | bytes 7471104 | tf_op jit(solution)/shard_map/value_project/pallas_call | solution.py:157
  109.4 0.9 collective-permute-start.13
  110.2 1.5 collective-permute-start.15
  111.7 14.2 %collective-permute-done.9 = bf16[6,64,512]{2,1,0:T(8,128)(2,1)S(1)} collective-permute-done((bf16[6,64,512]{2,1,0:T(8,128)(2,1)}, bf16[6,64,512]{2,1,0:T(8,128)(2,1)S(1)}, u32[]{:S(2)}, u32[]{:S(2)}) %collective-permute-start.9) | collective-permute-done | bytes 393248 | tf_op jit(solution)/shard_map/ppermute | solution.py:234
  125.9 0.0 collective-permute-start.10
  125.9 0.0 collective-permute-done.8
  125.9 1.5 collective-permute-start.17
  127.4 0.2 collective-permute-start.12
  127.6 1.0 bitcast_dynamic-update-slice_fusion.14
  128.7 5.5 %collective-permute-done.13 = bf16[6,64,512]{2,1,0:T(8,128)(2,1)S(1)} collective-permute-done((bf16[6,64,512]{2,1,0:T(8,128)(2,1)}, bf16[6,64,512]{2,1,0:T(8,128)(2,1)S(1)}, u32[]{:S(2)}, u32[]{:S(2)}) %collective-permute-start.13) | collective-permute-done | bytes 393248 | tf_op jit(solution)/shard_map/ppermute | solution.py:234
  134.2 1.5 collective-permute-start.19
  135.6 0.0 collective-permute-done.10
  135.6 0.5 collective-permute-start.21
  136.3 0.1 collective-permute-start.14
  136.4 0.5 collective-permute-start.16
  136.9 1.0 collective-permute-done.17
  137.8 8.4 %collective-permute-done.19 = bf16[6,64,512]{2,1,0:T(8,128)(2,1)S(1)} collective-permute-done((bf16[6,64,512]{2,1,0:T(8,128)(2,1)S(1)}, bf16[6,64,512]{2,1,0:T(8,128)(2,1)S(1)}, u32[]{:S(2)}, u32[]{:S(2)}) %collective-permute-start.19) | collective-permute-done | bytes 393248 | tf_op jit(solution)/shard_map/ppermute | solution.py:234
  146.3 8.0 %collective-permute-done.21 = bf16[6,64,512]{2,1,0:T(8,128)(2,1)S(1)} collective-permute-done((bf16[6,64,512]{2,1,0:T(8,128)(2,1)S(1)}, bf16[6,64,512]{2,1,0:T(8,128)(2,1)S(1)}, u32[]{:S(2)}, u32[]{:S(2)}) %collective-permute-start.21) | collective-permute-done | bytes 393248 | tf_op jit(solution)/shard_map/ppermute | solution.py:234
  154.8 1.3 collective-permute-done.22
  156.1 5.4 %row_mix.1 = bf16[4,512,768]{2,1,0:T(8,128)(2,1)} custom-call(bf16[2,8,6,64,512]{4,3,2,1,0:T(8,128)(2,1)S(1)} %bitcast_dynamic-update-slice_fusion.p_ref, bf16[12,512,256]{2,1,0:T(8,128)(2,1)S(1)} %value_project.1.v_ref), custom_call_target="tpu_custom_call" | custom-call | flops 1610612736 | bytes 12582912 | tf_op jit(solution)/shard_map/row_mix/pallas_call | solution.py:197
  161.4 2.6 %convert_bitcast_fusion = f32[48,2,6,8,64]{0,4,2,3,1:T(8,128)} fusion(s32[]{:T(128)S(6)} %select_n.182, bf16[2,8,6,64,512]{4,3,2,1,0:T(8,128)(2,1)S(1)} %bitcast_dynamic-update-slice_fusion.p_ref), kind=kLoop, calls=%fused_computation.4 | loop fusion | flops 294912 | bytes 7471108 | tf_op jit(solution)/shard_map/convert_element_type | solution.py:421
  164.0 3.4 %copy.10 = f32[48,2,6,8,64]{4,3,0,2,1:T(8,128)} copy(f32[48,2,6,8,64]{0,4,2,3,1:T(8,128)} %convert_bitcast_fusion) | data formatting | bytes 2359296 | tf_op jit(solution)/shard_map/convert_element_type | solution.py:421
  167.4 2.0 reshape.56
  169.4 3.5 %copy.9 = bf16[8,64,2,6,512]{4,1,0,3,2:T(8,128)(2,1)S(1)} copy(bf16[8,64,2,6,512]{4,1,3,0,2:T(8,128)(2,1)} %bitcast.96) | data formatting | bytes 12582912 | tf_op jit(solution)/shard_map/transpose | solution.py:412
  173.0 0.2 multiply_convert_fusion
  173.2 0.3 copy.11
  173.5 0.1 reshape.54.pf_ref
  173.7 0.5 copy-done.4
  174.2 1.4 copy-done.3
  175.6 32.6 %contact_head.1 = f32[32,512]{1,0:T(8,128)} custom-call(s32[1]{0:T(128)} %bitcast.36.row_ref, bf16[12,48,512]{2,1,0:T(8,128)(2,1)S(1)} %reshape.54.pf_ref, bf16[48,256]{1,0:T(8,128)(2,1)S(1)} %mul.92.pair_ref, bf16[2,3,384,256]{3,2,1,0:T(8,128)(2,1)S(1)} %copy-done.4, bf16[2,3,512,256]{3,2,1,0:T(8,128)(2,1)S(1)} %copy-done.3, ...), custom_call_target="tpu_custom_call" | custom-call | flops 5469372416 | bytes 4194304 | tf_op jit(solution)/shard_map/contact_head/pallas_call | solution.py:429
  (44 shorter events, 0.5 us)
Async XLA Ops:
  9.4 1.6 copy-start.2
  11.1 6.6 %collective-permute-start = (bf16[2,6,512,256]{3,2,1,0:T(8,128)(2,1)}, bf16[2,6,512,256]{3,2,1,0:T(8,128)(2,1)S(1)}, u32[]{:S(2)}, u32[]{:S(2)}) collective-permute-start(bf16[2,6,512,256]{3,2,1,0:T(8,128)(2,1)} %get-tuple-element.7), channel_id=1, source_target_pairs={{0,1},{1,0},{2,3},{3,2},{4,5},{5,4},{6,7},{7,6},{8,9},{9,8},{10,11... | collective-permute-start | bytes 9437192 | tf_op jit(solution)/shard_map/ppermute | solution.py:234
  21.9 30.6 %copy-start.1 = (f32[8,6,64,512]{3,2,1,0:T(8,128)}, f32[8,6,64,512]{3,2,1,0:T(8,128)S(1)}, u32[]{:S(2)}) copy-start(f32[8,6,64,512]{3,2,1,0:T(8,128)S(1)} %scores.1) | copy-start | bytes 18874372
  23.1 12.6 %collective-permute-start.1 = (f16[6,64,512]{2,1,0:T(8,128)(2,1)S(1)}, f16[6,64,512]{2,1,0:T(8,128)(2,1)S(1)}, u32[]{:S(2)}, u32[]{:S(2)}) collective-permute-start(f16[6,64,512]{2,1,0:T(8,128)(2,1)S(1)} %get-tuple-element.13), channel_id=1, source_target_pairs={{0,2},{1,3},{2,0},{3,1},{4,6},{5,7},{6,4},{7,5},{8,10},{9,11},{10,... | collective-permute-start | bytes 1179656 | tf_op jit(solution)/shard_map/ppermute | solution.py:234
  25.6 18.4 %collective-permute-start.5 = (f16[6,64,512]{2,1,0:T(8,128)(2,1)S(1)}, f16[6,64,512]{2,1,0:T(8,128)(2,1)S(1)}, u32[]{:S(2)}, u32[]{:S(2)}) collective-permute-start(f16[6,64,512]{2,1,0:T(8,128)(2,1)S(1)} %get-tuple-element.15), channel_id=1, source_target_pairs={{0,2},{1,3},{2,0},{3,1},{4,6},{5,7},{6,4},{7,5},{8,10},{9,11},{10,... | collective-permute-start | bytes 1179656 | tf_op jit(solution)/shard_map/ppermute | solution.py:234
  25.7 26.7 %collective-permute-start.3 = (f16[6,64,512]{2,1,0:T(8,128)(2,1)S(1)}, f16[6,64,512]{2,1,0:T(8,128)(2,1)S(1)}, u32[]{:S(2)}, u32[]{:S(2)}) collective-permute-start(f16[6,64,512]{2,1,0:T(8,128)(2,1)S(1)} %get-tuple-element.16), channel_id=1, source_target_pairs={{0,2},{1,3},{2,0},{3,1},{4,6},{5,7},{6,4},{7,5},{8,10},{9,11},{10,... | collective-permute-start | bytes 1179656 | tf_op jit(solution)/shard_map/ppermute | solution.py:234
  27.7 33.0 %collective-permute-start.7 = (f16[6,64,512]{2,1,0:T(8,128)(2,1)S(1)}, f16[6,64,512]{2,1,0:T(8,128)(2,1)S(1)}, u32[]{:S(2)}, u32[]{:S(2)}) collective-permute-start(f16[6,64,512]{2,1,0:T(8,128)(2,1)S(1)} %get-tuple-element.14), channel_id=1, source_target_pairs={{0,2},{1,3},{2,0},{3,1},{4,6},{5,7},{6,4},{7,5},{8,10},{9,11},{10,... | collective-permute-start | bytes 1179656 | tf_op jit(solution)/shard_map/ppermute | solution.py:234
  52.9 46.6 %copy-start.6 = (bf16[64,12]{0,1:T(8,128)(2,1)S(1)}, bf16[64,12]{0,1:T(8,128)(2,1)}, u32[]{:S(2)}) copy-start(bf16[64,12]{0,1:T(8,128)(2,1)} %param.9) | copy-start | bytes 4612
  52.9 46.8 %copy-start.5 = (bf16[4,9,64,64]{3,2,1,0:T(8,128)(2,1)S(1)}, bf16[4,9,64,64]{3,2,1,0:T(8,128)(2,1)}, u32[]{:S(2)}) copy-start(bf16[4,9,64,64]{3,2,1,0:T(8,128)(2,1)} %param.10) | copy-start | bytes 884740
  52.9 50.7 %copy-start.7 = (f32[64]{0:T(128)S(1)}, f32[64]{0:T(128)}, u32[]{:S(2)}) copy-start(f32[64]{0:T(128)} %param.11) | copy-start | bytes 772
  52.9 13.7 %collective-permute-start.6 = (f16[6,64,512]{2,1,0:T(8,128)(2,1)S(1)}, f16[6,64,512]{2,1,0:T(8,128)(2,1)S(1)}, u32[]{:S(2)}, u32[]{:S(2)}) collective-permute-start(f16[6,64,512]{2,1,0:T(8,128)(2,1)S(1)} %get-tuple-element.11), channel_id=1, source_target_pairs={{0,12},{1,13},{2,14},{3,15},{4,0},{5,1},{6,2},{7,3},{8,4},{9,5},{1... | collective-permute-start | bytes 1179656 | tf_op jit(solution)/shard_map/ppermute | solution.py:234
  57.0 19.0 %collective-permute-start.4 = (f16[6,64,512]{2,1,0:T(8,128)(2,1)S(1)}, f16[6,64,512]{2,1,0:T(8,128)(2,1)S(1)}, u32[]{:S(2)}, u32[]{:S(2)}) collective-permute-start(f16[6,64,512]{2,1,0:T(8,128)(2,1)S(1)} %get-tuple-element.12), channel_id=1, source_target_pairs={{0,4},{1,5},{2,6},{3,7},{4,8},{5,9},{6,10},{7,11},{8,12},{9,13},{1... | collective-permute-start | bytes 1179656 | tf_op jit(solution)/shard_map/ppermute | solution.py:234
  57.0 33.2 %collective-permute-start.2 = (f16[6,64,512]{2,1,0:T(8,128)(2,1)S(1)}, f16[6,64,512]{2,1,0:T(8,128)(2,1)}, u32[]{:S(2)}, u32[]{:S(2)}) collective-permute-start(f16[6,64,512]{2,1,0:T(8,128)(2,1)S(1)} %get-tuple-element.10), channel_id=1, source_target_pairs={{0,8},{1,9},{2,10},{3,11},{4,12},{5,13},{6,14},{7,15},{8,0},{9,1},... | collective-permute-start | bytes 1179656 | tf_op jit(solution)/shard_map/ppermute | solution.py:234
  96.2 31.4 %slice-start = ((s8[6291456]{0:T(1024)(128)(4,1)}), s8[2097152]{0:T(1024)(128)(4,1)S(1)}, s32[]{:S(2)}) async-start(s8[6291456]{0:T(1024)(128)(4,1)} %bitcast.94), calls=%async_computation | async-start | bytes 4194304
  96.2 29.7 %collective-permute-start.8 = (bf16[6,64,512]{2,1,0:T(8,128)(2,1)}, bf16[6,64,512]{2,1,0:T(8,128)(2,1)}, u32[]{:S(2)}, u32[]{:S(2)}) collective-permute-start(bf16[6,64,512]{2,1,0:T(8,128)(2,1)} %get-tuple-element.18), channel_id=1, source_target_pairs={{0,1},{1,0},{2,3},{3,2},{4,5},{5,4},{6,7},{7,6},{8,9},{9,8},{10,11... | collective-permute-start | bytes 1179656 | tf_op jit(solution)/shard_map/ppermute | solution.py:234
  96.2 29.7 %collective-permute-start.9 = (bf16[6,64,512]{2,1,0:T(8,128)(2,1)}, bf16[6,64,512]{2,1,0:T(8,128)(2,1)S(1)}, u32[]{:S(2)}, u32[]{:S(2)}) collective-permute-start(bf16[6,64,512]{2,1,0:T(8,128)(2,1)} %get-tuple-element.18), channel_id=1, source_target_pairs={{0,8},{1,9},{2,10},{3,11},{4,12},{5,13},{6,14},{7,15},{8,0},{9,1},... | collective-permute-start | bytes 1179656 | tf_op jit(solution)/shard_map/ppermute | solution.py:234
  96.2 31.1 %collective-permute-start.11 = (bf16[6,64,512]{2,1,0:T(8,128)(2,1)}, bf16[6,64,512]{2,1,0:T(8,128)(2,1)S(1)}, u32[]{:S(2)}, u32[]{:S(2)}) collective-permute-start(bf16[6,64,512]{2,1,0:T(8,128)(2,1)} %get-tuple-element.18), channel_id=1, source_target_pairs={{0,4},{1,5},{2,6},{3,7},{4,8},{5,9},{6,10},{7,11},{8,12},{9,13},{1... | collective-permute-start | bytes 1179656 | tf_op jit(solution)/shard_map/ppermute | solution.py:234
  103.7 23.9 %slice-start.1 = ((s8[6291456]{0:T(1024)(128)(4,1)}), s8[4194304]{0:T(1024)(128)(4,1)S(1)}, s32[]{:S(2)}) async-start(s8[6291456]{0:T(1024)(128)(4,1)} %bitcast.94), calls=%async_computation.1 | async-start | bytes 8388608
  109.4 24.8 %collective-permute-start.13 = (bf16[6,64,512]{2,1,0:T(8,128)(2,1)}, bf16[6,64,512]{2,1,0:T(8,128)(2,1)S(1)}, u32[]{:S(2)}, u32[]{:S(2)}) collective-permute-start(bf16[6,64,512]{2,1,0:T(8,128)(2,1)} %get-tuple-element.18), channel_id=1, source_target_pairs={{0,12},{1,13},{2,14},{3,15},{4,0},{5,1},{6,2},{7,3},{8,4},{9,5},{1... | collective-permute-start | bytes 1179656 | tf_op jit(solution)/shard_map/ppermute | solution.py:234
  110.2 26.0 %collective-permute-start.15 = (bf16[6,64,512]{2,1,0:T(8,128)(2,1)}, bf16[6,64,512]{2,1,0:T(8,128)(2,1)S(1)}, u32[]{:S(2)}, u32[]{:S(2)}) collective-permute-start(bf16[6,64,512]{2,1,0:T(8,128)(2,1)} %get-tuple-element.18), channel_id=1, source_target_pairs={{0,2},{1,3},{2,0},{3,1},{4,6},{5,7},{6,4},{7,5},{8,10},{9,11},{10,... | collective-permute-start | bytes 1179656 | tf_op jit(solution)/shard_map/ppermute | solution.py:234
  125.9 9.7 %collective-permute-start.10 = (bf16[6,64,512]{2,1,0:T(8,128)(2,1)S(1)}, bf16[6,64,512]{2,1,0:T(8,128)(2,1)S(1)}, u32[]{:S(2)}, u32[]{:S(2)}) collective-permute-start(bf16[6,64,512]{2,1,0:T(8,128)(2,1)S(1)} %collective-permute-done.9), channel_id=1, source_target_pairs={{0,1},{1,0},{2,3},{3,2},{4,5},{5,4},{6,7},{7,6},{8,9},{9,8},{10,11... | collective-permute-start | bytes 1179656 | tf_op jit(solution)/shard_map/ppermute | solution.py:234
  125.9 11.9 %collective-permute-start.17 = (bf16[6,64,512]{2,1,0:T(8,128)(2,1)S(1)}, bf16[6,64,512]{2,1,0:T(8,128)(2,1)S(1)}, u32[]{:S(2)}, u32[]{:S(2)}) collective-permute-start(bf16[6,64,512]{2,1,0:T(8,128)(2,1)S(1)} %collective-permute-done.9), channel_id=1, source_target_pairs={{0,2},{1,3},{2,0},{3,1},{4,6},{5,7},{6,4},{7,5},{8,10},{9,11},{10,... | collective-permute-start | bytes 1179656 | tf_op jit(solution)/shard_map/ppermute | solution.py:234
  127.4 9.0 %collective-permute-start.12 = (bf16[6,64,512]{2,1,0:T(8,128)(2,1)S(1)}, bf16[6,64,512]{2,1,0:T(8,128)(2,1)S(1)}, u32[]{:S(2)}, u32[]{:S(2)}) collective-permute-start(bf16[6,64,512]{2,1,0:T(8,128)(2,1)S(1)} %collective-permute-done.11), channel_id=1, source_target_pairs={{0,1},{1,0},{2,3},{3,2},{4,5},{5,4},{6,7},{7,6},{8,9},{9,8},{10,11... | collective-permute-start | bytes 1179656 | tf_op jit(solution)/shard_map/ppermute | solution.py:234
  134.2 12.1 %collective-permute-start.19 = (bf16[6,64,512]{2,1,0:T(8,128)(2,1)S(1)}, bf16[6,64,512]{2,1,0:T(8,128)(2,1)S(1)}, u32[]{:S(2)}, u32[]{:S(2)}) collective-permute-start(bf16[6,64,512]{2,1,0:T(8,128)(2,1)S(1)} %collective-permute-done.11), channel_id=1, source_target_pairs={{0,2},{1,3},{2,0},{3,1},{4,6},{5,7},{6,4},{7,5},{8,10},{9,11},{10,... | collective-permute-start | bytes 1179656 | tf_op jit(solution)/shard_map/ppermute | solution.py:234
  135.6 18.7 %collective-permute-start.21 = (bf16[6,64,512]{2,1,0:T(8,128)(2,1)S(1)}, bf16[6,64,512]{2,1,0:T(8,128)(2,1)S(1)}, u32[]{:S(2)}, u32[]{:S(2)}) collective-permute-start(bf16[6,64,512]{2,1,0:T(8,128)(2,1)S(1)} %collective-permute-done.13), channel_id=1, source_target_pairs={{0,2},{1,3},{2,0},{3,1},{4,6},{5,7},{6,4},{7,5},{8,10},{9,11},{10,... | collective-permute-start | bytes 1179656 | tf_op jit(solution)/shard_map/ppermute | solution.py:234
  136.3 18.1 %collective-permute-start.14 = (bf16[6,64,512]{2,1,0:T(8,128)(2,1)S(1)}, bf16[6,64,512]{2,1,0:T(8,128)(2,1)S(1)}, u32[]{:S(2)}, u32[]{:S(2)}) collective-permute-start(bf16[6,64,512]{2,1,0:T(8,128)(2,1)S(1)} %collective-permute-done.13), channel_id=1, source_target_pairs={{0,1},{1,0},{2,3},{3,2},{4,5},{5,4},{6,7},{7,6},{8,9},{9,8},{10,11... | collective-permute-start | bytes 1179656 | tf_op jit(solution)/shard_map/ppermute | solution.py:234
  136.4 18.1 %collective-permute-start.16 = (bf16[6,64,512]{2,1,0:T(8,128)(2,1)S(1)}, bf16[6,64,512]{2,1,0:T(8,128)(2,1)S(1)}, u32[]{:S(2)}, u32[]{:S(2)}) collective-permute-start(bf16[6,64,512]{2,1,0:T(8,128)(2,1)S(1)} %collective-permute-done.15), channel_id=1, source_target_pairs={{0,1},{1,0},{2,3},{3,2},{4,5},{5,4},{6,7},{7,6},{8,9},{9,8},{10,11... | collective-permute-start | bytes 1179656 | tf_op jit(solution)/shard_map/ppermute | solution.py:234
  137.8 16.8 %collective-permute-start.18 = (bf16[6,64,512]{2,1,0:T(8,128)(2,1)S(1)}, bf16[6,64,512]{2,1,0:T(8,128)(2,1)S(1)}, u32[]{:S(2)}, u32[]{:S(2)}) collective-permute-start(bf16[6,64,512]{2,1,0:T(8,128)(2,1)S(1)} %collective-permute-done.17), channel_id=1, source_target_pairs={{0,1},{1,0},{2,3},{3,2},{4,5},{5,4},{6,7},{7,6},{8,9},{9,8},{10,11... | collective-permute-start | bytes 1179656 | tf_op jit(solution)/shard_map/ppermute | solution.py:234
  146.3 8.4 %collective-permute-start.20 = (bf16[6,64,512]{2,1,0:T(8,128)(2,1)S(1)}, bf16[6,64,512]{2,1,0:T(8,128)(2,1)S(1)}, u32[]{:S(2)}, u32[]{:S(2)}) collective-permute-start(bf16[6,64,512]{2,1,0:T(8,128)(2,1)S(1)} %collective-permute-done.19), channel_id=1, source_target_pairs={{0,1},{1,0},{2,3},{3,2},{4,5},{5,4},{6,7},{7,6},{8,9},{9,8},{10,11... | collective-permute-start | bytes 1179656 | tf_op jit(solution)/shard_map/ppermute | solution.py:234
  154.3 1.7 collective-permute-start.22
  156.1 5.4 %copy-start = (bf16[2,8,6,64,512]{4,3,2,1,0:T(8,128)(2,1)}, bf16[2,8,6,64,512]{4,3,2,1,0:T(8,128)(2,1)S(1)}, u32[]{:S(2)}) copy-start(bf16[2,8,6,64,512]{4,3,2,1,0:T(8,128)(2,1)S(1)} %bitcast_dynamic-update-slice_fusion.p_ref) | copy-start | bytes 18874372
  172.9 1.3 copy-start.4
  174.2 1.4 copy-start.3
where the time goes:
time: 209 us; the launch traced here: 208 us
  waiting for transfers between devices  95.2 us (46%)
  Pallas kernels  64.8 us (31%)
  starting transfers between devices  20.1 us (10%)
  local copies, waits for them, and re-layouts  19.6 us (9%)
  other arithmetic  6.74 us (3%)
    ppermute x23, waiting for transfers between devices, send(): return lax.ppermute(value, 'seq', pairs)  95.2 us
    pallas_call x1, Pallas kernels, contact_head(): pl.pallas_call(contact_kernel, out_shape=jax.ShapeDtypeStruct((own_rows,...  32.6 us
    ppermute x23, starting transfers between devices, send(): return lax.ppermute(value, 'seq', pairs)  20.1 us
    pallas_call x1, Pallas kernels, projections(): pl.pallas_call(norm_send_kernel, out_shape=(jax.ShapeDtypeStruct(alignmen...  8.13 us
    pallas_call x1, Pallas kernels, projections(): pl.pallas_call(own_kernel, out_shape=qk_shape, grid_spec=pltpu.PrefetchSc...  5.98 us
    pallas_call x1, Pallas kernels, projections(): pl.pallas_call(value_kernel, out_shape=jax.ShapeDtypeStruct((head_count,...  5.61 us
    pallas_call x1, Pallas kernels, row_mix_of(): pl.pallas_call(mix_kernel, out_shape=jax.ShapeDtypeStruct((seqs, residues...  5.37 us
    convert_element_type x2, local copies, waits for them, and re-layouts, contact_head(): band_cols.astype(jnp.float32)  5.35 us
  transfers between devices with their start and end apart: 23, of which 13 were waited for; matrix products, arithmetic and copies ran while one was open for 2% of the time, Pallas kernels for 7%

commit v1 on v0

--- a/solution.py
+++ b/solution.py
@@ -17,6 +17,17 @@
     while (2 * width) ** 2 <= chips:
         width *= 2
     return chips // width, width
+
+
+def ring_of(chips):
+    tall, wide = grid_of(chips)
+    if tall % 2 or wide < 2:
+        return list(range(chips))
+    ring = [0]
+    for row in range(tall):
+        columns = range(1, wide) if row % 2 == 0 else range(wide - 1, 0, -1)
+        ring += [row * wide + column for column in columns]
+    return ring + [row * wide for row in range(tall - 1, 0, -1)]
 
 
 def head_major(values, seqs, rows, size):
@@ -213,65 +224,98 @@
     def __init__(self):
         self.devices = lax.axis_size("seq")
         self.chips = self.devices // 2
-        self.tall, self.wide = grid_of(self.chips)
-        index = lax.axis_index("seq")
-        self.index = index
-        self.core = index % 2
-        self.chip = index // 2
-        self.z = self.chip // self.wide
-        self.y = self.chip % self.wide
-
-    def at(self, dz, dy):
-        return (self.z + dz) % self.tall * self.wide + (self.y + dy) % self.wide
-
-    def send(self, value, dz, dy, swap=False):
+        self.ring = ring_of(self.chips)
+        self.index = lax.axis_index("seq")
+        self.core = self.index % 2
+        self.chip = self.index // 2
+        places = [self.ring.index(chip) for chip in range(self.chips)]
+        self.place = jnp.asarray(places, jnp.int32)[self.chip]
+
+    def at(self, ahead):
+        return jnp.asarray(self.ring, jnp.int32)[(self.place + ahead) % self.chips]
+
+    def send(self, value, ahead):
         pairs = []
-        for source in range(self.devices):
-            chip, core = divmod(source, 2)
-            z, y = divmod(chip, self.wide)
-            target = (z + dz) % self.tall * self.wide + (y + dy) % self.wide
-            pairs.append((source, 2 * target + (1 - core if swap else core)))
+        for place, chip in enumerate(self.ring):
+            target = self.ring[(place + ahead) % self.chips]
+            pairs += [(2 * chip + core, 2 * target + core) for core in range(2)]
         return lax.ppermute(value, "seq", pairs)
 
-
-def reduce_scatter(links, scores):
-    def piece(dz, dy):
-        return scores[dz * links.wide + dy]
-
-    half = jnp.float16
-    far = sorted(range(links.tall), key=lambda dz: -min(dz, links.tall - dz))
-    column = {}
-    for dz in far:
-        column[dz] = [
-            links.send(piece(dz, dy).astype(half), 0, dy) for dy in range(1, links.wide)
-        ]
-    total = None
-    for dz in far:
-        summed = piece(dz, 0)
-        for arrived in column[dz]:
-            summed = summed + arrived.astype(jnp.float32)
-        if dz:
-            summed = links.send(summed.astype(half), dz, 0).astype(jnp.float32)
-        total = summed if total is None else total + summed
-    return total
-
-
-def all_gather(links, own):
-    gathered = jnp.zeros((2, links.chips) + own.shape, own.dtype)
-    far = sorted(range(links.tall), key=lambda dz: -min(dz, links.tall - dz))
-    zeros = (0,) * own.ndim
-    pieces = []
-    for dz in far:
-        pieces.append((-dz, 0, links.send(own, dz, 0) if dz else own))
-    pieces = pieces[-1:] + pieces[:-1]
+    def swap(self, value):
+        return lax.ppermute(value, "seq", [(i, i ^ 1) for i in range(self.devices)])
+
+
+def reduce_scatter(links, scores, side):
+    chips, _, rows, _ = scores.shape
+    half = rows // 2
+    low, high = slice(0, half), slice(half, rows)
+    deep = chips // 2
+    chains = [[(1, low), (-1, high)], [(1, high), (-1, low)]]
+
+    def share(way, part, far):
+        return scores[way * far % chips, :, part]
+
+    moving = [None, None]
+    gate = None
+    side = list(side)
+    done = []
+    for far in range(deep, 0, -1):
+        for group in range(2):
+            if group == 1 and far == deep:
+                continue
+            chain = chains[group]
+            if moving[group] is None:
+                sums = [share(way, part, far).astype(jnp.float16) for way, part in chain]
+            else:
+                arrived = moving[group]
+                if gate is not None:
+                    arrived, _ = lax.optimization_barrier((arrived, gate))
+                if side:
+                    arrived, kept = lax.optimization_barrier((arrived, side.pop(0)))
+                    done.append(kept)
+                sums = [
+                    (value.astype(jnp.float32) + share(way, part, far)).astype(jnp.float16)
+                    for value, (way, part) in zip(arrived, chain)
+                ]
+            gate = sums
+            moving[group] = [links.send(value, way) for value, (way, _) in zip(sums, chain)]
+    (low_ahead, high_back), (high_ahead, low_back) = moving if deep > 1 else (moving[0], (0.0, 0.0))
+
+    def settle(part, *arrived):
+        total = scores[0, :, part]
+        for value in arrived:
+            total = total + value.astype(jnp.float32)
+        return total
+
+    if deep > 1:
+        parts = [settle(low, low_ahead, low_back), settle(high, high_ahead, high_back)]
+    else:
+        parts = [settle(low, low_ahead), settle(high, high_back)]
+    return jnp.concatenate(parts, axis=1), done + side
+
+
+def all_gather(links, own, gathered):
+    chips = links.chips
+    half = own.shape[1] // 2
+    deep = chips // 2
+    pieces = [(0, 0, own)]
+    ahead = back = own
+    for far in range(1, deep):
+        ahead = links.send(ahead, 1)
+        back = links.send(back, -1)
+        pieces += [(-far, 0, ahead), (far, 0, back)]
     pieces += [
-        (dz, -dy, links.send(value, 0, dy)) for dz, _, value in pieces for dy in range(1, links.wide)
+        (-deep, 0, links.send(ahead[:, :half], 1)),
+        (deep, half, links.send(back[:, half:], -1)),
     ]
-    swapped = [links.send(value, 0, 0, swap=True) for _, _, value in pieces]
-    for (dz, dy, value), other in zip(pieces, swapped):
-        chip = links.at(dz, dy)
-        gathered = lax.dynamic_update_slice(gathered, value[None, None], (links.core, chip) + zeros)
-        gathered = lax.dynamic_update_slice(gathered, other[None, None], (1 - links.core, chip) + zeros)
+    swapped = [links.swap(value) for _, _, value in pieces]
+    for (far, row, value), other in zip(pieces, swapped):
+        chip = links.at(far)
+        where = (0, row, 0)
+        gathered = lax.dynamic_update_slice(gathered, value[None, None], (links.core, chip) + where)
+        gathered = lax.dynamic_update_slice(
+            gathered, other[None, None], (1 - links.core, chip) + where
+        )
     return gathered
 
 
@@ -451,17 +495,19 @@
     half = links.core.astype(jnp.int32).reshape(1)
     use = jnp.clip(depth - links.index * seqs, 0, seqs).astype(jnp.int32).reshape(1)
     sent, own, values = projections(alignment, qkv_weight, half, use, head_count)
-    other = links.send(sent, 0, 0, swap=True)
-    order = jnp.stack(
-        [links.at(dz, dy) for dz in range(links.tall) for dy in range(links.wide)]
-    ).astype(jnp.int32)
+    other = links.swap(sent)
+    order = jnp.stack([links.at(ahead) for ahead in range(links.chips)])
     scale = size**-0.5 / jnp.sqrt(depth.astype(jnp.float32)) * LINK_SCALE
     scores = scores_of(own, other, order, scale.reshape(1), links.chips)
-    summed = reduce_scatter(links, scores) * (1.0 / LINK_SCALE)
-    probabilities = jax.nn.softmax(summed, axis=-1).astype(jnp.bfloat16)
-    gathered = all_gather(links, probabilities)
+    rows = residues // links.chips
+    room = jnp.zeros((2, links.chips, head_count // 2, rows, residues), jnp.bfloat16)
+    summed, (room, taps, values) = reduce_scatter(
+        links, scores, (room, spread_taps(conv_weight), values)
+    )
+    probabilities = jax.nn.softmax(summed * (1.0 / LINK_SCALE), axis=-1).astype(jnp.bfloat16)
+    gathered = all_gather(links, probabilities, room)
     row_mix = row_mix_of(gathered, values, seqs, head_count)
-    contacts = contact_head(links, gathered, pair_weight, spread_taps(conv_weight), head_weight)
+    contacts = contact_head(links, gathered, pair_weight, taps, head_weight)
     return (row_mix, contacts)
 
 

time: 209 us -> 202 us (0.967)
  waiting for transfers between devices: 95.2 us -> 46 us
  between operations: 1.69 us -> 28.3 us
  local copies, waits for them, and re-layouts: 19.6 us -> 30.7 us
  starting transfers between devices: 20.1 us -> 25.1 us
    ppermute x23 -> x22, waiting for transfers between devices: 95.2 us -> 44.8 us  [send(): return lax.ppermute(value, 'seq', pairs)]
    unnamed x20 -> x34, local copies, waits for them, and re-layouts: 3.62 us -> 9.79 us
    another operation x1, local copies, waits for them, and re-layouts: 0.09 us -> 4.98 us  [local(): order = jnp.stack([links.at(ahead) for ahead in range(links.chips)])]
    ppermute x23 -> x22, starting transfers between devices: 20.1 us -> 23.7 us  [send(): return lax.ppermute(value, 'seq', pairs)]
    div x1 -> x0, other arithmetic: 2.64 us -> none  [local(): probabilities = jax.nn.softmax(summed, axis=-1).astype(jnp.bfloat16)]
    broadcast_in_dim x1, local copies, waits for them, and re-layouts: 3.4 us -> 0.77 us  [local(): jnp.zeros((2, links.chips, head_count // 2, rows, residues), jnp.bfloat16)]
    convert_element_type x1 -> x6, other arithmetic: 0.43 us -> 2.65 us  [the longest x5 1.68 us: reduce_scatter(): (value.astype(jnp.float32) + share(way, part, far)).astype(jnp.float16)]
  transfers between devices with their start and end apart: 23 -> 32, of which waited for: 13 -> 16; matrix products, arithmetic and copies ran while one was open for 2% -> 5% of each run, Pallas kernels for 7% -> 7%
where the time goes in v1:
time: 202 us; the launch traced here: 201 us
  Pallas kernels  64.4 us (32%)
  waiting for transfers between devices  46 us (23%)
  local copies, waits for them, and re-layouts  30.7 us (15%)
  between operations  28.3 us (14%)
  starting transfers between devices  25.1 us (12%)
  other arithmetic  6.43 us (3%)
    ppermute x22, waiting for transfers between devices, send(): return lax.ppermute(value, 'seq', pairs)  44.8 us
    pallas_call x1, Pallas kernels, contact_head(): pl.pallas_call(contact_kernel, out_shape=jax.ShapeDtypeStruct((own_rows,...  32.6 us
    ppermute x22, starting transfers between devices, send(): return lax.ppermute(value, 'seq', pairs)  23.7 us
    unnamed x34, local copies, waits for them, and re-layouts  9.79 us
    pallas_call x1, Pallas kernels, projections(): pl.pallas_call(norm_send_kernel, out_shape=(jax.ShapeDtypeStruct(alignmen...  8.12 us
    pallas_call x1, Pallas kernels, projections(): pl.pallas_call(own_kernel, out_shape=qk_shape, grid_spec=pltpu.PrefetchSc...  5.98 us
    pallas_call x1, Pallas kernels, projections(): pl.pallas_call(value_kernel, out_shape=jax.ShapeDtypeStruct((head_count,...  5.67 us
    convert_element_type x2, local copies, waits for them, and re-layouts, contact_head(): band_cols.astype(jnp.float32)  5 us
  transfers between devices with their start and end apart: 32, of which 16 were waited for; matrix products, arithmetic and copies ran while one was open for 5% of the time, Pallas kernels for 7%

profile of v1, /device:TPU:0, one launch (start us, length us, event | category | flops | bytes accessed | tf_op | source)
XLA Modules:
  0.0 201.0 jit_solution(7235030350974683749)
XLA Ops:
  1.3 8.1 %norm_send.1 = (bf16[4,512,768]{2,1,0:T(8,128)(2,1)S(1)}, bf16[2,6,512,256]{3,2,1,0:T(8,128)(2,1)}) custom-call(s32[1]{0:T(128)} %bitcast.3.half_ref, s32[1]{0:T(128)} %bitcast.4.use_ref, bf16[4,512,768]{2,1,0:T(8,128)(2,1)} %x_ref.1, bf16[768,2304]{1,0:T(8,128)(2,1)} %w_ref.1, bf16[768,2304]{1,0:T(8,128)(2,1)} %w_ref.1), custom_call_target="tpu_custom_call" | custom-call | flops 2415919104 | bytes 10616832 | tf_op jit(solution)/shard_map/norm_send/pallas_call | solution.py:142
  9.5 1.7 copy-done.3
  11.1 0.5 collective-permute-start
  11.6 0.6 dynamic_slice.60
  21.9 0.7 fusion.32
  22.6 5.0 %stack.3.order_ref = s32[8]{0:T(128)S(1)} concatenate(s32[1]{0:T(128)} %get-tuple-element.73, s32[1]{0:T(128)} %get-tuple-element.72, s32[1]{0:T(128)} %get-tuple-element.71, s32[1]{0:T(128)} %get-tuple-element.70, s32[1]{0:T(128)} %get-tuple-element.69, s32[1]{0:T(128)} %get-tuple-element.68, s32[1]{0:T(128)} %get-tuple-element.67, s32[1]{0:T(128)} %get-tuple-element.66), dimensions={0} | concatenate | bytes 64 | tf_op jit(solution)/shard_map/stack | solution.py:499
  27.6 6.0 %own_project.1.own_ref = bf16[2,6,512,256]{3,2,1,0:T(8,128)(2,1)S(1)} custom-call(s32[1]{0:T(128)} %bitcast.3.half_ref, s32[1]{0:T(128)} %bitcast.4.use_ref, bf16[4,512,768]{2,1,0:T(8,128)(2,1)} %copy-done.3, bf16[768,2304]{1,0:T(8,128)(2,1)} %w_ref.1, bf16[768,2304]{1,0:T(8,128)(2,1)} %w_ref.1), custom_call_target="tpu_custom_call" | custom-call | flops 2415919104 | bytes 7471104 | tf_op jit(solution)/shard_map/own_project/pallas_call | solution.py:155
  33.6 4.2 %scores.1 = f32[8,6,64,512]{3,2,1,0:T(8,128)S(1)} custom-call(s32[8]{0:T(128)S(1)} %stack.3.order_ref, f32[1]{0:T(128)} %bitcast.2.scale_ref, bf16[2,6,512,256]{3,2,1,0:T(8,128)(2,1)S(1)} %own_project.1.own_ref, bf16[2,6,512,256]{3,2,1,0:T(8,128)(2,1)S(1)} %collective-permute-done.other_ref), custom_call_target="tpu_custom_call" | custom-call | flops 1610612736 | bytes 12582912 | tf_op jit(solution)/shard_map/scores/pallas_call | solution.py:188
  37.9 2.6 %copy-done.2 = f32[8,6,64,512]{3,2,1,0:T(8,128)} copy-done((f32[8,6,64,512]{3,2,1,0:T(8,128)}, f32[8,6,64,512]{3,2,1,0:T(8,128)S(1)}, u32[]{:S(2)}) %copy-start.2) | copy-done | bytes 6291480
  40.5 0.7 convert.8
  41.4 2.6 %collective-permute-start.1 = (f16[6,32,512]{2,1,0:T(8,128)(2,1)S(1)}, f16[6,32,512]{2,1,0:T(8,128)(2,1)S(1)}, u32[]{:S(2)}, u32[]{:S(2)}) collective-permute-start(f16[6,32,512]{2,1,0:T(8,128)(2,1)S(1)} %get-tuple-element.63), channel_id=1, source_target_pairs={{0,2},{1,3},{2,6},{3,7},{6,10},{7,11},{10,14},{11,15},{14,12},{15,... | collective-permute-start | bytes 589832 | tf_op jit(solution)/shard_map/ppermute | solution.py:242
  44.1 1.0 copy.27
  45.2 3.1 %spread_taps.1 = (bf16[2,3,384,256]{3,2,1,0:T(8,128)(2,1)}, bf16[2,3,512,256]{3,2,1,0:T(8,128)(2,1)}) custom-call(bf16[36,64,64]{2,1,0:T(8,128)(2,1)} %bitcast.150), custom_call_target="tpu_custom_call" | custom-call | bytes 6291456 | tf_op jit(solution)/shard_map/spread_taps/pallas_call | solution.py:437
  48.2 1.4 collective-permute-done.1
  49.6 1.4 collective-permute-done.2
  51.0 1.2 fusion.26
  52.3 1.6 collective-permute-start.3
  53.9 0.4 collective-permute-start.4
  54.3 5.7 %value_project.1.v_ref = bf16[12,512,256]{2,1,0:T(8,128)(2,1)S(1)} custom-call(bf16[4,512,768]{2,1,0:T(8,128)(2,1)} %copy-done.3, bf16[768,2304]{1,0:T(8,128)(2,1)} %w_ref.1), custom_call_target="tpu_custom_call" | custom-call | flops 2415919104 | bytes 7471104 | tf_op jit(solution)/shard_map/value_project/pallas_call | solution.py:168
  60.1 1.6 collective-permute-start.7
  61.7 0.4 collective-permute-start.8
  62.3 1.6 collective-permute-start.5
  63.9 0.4 collective-permute-start.6
  64.4 3.4 %collective-permute-done.7 = f16[6,32,512]{2,1,0:T(8,128)(2,1)S(1)} collective-permute-done((f16[6,32,512]{2,1,0:T(8,128)(2,1)S(1)}, f16[6,32,512]{2,1,0:T(8,128)(2,1)S(1)}, u32[]{:S(2)}, u32[]{:S(2)}) %collective-permute-start.7) | collective-permute-done | bytes 196640 | tf_op jit(solution)/shard_map/ppermute | solution.py:242
  67.8 1.3 collective-permute-done.8
  69.2 1.6 collective-permute-start.10
  70.9 0.4 collective-permute-start.11
  71.3 0.7 collective-permute-done.5
  72.0 1.3 collective-permute-done.6
  73.4 1.6 collective-permute-done.10
  75.0 1.9 collective-permute-done.11
  76.9 0.5 collective-permute-start.12
  77.4 1.7 collective-permute-start.9
  79.1 0.4 collective-permute-start.14
  79.5 3.4 %collective-permute-done.12 = f16[6,32,512]{2,1,0:T(8,128)(2,1)S(1)} collective-permute-done((f16[6,32,512]{2,1,0:T(8,128)(2,1)S(1)}, f16[6,32,512]{2,1,0:T(8,128)(2,1)S(1)}, u32[]{:S(2)}, u32[]{:S(2)}) %collective-permute-start.12) | collective-permute-done | bytes 196640 | tf_op jit(solution)/shard_map/ppermute | solution.py:242
  82.9 2.1 %collective-permute-done.9 = f16[6,32,512]{2,1,0:T(8,128)(2,1)S(1)} collective-permute-done((f16[6,32,512]{2,1,0:T(8,128)(2,1)S(1)}, f16[6,32,512]{2,1,0:T(8,128)(2,1)S(1)}, u32[]{:S(2)}, u32[]{:S(2)}) %collective-permute-start.9) | collective-permute-done | bytes 196640 | tf_op jit(solution)/shard_map/ppermute | solution.py:242
  85.1 1.6 collective-permute-start.13
  98.0 1.1 fusion.10
  99.2 0.3 fusion.4
  99.5 1.0 divide_convert_fusion
  100.5 1.9 collective-permute-start.16
  108.4 0.8 broadcast_in_dim.61
  109.2 0.2 fusion.6
  109.4 2.8 %collective-permute-done.16 = bf16[6,64,512]{2,1,0:T(8,128)(2,1)S(1)} collective-permute-done((bf16[6,64,512]{2,1,0:T(8,128)(2,1)}, bf16[6,64,512]{2,1,0:T(8,128)(2,1)S(1)}, u32[]{:S(2)}, u32[]{:S(2)}) %collective-permute-start.16) | collective-permute-done | bytes 393248 | tf_op jit(solution)/shard_map/ppermute | solution.py:242
  112.2 1.9 collective-permute-start.20
  114.5 9.2 %collective-permute-done.20 = bf16[6,64,512]{2,1,0:T(8,128)(2,1)S(1)} collective-permute-done((bf16[6,64,512]{2,1,0:T(8,128)(2,1)S(1)}, bf16[6,64,512]{2,1,0:T(8,128)(2,1)S(1)}, u32[]{:S(2)}, u32[]{:S(2)}) %collective-permute-start.20) | collective-permute-done | bytes 393248 | tf_op jit(solution)/shard_map/ppermute | solution.py:242
  123.7 1.9 collective-permute-start.24
  126.2 9.1 %collective-permute-done.24 = bf16[6,64,512]{2,1,0:T(8,128)(2,1)S(1)} collective-permute-done((bf16[6,64,512]{2,1,0:T(8,128)(2,1)S(1)}, bf16[6,64,512]{2,1,0:T(8,128)(2,1)S(1)}, u32[]{:S(2)}, u32[]{:S(2)}) %collective-permute-start.24) | collective-permute-done | bytes 393248 | tf_op jit(solution)/shard_map/ppermute | solution.py:242
  135.3 2.0 collective-permute-start.28
  137.3 0.5 collective-permute-start.30
  137.7 0.5 collective-permute-start.27
  138.4 3.5 %collective-permute-done.28 = bf16[6,32,512]{2,1,0:T(8,128)(2,1)S(1)} collective-permute-done((bf16[6,32,512]{2,1,0:T(8,128)(2,1)S(1)}, bf16[6,32,512]{2,1,0:T(8,128)(2,1)S(1)}, u32[]{:S(2)}, u32[]{:S(2)}) %collective-permute-start.28) | collective-permute-done | bytes 196640 | tf_op jit(solution)/shard_map/ppermute | solution.py:242
  141.9 1.9 collective-permute-done.30
  144.0 1.2 collective-permute-done.31
  145.2 2.6 %copy-done = bf16[2,8,6,64,512]{4,3,2,1,0:T(8,128)(2,1)} copy-done((bf16[2,8,6,64,512]{4,3,2,1,0:T(8,128)(2,1)}, bf16[2,8,6,64,512]{4,3,2,1,0:T(8,128)(2,1)S(1)}, u32[]{:S(2)}) %copy-start) | copy-done | bytes 6291480
  147.9 0.9 convert_bitcast_fusion
  148.7 2.2 %copy.29 = f32[48,2,6,8,64]{4,3,0,2,1:T(8,128)} copy(f32[48,2,6,8,64]{0,4,2,3,1:T(8,128)S(1)} %convert_bitcast_fusion) | data formatting | bytes 2359296 | tf_op jit(solution)/shard_map/convert_element_type | solution.py:465
  150.9 2.8 %reshape.97 = f32[48,12,512]{2,0,1:T(8,128)} reshape(f32[48,2,6,8,64]{4,3,0,2,1:T(8,128)} %copy.29) | data formatting | bytes 2359296 | tf_op jit(solution)/shard_map/convert_element_type | solution.py:465
  153.7 3.6 %copy.28 = bf16[8,64,2,6,512]{4,1,0,3,2:T(8,128)(2,1)S(1)} copy(bf16[8,64,2,6,512]{4,1,3,0,2:T(8,128)(2,1)} %bitcast.144) | data formatting | bytes 12582912 | tf_op jit(solution)/shard_map/transpose | solution.py:456
  157.6 1.2 copy.30
  158.8 2.0 reshape.96.pf_ref
  160.8 2.8 %copy-done.1 = bf16[2,8,6,64,512]{4,3,2,1,0:T(8,128)(2,1)S(1)} copy-done((bf16[2,8,6,64,512]{4,3,2,1,0:T(8,128)(2,1)S(1)}, bf16[2,8,6,64,512]{4,3,2,1,0:T(8,128)(2,1)}, u32[]{:S(2)}) %copy-start.1) | copy-done | bytes 6291480
  163.6 4.8 %row_mix.1 = bf16[4,512,768]{2,1,0:T(8,128)(2,1)} custom-call(bf16[2,8,6,64,512]{4,3,2,1,0:T(8,128)(2,1)S(1)} %copy-done.1, bf16[12,512,256]{2,1,0:T(8,128)(2,1)S(1)} %copy-done.5), custom_call_target="tpu_custom_call" | custom-call | flops 1610612736 | bytes 12582912 | tf_op jit(solution)/shard_map/row_mix/pallas_call | solution.py:208
  168.4 32.6 %contact_head.1 = f32[32,512]{1,0:T(8,128)} custom-call(s32[1]{0:T(128)} %bitcast.51.row_ref, bf16[12,48,512]{2,1,0:T(8,128)(2,1)S(1)} %copy-done.6, bf16[48,256]{1,0:T(8,128)(2,1)S(1)} %mul.68.pair_ref, bf16[2,3,384,256]{3,2,1,0:T(8,128)(2,1)S(1)} %copy-done.8, bf16[2,3,512,256]{3,2,1,0:T(8,128)(2,1)S(1)} %copy-done.7, ...), custom_call_target="tpu_custom_call" | custom-call | flops 5469372416 | bytes 4194304 | tf_op jit(solution)/shard_map/contact_head/pallas_call | solution.py:473
  (91 shorter events, 3.0 us)
Async XLA Ops:
  0.6 11.0 %copy-start.14 = (s32[8]{0:T(128)S(1)}, s32[8]{0:T(128)}, u32[]{:S(2)}) copy-start(s32[8]{0:T(128)} %constant.135.clone) | copy-start | bytes 100
  0.6 21.3 %copy-start.11 = (s32[8]{0:T(128)S(1)}, s32[8]{0:T(128)}, u32[]{:S(2)}) copy-start(s32[8]{0:T(128)} %constant.136.clone) | copy-start | bytes 100
  9.5 1.7 copy-start.3
  11.1 22.5 %collective-permute-start = (bf16[2,6,512,256]{3,2,1,0:T(8,128)(2,1)}, bf16[2,6,512,256]{3,2,1,0:T(8,128)(2,1)S(1)}, u32[]{:S(2)}, u32[]{:S(2)}) collective-permute-start(bf16[2,6,512,256]{3,2,1,0:T(8,128)(2,1)} %get-tuple-element.27), channel_id=1, source_target_pairs={{0,1},{1,0},{2,3},{3,2},{4,5},{5,4},{6,7},{7,6},{8,9},{9,8},{10,11... | collective-permute-start | bytes 9437192 | tf_op jit(solution)/shard_map/ppermute | solution.py:245
  37.9 2.6 %copy-start.2 = (f32[8,6,64,512]{3,2,1,0:T(8,128)}, f32[8,6,64,512]{3,2,1,0:T(8,128)S(1)}, u32[]{:S(2)}) copy-start(f32[8,6,64,512]{3,2,1,0:T(8,128)S(1)} %scores.1) | copy-start | bytes 18874372
  40.5 3.6 %copy-start.10 = (bf16[4,9,64,64]{3,2,1,0:T(8,128)(2,1)S(1)}, bf16[4,9,64,64]{3,2,1,0:T(8,128)(2,1)}, u32[]{:S(2)}) copy-start(bf16[4,9,64,64]{3,2,1,0:T(8,128)(2,1)} %param.28) | copy-start | bytes 884740
  41.4 8.2 %collective-permute-start.1 = (f16[6,32,512]{2,1,0:T(8,128)(2,1)S(1)}, f16[6,32,512]{2,1,0:T(8,128)(2,1)S(1)}, u32[]{:S(2)}, u32[]{:S(2)}) collective-permute-start(f16[6,32,512]{2,1,0:T(8,128)(2,1)S(1)} %get-tuple-element.63), channel_id=1, source_target_pairs={{0,2},{1,3},{2,6},{3,7},{6,10},{7,11},{10,14},{11,15},{14,12},{15,... | collective-permute-start | bytes 589832 | tf_op jit(solution)/shard_map/ppermute | solution.py:242
  44.0 7.0 %collective-permute-start.2 = (f16[6,32,512]{2,1,0:T(8,128)(2,1)S(1)}, f16[6,32,512]{2,1,0:T(8,128)(2,1)S(1)}, u32[]{:S(2)}, u32[]{:S(2)}) collective-permute-start(f16[6,32,512]{2,1,0:T(8,128)(2,1)S(1)} %get-tuple-element.62), channel_id=1, source_target_pairs={{0,4},{1,5},{2,0},{3,1},{6,2},{7,3},{10,6},{11,7},{14,10},{15,11},... | collective-permute-start | bytes 589832 | tf_op jit(solution)/shard_map/ppermute | solution.py:242
  45.2 17.0 %slice-start = ((s8[6291456]{0:T(1024)(128)(4,1)}), s8[2097152]{0:T(1024)(128)(4,1)S(1)}, s32[]{:S(2)}) async-start(s8[6291456]{0:T(1024)(128)(4,1)} %bitcast.145), calls=%async_computation | async-start | bytes 4194304
  52.3 9.9 %collective-permute-start.3 = (f16[6,32,512]{2,1,0:T(8,128)(2,1)S(1)}, f16[6,32,512]{2,1,0:T(8,128)(2,1)S(1)}, u32[]{:S(2)}, u32[]{:S(2)}) collective-permute-start(f16[6,32,512]{2,1,0:T(8,128)(2,1)S(1)} %get-tuple-element.59), channel_id=1, source_target_pairs={{0,2},{1,3},{2,6},{3,7},{6,10},{7,11},{10,14},{11,15},{14,12},{15,... | collective-permute-start | bytes 589832 | tf_op jit(solution)/shard_map/ppermute | solution.py:242
  53.9 8.3 %slice-start.1 = ((s8[6291456]{0:T(1024)(128)(4,1)}), s8[4194304]{0:T(1024)(128)(4,1)S(1)}, s32[]{:S(2)}) async-start(s8[6291456]{0:T(1024)(128)(4,1)} %bitcast.145), calls=%async_computation.1 | async-start | bytes 8388608
  53.9 8.3 %collective-permute-start.4 = (f16[6,32,512]{2,1,0:T(8,128)(2,1)S(1)}, f16[6,32,512]{2,1,0:T(8,128)(2,1)S(1)}, u32[]{:S(2)}, u32[]{:S(2)}) collective-permute-start(f16[6,32,512]{2,1,0:T(8,128)(2,1)S(1)} %get-tuple-element.58), channel_id=1, source_target_pairs={{0,4},{1,5},{2,0},{3,1},{6,2},{7,3},{10,6},{11,7},{14,10},{15,11},... | collective-permute-start | bytes 589832 | tf_op jit(solution)/shard_map/ppermute | solution.py:242
  60.0 25.0 %copy-start.4 = (bf16[12,512,256]{2,1,0:T(8,128)(2,1)}, bf16[12,512,256]{2,1,0:T(8,128)(2,1)S(1)}, u32[]{:S(2)}) copy-start(bf16[12,512,256]{2,1,0:T(8,128)(2,1)S(1)} %value_project.1.v_ref) | copy-start | bytes 9437188
  60.0 42.4 %copy-start.12 = (bf16[64,12]{0,1:T(8,128)(2,1)S(1)}, bf16[64,12]{0,1:T(8,128)(2,1)}, u32[]{:S(2)}) copy-start(bf16[64,12]{0,1:T(8,128)(2,1)} %param.27) | copy-start | bytes 4612
  60.1 42.6 %copy-start.13 = (f32[64]{0:T(128)S(1)}, f32[64]{0:T(128)}, u32[]{:S(2)}) copy-start(f32[64]{0:T(128)} %param.29) | copy-start | bytes 772
  60.1 7.7 %collective-permute-start.7 = (f16[6,32,512]{2,1,0:T(8,128)(2,1)S(1)}, f16[6,32,512]{2,1,0:T(8,128)(2,1)S(1)}, u32[]{:S(2)}, u32[]{:S(2)}) collective-permute-start(f16[6,32,512]{2,1,0:T(8,128)(2,1)S(1)} %get-tuple-element.61), channel_id=1, source_target_pairs={{0,2},{1,3},{2,6},{3,7},{6,10},{7,11},{10,14},{11,15},{14,12},{15,... | collective-permute-start | bytes 589832 | tf_op jit(solution)/shard_map/ppermute | solution.py:242
  61.7 7.4 %collective-permute-start.8 = (f16[6,32,512]{2,1,0:T(8,128)(2,1)S(1)}, f16[6,32,512]{2,1,0:T(8,128)(2,1)S(1)}, u32[]{:S(2)}, u32[]{:S(2)}) collective-permute-start(f16[6,32,512]{2,1,0:T(8,128)(2,1)S(1)} %get-tuple-element.60), channel_id=1, source_target_pairs={{0,4},{1,5},{2,0},{3,1},{6,2},{7,3},{10,6},{11,7},{14,10},{15,11},... | collective-permute-start | bytes 589832 | tf_op jit(solution)/shard_map/ppermute | solution.py:242
  62.3 9.7 %collective-permute-start.5 = (f16[6,32,512]{2,1,0:T(8,128)(2,1)S(1)}, f16[6,32,512]{2,1,0:T(8,128)(2,1)S(1)}, u32[]{:S(2)}, u32[]{:S(2)}) collective-permute-start(f16[6,32,512]{2,1,0:T(8,128)(2,1)S(1)} %get-tuple-element.57), channel_id=1, source_target_pairs={{0,2},{1,3},{2,6},{3,7},{6,10},{7,11},{10,14},{11,15},{14,12},{15,... | collective-permute-start | bytes 589832 | tf_op jit(solution)/shard_map/ppermute | solution.py:242
  63.9 9.3 %collective-permute-start.6 = (f16[6,32,512]{2,1,0:T(8,128)(2,1)S(1)}, f16[6,32,512]{2,1,0:T(8,128)(2,1)S(1)}, u32[]{:S(2)}, u32[]{:S(2)}) collective-permute-start(f16[6,32,512]{2,1,0:T(8,128)(2,1)S(1)} %get-tuple-element.56), channel_id=1, source_target_pairs={{0,4},{1,5},{2,0},{3,1},{6,2},{7,3},{10,6},{11,7},{14,10},{15,11},... | collective-permute-start | bytes 589832 | tf_op jit(solution)/shard_map/ppermute | solution.py:242
  69.2 5.7 %collective-permute-start.10 = (f16[6,32,512]{2,1,0:T(8,128)(2,1)S(1)}, f16[6,32,512]{2,1,0:T(8,128)(2,1)S(1)}, u32[]{:S(2)}, u32[]{:S(2)}) collective-permute-start(f16[6,32,512]{2,1,0:T(8,128)(2,1)S(1)} %get-tuple-element.55), channel_id=1, source_target_pairs={{0,2},{1,3},{2,6},{3,7},{6,10},{7,11},{10,14},{11,15},{14,12},{15,... | collective-permute-start | bytes 589832 | tf_op jit(solution)/shard_map/ppermute | solution.py:242
  70.9 6.0 %collective-permute-start.11 = (f16[6,32,512]{2,1,0:T(8,128)(2,1)S(1)}, f16[6,32,512]{2,1,0:T(8,128)(2,1)S(1)}, u32[]{:S(2)}, u32[]{:S(2)}) collective-permute-start(f16[6,32,512]{2,1,0:T(8,128)(2,1)S(1)} %get-tuple-element.54), channel_id=1, source_target_pairs={{0,4},{1,5},{2,0},{3,1},{6,2},{7,3},{10,6},{11,7},{14,10},{15,11},... | collective-permute-start | bytes 589832 | tf_op jit(solution)/shard_map/ppermute | solution.py:242
  76.9 5.9 %collective-permute-start.12 = (f16[6,32,512]{2,1,0:T(8,128)(2,1)S(1)}, f16[6,32,512]{2,1,0:T(8,128)(2,1)S(1)}, u32[]{:S(2)}, u32[]{:S(2)}) collective-permute-start(f16[6,32,512]{2,1,0:T(8,128)(2,1)S(1)} %fusion.12), channel_id=1, source_target_pairs={{0,4},{1,5},{2,0},{3,1},{6,2},{7,3},{10,6},{11,7},{14,10},{15,11},... | collective-permute-start | bytes 589832 | tf_op jit(solution)/shard_map/ppermute | solution.py:242
  77.4 7.5 %collective-permute-start.9 = (f16[6,32,512]{2,1,0:T(8,128)(2,1)S(1)}, f16[6,32,512]{2,1,0:T(8,128)(2,1)S(1)}, u32[]{:S(2)}, u32[]{:S(2)}) collective-permute-start(f16[6,32,512]{2,1,0:T(8,128)(2,1)S(1)} %get-tuple-element.52), channel_id=1, source_target_pairs={{0,2},{1,3},{2,6},{3,7},{6,10},{7,11},{10,14},{11,15},{14,12},{15,... | collective-permute-start | bytes 589832 | tf_op jit(solution)/shard_map/ppermute | solution.py:242
  79.1 18.9 %collective-permute-start.14 = (f16[6,32,512]{2,1,0:T(8,128)(2,1)S(1)}, f16[6,32,512]{2,1,0:T(8,128)(2,1)S(1)}, u32[]{:S(2)}, u32[]{:S(2)}) collective-permute-start(f16[6,32,512]{2,1,0:T(8,128)(2,1)S(1)} %get-tuple-element.53), channel_id=1, source_target_pairs={{0,4},{1,5},{2,0},{3,1},{6,2},{7,3},{10,6},{11,7},{14,10},{15,11},... | collective-permute-start | bytes 589832 | tf_op jit(solution)/shard_map/ppermute | solution.py:242
  85.1 12.9 %collective-permute-start.13 = (f16[6,32,512]{2,1,0:T(8,128)(2,1)S(1)}, f16[6,32,512]{2,1,0:T(8,128)(2,1)S(1)}, u32[]{:S(2)}, u32[]{:S(2)}) collective-permute-start(f16[6,32,512]{2,1,0:T(8,128)(2,1)S(1)} %get-tuple-element.51), channel_id=1, source_target_pairs={{0,2},{1,3},{2,6},{3,7},{6,10},{7,11},{10,14},{11,15},{14,12},{15,... | collective-permute-start | bytes 589832 | tf_op jit(solution)/shard_map/ppermute | solution.py:242
  100.5 14.0 %collective-permute-start.15 = (bf16[6,64,512]{2,1,0:T(8,128)(2,1)}, bf16[6,64,512]{2,1,0:T(8,128)(2,1)S(1)}, u32[]{:S(2)}, u32[]{:S(2)}) collective-permute-start(bf16[6,64,512]{2,1,0:T(8,128)(2,1)} %divide_convert_fusion), channel_id=1, source_target_pairs={{0,1},{1,0},{2,3},{3,2},{4,5},{5,4},{6,7},{7,6},{8,9},{9,8},{10,11... | collective-permute-start | bytes 1179656 | tf_op jit(solution)/shard_map/ppermute | solution.py:245
  100.5 11.7 %collective-permute-start.16 = (bf16[6,64,512]{2,1,0:T(8,128)(2,1)}, bf16[6,64,512]{2,1,0:T(8,128)(2,1)S(1)}, u32[]{:S(2)}, u32[]{:S(2)}) collective-permute-start(bf16[6,64,512]{2,1,0:T(8,128)(2,1)} %divide_convert_fusion), channel_id=1, source_target_pairs={{0,2},{1,3},{2,6},{3,7},{6,10},{7,11},{10,14},{11,15},{14,12},{15,... | collective-permute-start | bytes 1179656 | tf_op jit(solution)/shard_map/ppermute | solution.py:242
  102.4 11.7 %collective-permute-start.18 = (bf16[6,64,512]{2,1,0:T(8,128)(2,1)}, bf16[6,64,512]{2,1,0:T(8,128)(2,1)S(1)}, u32[]{:S(2)}, u32[]{:S(2)}) collective-permute-start(bf16[6,64,512]{2,1,0:T(8,128)(2,1)} %divide_convert_fusion), channel_id=1, source_target_pairs={{0,4},{1,5},{2,0},{3,1},{6,2},{7,3},{10,6},{11,7},{14,10},{15,11},... | collective-permute-start | bytes 1179656 | tf_op jit(solution)/shard_map/ppermute | solution.py:242
  112.2 13.7 %collective-permute-start.17 = (bf16[6,64,512]{2,1,0:T(8,128)(2,1)S(1)}, bf16[6,64,512]{2,1,0:T(8,128)(2,1)S(1)}, u32[]{:S(2)}, u32[]{:S(2)}) collective-permute-start(bf16[6,64,512]{2,1,0:T(8,128)(2,1)S(1)} %collective-permute-done.16), channel_id=1, source_target_pairs={{0,1},{1,0},{2,3},{3,2},{4,5},{5,4},{6,7},{7,6},{8,9},{9,8},{10,11... | collective-permute-start | bytes 1179656 | tf_op jit(solution)/shard_map/ppermute | solution.py:245
  112.2 11.5 %collective-permute-start.20 = (bf16[6,64,512]{2,1,0:T(8,128)(2,1)S(1)}, bf16[6,64,512]{2,1,0:T(8,128)(2,1)S(1)}, u32[]{:S(2)}, u32[]{:S(2)}) collective-permute-start(bf16[6,64,512]{2,1,0:T(8,128)(2,1)S(1)} %collective-permute-done.16), channel_id=1, source_target_pairs={{0,2},{1,3},{2,6},{3,7},{6,10},{7,11},{10,14},{11,15},{14,12},{15,... | collective-permute-start | bytes 1179656 | tf_op jit(solution)/shard_map/ppermute | solution.py:242
  114.1 12.0 %collective-permute-start.19 = (bf16[6,64,512]{2,1,0:T(8,128)(2,1)S(1)}, bf16[6,64,512]{2,1,0:T(8,128)(2,1)S(1)}, u32[]{:S(2)}, u32[]{:S(2)}) collective-permute-start(bf16[6,64,512]{2,1,0:T(8,128)(2,1)S(1)} %collective-permute-done.18), channel_id=1, source_target_pairs={{0,1},{1,0},{2,3},{3,2},{4,5},{5,4},{6,7},{7,6},{8,9},{9,8},{10,11... | collective-permute-start | bytes 1179656 | tf_op jit(solution)/shard_map/ppermute | solution.py:245
  114.3 11.3 %collective-permute-start.22 = (bf16[6,64,512]{2,1,0:T(8,128)(2,1)S(1)}, bf16[6,64,512]{2,1,0:T(8,128)(2,1)S(1)}, u32[]{:S(2)}, u32[]{:S(2)}) collective-permute-start(bf16[6,64,512]{2,1,0:T(8,128)(2,1)S(1)} %collective-permute-done.18), channel_id=1, source_target_pairs={{0,4},{1,5},{2,0},{3,1},{6,2},{7,3},{10,6},{11,7},{14,10},{15,11},... | collective-permute-start | bytes 1179656 | tf_op jit(solution)/shard_map/ppermute | solution.py:242
  123.7 14.0 %collective-permute-start.21 = (bf16[6,64,512]{2,1,0:T(8,128)(2,1)S(1)}, bf16[6,64,512]{2,1,0:T(8,128)(2,1)S(1)}, u32[]{:S(2)}, u32[]{:S(2)}) collective-permute-start(bf16[6,64,512]{2,1,0:T(8,128)(2,1)S(1)} %collective-permute-done.20), channel_id=1, source_target_pairs={{0,1},{1,0},{2,3},{3,2},{4,5},{5,4},{6,7},{7,6},{8,9},{9,8},{10,11... | collective-permute-start | bytes 1179656 | tf_op jit(solution)/shard_map/ppermute | solution.py:245
  123.7 11.5 %collective-permute-start.24 = (bf16[6,64,512]{2,1,0:T(8,128)(2,1)S(1)}, bf16[6,64,512]{2,1,0:T(8,128)(2,1)S(1)}, u32[]{:S(2)}, u32[]{:S(2)}) collective-permute-start(bf16[6,64,512]{2,1,0:T(8,128)(2,1)S(1)} %collective-permute-done.20), channel_id=1, source_target_pairs={{0,2},{1,3},{2,6},{3,7},{6,10},{7,11},{10,14},{11,15},{14,12},{15,... | collective-permute-start | bytes 1179656 | tf_op jit(solution)/shard_map/ppermute | solution.py:242
  125.6 12.7 %collective-permute-start.23 = (bf16[6,64,512]{2,1,0:T(8,128)(2,1)S(1)}, bf16[6,64,512]{2,1,0:T(8,128)(2,1)S(1)}, u32[]{:S(2)}, u32[]{:S(2)}) collective-permute-start(bf16[6,64,512]{2,1,0:T(8,128)(2,1)S(1)} %collective-permute-done.22), channel_id=1, source_target_pairs={{0,1},{1,0},{2,3},{3,2},{4,5},{5,4},{6,7},{7,6},{8,9},{9,8},{10,11... | collective-permute-start | bytes 1179656 | tf_op jit(solution)/shard_map/ppermute | solution.py:245
  125.9 11.4 %collective-permute-start.26 = (bf16[6,64,512]{2,1,0:T(8,128)(2,1)S(1)}, bf16[6,64,512]{2,1,0:T(8,128)(2,1)S(1)}, u32[]{:S(2)}, u32[]{:S(2)}) collective-permute-start(bf16[6,64,512]{2,1,0:T(8,128)(2,1)S(1)} %collective-permute-done.22), channel_id=1, source_target_pairs={{0,4},{1,5},{2,0},{3,1},{6,2},{7,3},{10,6},{11,7},{14,10},{15,11},... | collective-permute-start | bytes 1179656 | tf_op jit(solution)/shard_map/ppermute | solution.py:242
  135.3 6.6 %collective-permute-start.28 = (bf16[6,32,512]{2,1,0:T(8,128)(2,1)S(1)}, bf16[6,32,512]{2,1,0:T(8,128)(2,1)S(1)}, u32[]{:S(2)}, u32[]{:S(2)}) collective-permute-start(bf16[6,32,512]{2,1,0:T(8,128)(2,1)S(1)} %slice.92), channel_id=1, source_target_pairs={{0,2},{1,3},{2,6},{3,7},{6,10},{7,11},{10,14},{11,15},{14,12},{15,... | collective-permute-start | bytes 589832 | tf_op jit(solution)/shard_map/ppermute | solution.py:242
  137.3 6.5 %collective-permute-start.30 = (bf16[6,32,512]{2,1,0:T(8,128)(2,1)S(1)}, bf16[6,32,512]{2,1,0:T(8,128)(2,1)S(1)}, u32[]{:S(2)}, u32[]{:S(2)}) collective-permute-start(bf16[6,32,512]{2,1,0:T(8,128)(2,1)S(1)} %slice.93), channel_id=1, source_target_pairs={{0,4},{1,5},{2,0},{3,1},{6,2},{7,3},{10,6},{11,7},{14,10},{15,11},... | collective-permute-start | bytes 589832 | tf_op jit(solution)/shard_map/ppermute | solution.py:242
  137.7 6.0 %collective-permute-start.25 = (bf16[6,64,512]{2,1,0:T(8,128)(2,1)S(1)}, bf16[6,64,512]{2,1,0:T(8,128)(2,1)S(1)}, u32[]{:S(2)}, u32[]{:S(2)}) collective-permute-start(bf16[6,64,512]{2,1,0:T(8,128)(2,1)S(1)} %collective-permute-done.24), channel_id=1, source_target_pairs={{0,1},{1,0},{2,3},{3,2},{4,5},{5,4},{6,7},{7,6},{8,9},{9,8},{10,11... | collective-permute-start | bytes 1179656 | tf_op jit(solution)/shard_map/ppermute | solution.py:245
  137.7 6.1 %collective-permute-start.27 = (bf16[6,64,512]{2,1,0:T(8,128)(2,1)S(1)}, bf16[6,64,512]{2,1,0:T(8,128)(2,1)S(1)}, u32[]{:S(2)}, u32[]{:S(2)}) collective-permute-start(bf16[6,64,512]{2,1,0:T(8,128)(2,1)S(1)} %collective-permute-done.26), channel_id=1, source_target_pairs={{0,1},{1,0},{2,3},{3,2},{4,5},{5,4},{6,7},{7,6},{8,9},{9,8},{10,11... | collective-permute-start | bytes 1179656 | tf_op jit(solution)/shard_map/ppermute | solution.py:245
  141.9 2.1 %collective-permute-start.29 = (bf16[6,32,512]{2,1,0:T(8,128)(2,1)S(1)}, bf16[6,32,512]{2,1,0:T(8,128)(2,1)S(1)}, u32[]{:S(2)}, u32[]{:S(2)}) collective-permute-start(bf16[6,32,512]{2,1,0:T(8,128)(2,1)S(1)} %collective-permute-done.28), channel_id=1, source_target_pairs={{0,1},{1,0},{2,3},{3,2},{4,5},{5,4},{6,7},{7,6},{8,9},{9,8},{10,11... | collective-permute-start | bytes 589832 | tf_op jit(solution)/shard_map/ppermute | solution.py:245
  143.7 1.4 collective-permute-start.31
  145.2 2.7 %copy-start = (bf16[2,8,6,64,512]{4,3,2,1,0:T(8,128)(2,1)}, bf16[2,8,6,64,512]{4,3,2,1,0:T(8,128)(2,1)S(1)}, u32[]{:S(2)}) copy-start(bf16[2,8,6,64,512]{4,3,2,1,0:T(8,128)(2,1)S(1)} %bitcast_dynamic-update-slice_fusion.13.p_ref) | copy-start | bytes 18874372
  153.7 3.7 %copy-start.9 = (f32[48,12,512]{2,0,1:T(8,128)S(1)}, f32[48,12,512]{2,0,1:T(8,128)}, u32[]{:S(2)}) copy-start(f32[48,12,512]{2,0,1:T(8,128)} %reshape.97) | copy-start | bytes 3538948
  157.4 3.5 %copy-start.5 = (bf16[12,512,256]{2,1,0:T(8,128)(2,1)S(1)}, bf16[12,512,256]{2,1,0:T(8,128)(2,1)}, u32[]{:S(2)}) copy-start(bf16[12,512,256]{2,1,0:T(8,128)(2,1)} %copy-done.4) | copy-start | bytes 9437188
  160.8 2.8 %copy-start.1 = (bf16[2,8,6,64,512]{4,3,2,1,0:T(8,128)(2,1)S(1)}, bf16[2,8,6,64,512]{4,3,2,1,0:T(8,128)(2,1)}, u32[]{:S(2)}) copy-start(bf16[2,8,6,64,512]{4,3,2,1,0:T(8,128)(2,1)} %copy-done) | copy-start | bytes 18874372
  163.6 4.8 %copy-start.6 = (bf16[12,48,512]{2,1,0:T(8,128)(2,1)S(1)}, bf16[12,48,512]{2,1,0:T(8,128)(2,1)}, u32[]{:S(2)}) copy-start(bf16[12,48,512]{2,1,0:T(8,128)(2,1)} %reshape.96.pf_ref) | copy-start | bytes 1769476
  163.6 4.8 %copy-start.7 = (bf16[2,3,512,256]{3,2,1,0:T(8,128)(2,1)S(1)}, bf16[2,3,512,256]{3,2,1,0:T(8,128)(2,1)}, u32[]{:S(2)}) copy-start(bf16[2,3,512,256]{3,2,1,0:T(8,128)(2,1)} %get-tuple-element.49.far_ref) | copy-start | bytes 4718596
  163.6 4.8 %copy-start.8 = (bf16[2,3,384,256]{3,2,1,0:T(8,128)(2,1)S(1)}, bf16[2,3,384,256]{3,2,1,0:T(8,128)(2,1)}, u32[]{:S(2)}) copy-start(bf16[2,3,384,256]{3,2,1,0:T(8,128)(2,1)} %get-tuple-element.48.near_ref) | copy-start | bytes 3538948

commit v2 on v1

--- a/solution.py
+++ b/solution.py
@@ -1,5 +1,4 @@
 import functools
-import math
 
 import jax
 import jax.numpy as jnp
@@ -41,7 +40,13 @@
     return out
 
 
-def norm_send_kernel(half_ref, use_ref, x_ref, wq_ref, wk_ref, normed_ref, qk_ref):
+def ring_place(index_ref, table_ref, ahead):
+    chips = table_ref.shape[0] // 2
+    place = table_ref[lax.div(index_ref[0], 2)]
+    return table_ref[chips + lax.rem(place + ahead, chips)]
+
+
+def norm_send_kernel(index_ref, depth_ref, x_ref, wq_ref, wk_ref, normed_ref, qk_ref):
     seqs, rows, width = x_ref.shape
     size = qk_ref.shape[3] // seqs
     values = x_ref[...].reshape(seqs * rows, width).astype(jnp.float32)
@@ -50,21 +55,22 @@
     variance = jnp.mean(centered * centered, axis=-1, keepdims=True)
     normed = (centered * lax.rsqrt(variance + EPSILON)).astype(jnp.bfloat16)
     normed_ref[...] = normed.reshape(seqs, rows, width)
-    project(use_ref, normed, wq_ref, wk_ref, qk_ref, seqs, rows, size)
-
-
-def own_kernel(half_ref, use_ref, normed_ref, wq_ref, wk_ref, qk_ref):
+    project(index_ref, depth_ref, normed, wq_ref, wk_ref, qk_ref, seqs, rows, size)
+
+
+def own_kernel(index_ref, depth_ref, normed_ref, wq_ref, wk_ref, qk_ref):
     seqs, rows, width = normed_ref.shape
     size = qk_ref.shape[3] // seqs
     normed = normed_ref[...].reshape(seqs * rows, width)
-    project(use_ref, normed, wq_ref, wk_ref, qk_ref, seqs, rows, size)
-
-
-def project(use_ref, normed, wq_ref, wk_ref, qk_ref, seqs, rows, size):
+    project(index_ref, depth_ref, normed, wq_ref, wk_ref, qk_ref, seqs, rows, size)
+
+
+def project(index_ref, depth_ref, normed, wq_ref, wk_ref, qk_ref, seqs, rows, size):
     q = jnp.dot(normed, wq_ref[...], preferred_element_type=jnp.float32).astype(jnp.bfloat16)
     for head, block in enumerate(head_major(q, seqs, rows, size)):
         lane = lax.broadcasted_iota(jnp.int32, block.shape, 1)
-        qk_ref[0, head] = jnp.where(lane < use_ref[0] * size, block, jnp.zeros_like(block))
+        in_use = (depth_ref[0] - index_ref[0] * seqs) * size
+        qk_ref[0, head] = jnp.where(lane < in_use, block, jnp.zeros_like(block))
     k = jnp.dot(normed, wk_ref[...], preferred_element_type=jnp.float32).astype(jnp.bfloat16)
     for head, block in enumerate(head_major(k, seqs, rows, size)):
         qk_ref[1, head] = block
@@ -79,46 +85,52 @@
         v_ref[head] = block
 
 
-def score_kernel(order_ref, scale_ref, own_ref, other_ref, s_ref):
-    chips, _, rows, _ = s_ref.shape
+def score_kernel(size, index_ref, table_ref, depth_ref, own_ref, other_ref, s_ref):
+    chips, _, rows, residues = s_ref.shape
+    depth = jnp.full((1, residues), depth_ref[0], jnp.int32).astype(jnp.float32)
+    scale = size**-0.5 / jnp.sqrt(depth) * LINK_SCALE
+    places = [
+        pl.ds(pl.multiple_of(ring_place(index_ref, table_ref, ahead) * rows, rows), rows)
+        for ahead in range(chips)
+    ]
     total = None
     for ref in (own_ref, other_ref):
-        q = jnp.concatenate(
-            [
-                ref[0, 0, pl.ds(pl.multiple_of(order_ref[chip] * rows, rows), rows), :]
-                for chip in range(chips)
-            ],
-            axis=0,
-        )
+        q = jnp.concatenate([ref[0, 0, place, :] for place in places], axis=0)
         part = lax.dot_general(
             q, ref[1, 0], (((1,), (1,)), ((), ())), preferred_element_type=jnp.float32
         )
         total = part if total is None else total + part
-    total = total * scale_ref[0]
+    total = total * scale
     s_ref[...] = total.reshape(chips, 1, rows, total.shape[1])
 
 
-def mix_kernel(p_ref, v_ref, o_ref):
+def mix_kernel(index_ref, table_ref, p_ref, v_ref, o_ref):
     seqs = o_ref.shape[0]
     size = v_ref.shape[2] // seqs
+    _, chips, _, rows, residues = p_ref.shape
     mixed = []
     for head in range(v_ref.shape[0]):
-        probs = p_ref[0, :, head]
-        probs = probs.reshape(probs.shape[0] * probs.shape[1], probs.shape[2])
+        probs = p_ref[0, :, head].reshape(chips * rows, residues)
         mixed.append(
             jnp.dot(probs, v_ref[head], preferred_element_type=jnp.float32).astype(jnp.bfloat16)
         )
+    places = [
+        pl.ds(pl.multiple_of(ring_place(index_ref, table_ref, ahead) * rows, rows), rows)
+        for ahead in range(chips)
+    ]
     for seq in range(seqs):
-        o_ref[seq] = jnp.concatenate(
+        joined = jnp.concatenate(
             [block[:, seq * size : (seq + 1) * size] for block in mixed], axis=1
         )
+        for ahead, place in enumerate(places):
+            o_ref[seq, place, :] = joined[ahead * rows : (ahead + 1) * rows]
 
 
 def cost(flops, moved):
     return pl.CostEstimate(flops=int(flops), bytes_accessed=int(moved), transcendentals=0)
 
 
-def projections(alignment, qkv_weight, half, use, head_count):
+def projections(alignment, qkv_weight, index, depth_count, head_count):
     seqs, residues, features = alignment.shape
     heads = head_count // 2
     size = features // head_count
@@ -133,8 +145,8 @@
 
     def weight_specs(pick):
         return [
-            pl.BlockSpec((features, cols), lambda i, half, use: (0, pick(half[0]))),
-            pl.BlockSpec((features, cols), lambda i, half, use: (0, 2 + pick(half[0]))),
+            pl.BlockSpec((features, cols), lambda i, index, _: (0, pick(lax.rem(index[0], 2)))),
+            pl.BlockSpec((features, cols), lambda i, index, _: (0, 2 + pick(lax.rem(index[0], 2)))),
         ]
 
     flops = 4 * seqs * residues * features * cols
@@ -151,7 +163,7 @@
         compiler_params=params,
         cost_estimate=cost(flops, moved + 2 * alignment.size),
         name="norm_send",
-    )(half, use, alignment, qkv_weight, qkv_weight)
+    )(index, depth_count, alignment, qkv_weight, qkv_weight)
     own = pl.pallas_call(
         own_kernel,
         out_shape=qk_shape,
@@ -164,7 +176,7 @@
         compiler_params=params,
         cost_estimate=cost(flops, moved),
         name="own_project",
-    )(half, use, normed, qkv_weight, qkv_weight)
+    )(index, depth_count, normed, qkv_weight, qkv_weight)
     values = pl.pallas_call(
         value_kernel,
         out_shape=jax.ShapeDtypeStruct((head_count, residues, seqs * size), bf16),
@@ -181,43 +193,57 @@
     return sent, own, values
 
 
-def scores_of(own, other, order, scale, chips):
+def scores_of(own, other, index, table, depth_count, size):
     _, heads, residues, inner = own.shape
+    chips = table.shape[0] // 2
     rows = residues // chips
     spec = pl.BlockSpec((2, 1, residues, inner), lambda h, *_: (0, h, 0, 0))
     return pl.pallas_call(
-        score_kernel,
+        functools.partial(score_kernel, size),
         out_shape=jax.ShapeDtypeStruct((chips, heads, rows, residues), jnp.float32),
         grid_spec=pltpu.PrefetchScalarGridSpec(
-            num_scalar_prefetch=1,
+            num_scalar_prefetch=3,
             grid=(heads,),
-            in_specs=[pl.BlockSpec(memory_space=pltpu.SMEM), spec, spec],
+            in_specs=[spec, spec],
             out_specs=pl.BlockSpec((chips, 1, rows, residues), lambda h, *_: (0, h, 0, 0)),
         ),
         compiler_params=pltpu.CompilerParams(vmem_limit_bytes=32 << 20),
         cost_estimate=cost(4 * heads * residues * residues * inner, 4 * own.size + 4 * heads * residues**2),
         name="scores",
-    )(order, scale, own, other)
-
-
-def row_mix_of(probs, values, seqs, head_count):
+    )(index, table, depth_count, own, other)
+
+
+def row_mix_of(probs, values, index, table, seqs, head_count):
     _, chips, heads, rows, residues = probs.shape
     inner = values.shape[2]
     size = inner // seqs
     pairs = heads // 2
+
+    def pair_at(g, index):
+        core = lax.rem(index[0] + lax.div(g, pairs), 2)
+        return core * pairs + lax.rem(g, pairs)
+
     return pl.pallas_call(
         mix_kernel,
         out_shape=jax.ShapeDtypeStruct((seqs, residues, head_count * size), jnp.bfloat16),
-        grid=(2 * pairs,),
-        in_specs=[
-            pl.BlockSpec((1, chips, 2, rows, residues), lambda g: (g // pairs, 0, g % pairs, 0, 0)),
-            pl.BlockSpec((2, residues, inner), lambda g: (g, 0, 0)),
-        ],
-        out_specs=pl.BlockSpec((seqs, residues, 2 * size), lambda g: (0, 0, g)),
+        grid_spec=pltpu.PrefetchScalarGridSpec(
+            num_scalar_prefetch=2,
+            grid=(2 * pairs,),
+            in_specs=[
+                pl.BlockSpec(
+                    (1, chips, 2, rows, residues),
+                    lambda g, *_: (lax.div(g, pairs), 0, lax.rem(g, pairs), 0, 0),
+                ),
+                pl.BlockSpec((2, residues, inner), lambda g, index, _: (pair_at(g, index), 0, 0)),
+            ],
+            out_specs=pl.BlockSpec(
+                (seqs, residues, 2 * size), lambda g, index, _: (0, 0, pair_at(g, index))
+            ),
+        ),
         compiler_params=pltpu.CompilerParams(vmem_limit_bytes=32 << 20),
         cost_estimate=cost(2 * probs.size * inner, 2 * (probs.size + 2 * values.size)),
         name="row_mix",
-    )(probs, values)
+    )(index, table, probs, values)
 
 
 class Links:
@@ -225,14 +251,9 @@
         self.devices = lax.axis_size("seq")
         self.chips = self.devices // 2
         self.ring = ring_of(self.chips)
-        self.index = lax.axis_index("seq")
-        self.core = self.index % 2
-        self.chip = self.index // 2
         places = [self.ring.index(chip) for chip in range(self.chips)]
-        self.place = jnp.asarray(places, jnp.int32)[self.chip]
-
-    def at(self, ahead):
-        return jnp.asarray(self.ring, jnp.int32)[(self.place + ahead) % self.chips]
+        self.table = jnp.asarray(places + self.ring, jnp.int32)
+        self.index = lax.axis_index("seq").astype(jnp.int32).reshape(1)
 
     def send(self, value, ahead):
         pairs = []
@@ -303,19 +324,15 @@
     for far in range(1, deep):
         ahead = links.send(ahead, 1)
         back = links.send(back, -1)
-        pieces += [(-far, 0, ahead), (far, 0, back)]
+        pieces += [(chips - far, 0, ahead), (far, 0, back)]
     pieces += [
-        (-deep, 0, links.send(ahead[:, :half], 1)),
+        (deep, 0, links.send(ahead[:, :half], 1)),
         (deep, half, links.send(back[:, half:], -1)),
     ]
     swapped = [links.swap(value) for _, _, value in pieces]
     for (far, row, value), other in zip(pieces, swapped):
-        chip = links.at(far)
-        where = (0, row, 0)
-        gathered = lax.dynamic_update_slice(gathered, value[None, None], (links.core, chip) + where)
-        gathered = lax.dynamic_update_slice(
-            gathered, other[None, None], (1 - links.core, chip) + where
-        )
+        for core, piece in enumerate((value, other)):
+            gathered = lax.dynamic_update_slice(gathered, piece[None, None], (core, far, 0, row, 0))
     return gathered
 
 
@@ -342,7 +359,7 @@
 
 
 def contact_kernel(
-    row_ref, pf_ref, pair_ref, near_ref, far_ref, head_ref, o_ref, u_ref, v_ref, hid_ref
+    index_ref, pf_ref, pair_ref, near_ref, far_ref, head_ref, o_ref, u_ref, v_ref, hid_ref
 ):
     blocks, _, residues = pf_ref.shape
     lanes = pair_ref.shape[1]
@@ -353,7 +370,7 @@
     lane_row = lax.broadcasted_iota(jnp.int32, (1, lanes), 1) // size
 
     def masked(m, values):
-        row = row_ref[0] + ROWS * (m - 2) + lane_row
+        row = index_ref[0] * o_ref.shape[0] + ROWS * (m - 2) + lane_row
         return jnp.where((row >= 0) & (row < residues), values, 0.0)
 
     def spread(ref, m, values, dilation):
@@ -445,27 +462,95 @@
     )(flipped)
 
 
+def window_kernel(index_ref, table_ref, p_ref, pf_ref, cols_ref, rows_ref):
+    cores, chips, heads, rows, residues = p_ref.shape
+    blocks, taken, _ = pf_ref.shape
+    band = ROWS * blocks
+    own_rows = band - 4 * ROWS
+    first = index_ref[0] * own_rows - 2 * ROWS
+    wide = cols_ref.shape[1] // (cores * heads)
+    tall = rows_ref.shape[0] // (cores * heads)
+    left = jnp.clip(lax.div(first, 128) * 128, 0, residues - wide)
+    top = jnp.clip(lax.div(first, rows) * rows, 0, residues - tall)
+    core = lax.rem(index_ref[0], 2)
+    place = table_ref[lax.div(index_ref[0], 2)]
+    lanes = pl.ds(pl.multiple_of(left, 128), wide)
+    for ahead in range(chips):
+        chip = ring_place(index_ref, table_ref, ahead)
+        there = pl.ds(pl.multiple_of(chip * rows, rows), rows)
+        for side in range(cores):
+            for head in range(heads):
+                slot = side * heads + head
+                cols_ref[there, slot * wide : (slot + 1) * wide] = p_ref[side, ahead, head, :, lanes]
+    for step in range(tall // rows):
+        ahead = lax.rem(table_ref[lax.div(top, rows) + step] - place + chips, chips)
+        for side in range(cores):
+            for head in range(heads):
+                start = (side * heads + head) * tall + step * rows
+                rows_ref[start : start + rows, :] = p_ref[side, ahead, head]
+
+    def picks(extent, base, out_rows, start):
+        count = cores * heads * extent
+        at = lax.broadcasted_iota(jnp.int32, (1, count), 1)
+        slot = lax.div(at, extent)
+        side = lax.div(slot, heads)
+        head = lax.rem(side + core, 2) * heads + slot - side * heads
+        have = head * 2048 + base + at - slot * extent
+        out = start + lax.broadcasted_iota(jnp.int32, (out_rows, 1), 0)
+        block = lax.div(out, taken)
+        rest = out - block * taken
+        head = lax.div(rest, ROWS)
+        row = first + ROWS * block + rest - head * ROWS
+        want = jnp.where((row >= 0) & (row < residues), head * 2048 + row, -1)
+        return jnp.where(want == have, 1.0, 0.0).astype(jnp.bfloat16)
+
+    step = 3 if blocks % 3 == 0 else 1
+    for block in range(0, blocks, step):
+        by_col = lax.dot_general(
+            picks(wide, left, step * taken, block * taken),
+            cols_ref[...],
+            (((1,), (1,)), ((), ())),
+            preferred_element_type=jnp.float32,
+        )
+        by_row = jnp.dot(
+            picks(tall, top, step * taken, block * taken),
+            rows_ref[...],
+            preferred_element_type=jnp.float32,
+        )
+        both = ((by_col + by_row) * (residues * 0.5)).astype(jnp.bfloat16)
+        pf_ref[block : block + step] = both.reshape(step, taken, residues)
+
+
 def contact_head(links, probs, pair_weight, taps, head_weight):
-    _, chips, heads, rows, residues = probs.shape
+    cores, chips, heads, rows, residues = probs.shape
     own_rows = residues // links.devices
+    blocks = own_rows // ROWS + 4
+    count = cores * heads
+    wide = min(256, residues)
+    tall = max(2 * rows, 64)
+    smem = pl.BlockSpec(memory_space=pltpu.SMEM)
+    vmem = pl.BlockSpec(memory_space=pltpu.VMEM)
+    pair_features = pl.pallas_call(
+        window_kernel,
+        out_shape=jax.ShapeDtypeStruct((blocks, ROWS * count, residues), jnp.bfloat16),
+        in_specs=[smem, smem, vmem],
+        out_specs=vmem,
+        scratch_shapes=[
+            pltpu.VMEM((residues, count * wide), jnp.bfloat16),
+            pltpu.VMEM((count * tall, residues), jnp.bfloat16),
+        ],
+        compiler_params=pltpu.CompilerParams(vmem_limit_bytes=40 << 20),
+        cost_estimate=cost(2 * blocks * ROWS * count**2 * residues * (wide + tall), 2 * probs.size),
+        name="pair_window",
+    )(links.index, links.table, probs)
+    return contact_call(links.index, pair_features, pair_weight, taps, head_weight, own_rows)
+
+
+def contact_call(index, pair_features, pair_weight, taps, head_weight, own_rows):
+    blocks, _, residues = pair_features.shape
     channels = pair_weight.shape[0]
-    first_row = links.index * own_rows
-    margin = 2 * ROWS
-    band_rows = own_rows + 2 * margin
-    blocks = band_rows // ROWS
-    by_row = probs.transpose(1, 3, 0, 2, 4).reshape(residues, 2 * heads, residues)
-    band_probs = lax.dynamic_slice_in_dim(
-        jnp.pad(by_row, ((margin, margin), (0, 0), (0, 0))), first_row, band_rows, 0
-    )
-    band_cols = lax.dynamic_slice_in_dim(
-        jnp.pad(probs, ((0, 0), (0, 0), (0, 0), (0, 0), (margin, margin))), first_row, band_rows, 4
-    )
-    band_cols = band_cols.transpose(4, 0, 2, 1, 3).reshape(band_rows, 2 * heads, residues)
-    pair_features = (
-        (band_probs.astype(jnp.float32) + band_cols.astype(jnp.float32)) * (residues * 0.5)
-    ).astype(jnp.bfloat16)
-    pair_features = pair_features.reshape(blocks, ROWS * 2 * heads, residues)
-    pair = jnp.kron(jnp.eye(ROWS, dtype=pair_weight.dtype), pair_weight.T)
+    same = jnp.eye(ROWS, dtype=pair_weight.dtype)
+    pair = (pair_weight.T[:, None, None, :] * same[None, :, :, None]).reshape(-1, ROWS * channels)
     head = jnp.tile(head_weight, ROWS)[None]
     lanes = ROWS * channels
     vmem = pl.BlockSpec(memory_space=pltpu.VMEM)
@@ -483,7 +568,7 @@
         compiler_params=pltpu.CompilerParams(vmem_limit_bytes=48 << 20),
         cost_estimate=cost(work // 4, 4 << 20),
         name="contact_head",
-    )(first_row.astype(jnp.int32).reshape(1), pair_features, pair, taps[0], taps[1], head)
+    )(index, pair_features, pair, taps[0], taps[1], head)
 
 
 def local(alignment, depth_count, qkv_weight, pair_weight, conv_weight, head_weight):
@@ -491,14 +576,9 @@
     head_count = pair_weight.shape[1]
     size = features // head_count
     links = Links()
-    depth = depth_count[0]
-    half = links.core.astype(jnp.int32).reshape(1)
-    use = jnp.clip(depth - links.index * seqs, 0, seqs).astype(jnp.int32).reshape(1)
-    sent, own, values = projections(alignment, qkv_weight, half, use, head_count)
+    sent, own, values = projections(alignment, qkv_weight, links.index, depth_count, head_count)
     other = links.swap(sent)
-    order = jnp.stack([links.at(ahead) for ahead in range(links.chips)])
-    scale = size**-0.5 / jnp.sqrt(depth.astype(jnp.float32)) * LINK_SCALE
-    scores = scores_of(own, other, order, scale.reshape(1), links.chips)
+    scores = scores_of(own, other, links.index, links.table, depth_count, size)
     rows = residues // links.chips
     room = jnp.zeros((2, links.chips, head_count // 2, rows, residues), jnp.bfloat16)
     summed, (room, taps, values) = reduce_scatter(
@@ -506,7 +586,7 @@
     )
     probabilities = jax.nn.softmax(summed * (1.0 / LINK_SCALE), axis=-1).astype(jnp.bfloat16)
     gathered = all_gather(links, probabilities, room)
-    row_mix = row_mix_of(gathered, values, seqs, head_count)
+    row_mix = row_mix_of(gathered, values, links.index, links.table, seqs, head_count)
     contacts = contact_head(links, gathered, pair_weight, taps, head_weight)
     return (row_mix, contacts)
 

time: 202 us -> 165 us (0.82)
  between operations: 28.3 us -> 1.73 us
  local copies, waits for them, and re-layouts: 30.7 us -> 7.04 us
  waiting for transfers between devices: 46 us -> 55.9 us
  Pallas kernels: 64.4 us -> 71.4 us
  other arithmetic: 6.43 us -> 3.62 us
    ppermute x22, waiting for transfers between devices: 44.8 us -> 54.6 us  [send(): return lax.ppermute(value, 'seq', pairs)]
    convert_element_type x3 -> x0, local copies, waits for them, and re-layouts: 6.22 us -> none  [the longest x2 5 us: contact_head(): band_cols.astype(jnp.float32)]
    pallas_call x2 -> x3, Pallas kernels: 36.8 us -> 42.9 us  [the longest x1 32.7 us: contact_call(): pl.pallas_call(contact_kernel, out_shape=jax.ShapeDtypeStruct((own_rows,...]
    unnamed x34 -> x24, local copies, waits for them, and re-layouts: 9.79 us -> 4.41 us
    another operation x3 -> x2, local copies, waits for them, and re-layouts: 5.07 us -> 0.08 us  [contact_call(): head = jnp.tile(head_weight, ROWS)[None]]
    transpose x1 -> x0, local copies, waits for them, and re-layouts: 3.63 us -> none  [contact_head(): probs.transpose(1, 3, 0, 2, 4).reshape(residues, 2 * heads, residues)]
  transfers between devices with their start and end apart: 32 -> 32, of which waited for: 16 -> 19; matrix products, arithmetic and copies ran while one was open for 5% -> 2% of each run, Pallas kernels for 7% -> 9%
where the time goes in v2:
time: 165 us
  Pallas kernels  71.4 us (43%)
  waiting for transfers between devices  55.9 us (34%)
  starting transfers between devices  24.9 us (15%)
  local copies, waits for them, and re-layouts  7.04 us (4%)
  other arithmetic  3.62 us (2%)
  between operations  1.73 us (1%)
    ppermute x22, waiting for transfers between devices, send(): return lax.ppermute(value, 'seq', pairs)  54.6 us
    pallas_call x1, Pallas kernels, contact_call(): pl.pallas_call(contact_kernel, out_shape=jax.ShapeDtypeStruct((own_rows,...  32.7 us
    ppermute x22, starting transfers between devices, send(): return lax.ppermute(value, 'seq', pairs)  23.5 us
    pallas_call x1, Pallas kernels, projections(): pl.pallas_call(norm_send_kernel, out_shape=(jax.ShapeDtypeStruct(alignmen...  8.16 us
    pallas_call x1, Pallas kernels, projections(): pl.pallas_call(own_kernel, out_shape=qk_shape, grid_spec=pltpu.PrefetchSc...  6.01 us
    pallas_call x1, Pallas kernels, contact_head(): pl.pallas_call(window_kernel, out_shape=jax.ShapeDtypeStruct((blocks, ROW...  5.99 us
    pallas_call x1, Pallas kernels, projections(): pl.pallas_call(value_kernel, out_shape=jax.ShapeDtypeStruct((head_count,...  5.69 us
    pallas_call x1, Pallas kernels, row_mix_of(): pl.pallas_call(mix_kernel, out_shape=jax.ShapeDtypeStruct((seqs, residues...  5.57 us
  transfers between devices with their start and end apart: 32, of which 19 were waited for; matrix products, arithmetic and copies ran while one was open for 2% of the time, Pallas kernels for 9%

profile of v2, /device:TPU:0, one launch (start us, length us, event | category | flops | bytes accessed | tf_op | source)
XLA Modules:
  0.0 164.5 jit_solution(1679101151221543541)
XLA Ops:
  1.3 8.2 %norm_send.1 = (bf16[4,512,768]{2,1,0:T(8,128)(2,1)S(1)}, bf16[2,6,512,256]{3,2,1,0:T(8,128)(2,1)}) custom-call(s32[1]{0:T(128)} %bitcast.index_ref, s32[1]{0:T(128)S(6)} %copy.28.depth_ref, bf16[4,512,768]{2,1,0:T(8,128)(2,1)} %x_ref.1, bf16[768,2304]{1,0:T(8,128)(2,1)} %w_ref.1, bf16[768,2304]{1,0:T(8,128)(2,1)} %w_ref.1), custom_call_target="tpu_custom_call" | custom-call | flops 2415919104 | bytes 10616832 | tf_op jit(solution)/shard_map/norm_send/pallas_call | solution.py:154
  9.4 1.7 %copy-done.3 = bf16[4,512,768]{2,1,0:T(8,128)(2,1)} copy-done((bf16[4,512,768]{2,1,0:T(8,128)(2,1)}, bf16[4,512,768]{2,1,0:T(8,128)(2,1)S(1)}, u32[]{:S(2)}) %copy-start.3) | copy-done | bytes 3145752
  11.1 0.5 collective-permute-start
  11.6 6.0 %own_project.1.own_ref = bf16[2,6,512,256]{3,2,1,0:T(8,128)(2,1)S(1)} custom-call(s32[1]{0:T(128)} %bitcast.index_ref, s32[1]{0:T(128)S(6)} %copy.28.depth_ref, bf16[4,512,768]{2,1,0:T(8,128)(2,1)} %copy-done.3, bf16[768,2304]{1,0:T(8,128)(2,1)} %w_ref.1, bf16[768,2304]{1,0:T(8,128)(2,1)} %w_ref.1), custom_call_target="tpu_custom_call" | custom-call | flops 2415919104 | bytes 7471104 | tf_op jit(solution)/shard_map/own_project/pallas_call | solution.py:167
  17.6 4.3 %scores.1 = f32[8,6,64,512]{3,2,1,0:T(8,128)S(1)} custom-call(s32[1]{0:T(128)} %bitcast.index_ref, s32[16]{0:T(128)S(1)} %copy-done.4, s32[1]{0:T(128)S(6)} %copy.28.depth_ref, bf16[2,6,512,256]{3,2,1,0:T(8,128)(2,1)S(1)} %own_project.1.own_ref, bf16[2,6,512,256]{3,2,1,0:T(8,128)(2,1)S(1)} %collective-permute-done.other_ref), custom_call_target="tpu_custom_call" | custom-call | flops 1610612736 | bytes 12582912 | tf_op jit(solution)/shard_map/scores/pallas_call | solution.py:201
  21.9 2.7 %copy-done = f32[8,6,64,512]{3,2,1,0:T(8,128)} copy-done((f32[8,6,64,512]{3,2,1,0:T(8,128)}, f32[8,6,64,512]{3,2,1,0:T(8,128)S(1)}, u32[]{:S(2)}) %copy-start) | copy-done | bytes 6291480
  24.6 0.7 convert.6
  25.3 0.2 slice_bitcast_fusion.12
  25.5 2.6 %collective-permute-start.1 = (f16[6,32,512]{2,1,0:T(8,128)(2,1)S(1)}, f16[6,32,512]{2,1,0:T(8,128)(2,1)S(1)}, u32[]{:S(2)}, u32[]{:S(2)}) collective-permute-start(f16[6,32,512]{2,1,0:T(8,128)(2,1)S(1)} %get-tuple-element.63), channel_id=1, source_target_pairs={{0,2},{1,3},{2,6},{3,7},{6,10},{7,11},{10,14},{11,15},{14,12},{15,... | collective-permute-start | bytes 589832 | tf_op jit(solution)/shard_map/ppermute | solution.py:263
  28.2 1.0 copy.9
  29.2 3.0 %spread_taps.1 = (bf16[2,3,384,256]{3,2,1,0:T(8,128)(2,1)}, bf16[2,3,512,256]{3,2,1,0:T(8,128)(2,1)}) custom-call(bf16[36,64,64]{2,1,0:T(8,128)(2,1)} %bitcast.124), custom_call_target="tpu_custom_call" | custom-call | bytes 6291456 | tf_op jit(solution)/shard_map/spread_taps/pallas_call | solution.py:454
  32.3 1.4 collective-permute-done.1
  33.7 1.4 collective-permute-done.2
  35.1 1.3 fusion.26
  36.4 1.6 collective-permute-start.3
  38.0 0.5 collective-permute-start.4
  38.4 5.7 %value_project.1.v_ref = bf16[12,512,256]{2,1,0:T(8,128)(2,1)S(1)} custom-call(bf16[4,512,768]{2,1,0:T(8,128)(2,1)} %copy-done.3, bf16[768,2304]{1,0:T(8,128)(2,1)} %w_ref.1), custom_call_target="tpu_custom_call" | custom-call | flops 2415919104 | bytes 7471104 | tf_op jit(solution)/shard_map/value_project/pallas_call | solution.py:180
  44.2 1.6 collective-permute-start.7
  45.8 0.5 collective-permute-start.8
  46.3 0.1 fusion.22
  46.4 1.6 collective-permute-start.5
  48.0 0.5 collective-permute-start.6
  48.5 3.4 %collective-permute-done.7 = f16[6,32,512]{2,1,0:T(8,128)(2,1)S(1)} collective-permute-done((f16[6,32,512]{2,1,0:T(8,128)(2,1)S(1)}, f16[6,32,512]{2,1,0:T(8,128)(2,1)S(1)}, u32[]{:S(2)}, u32[]{:S(2)}) %collective-permute-start.7) | collective-permute-done | bytes 196640 | tf_op jit(solution)/shard_map/ppermute | solution.py:263
  51.9 1.3 collective-permute-done.8
  53.2 0.1 fusion.18
  53.3 1.6 collective-permute-start.10
  54.9 0.4 collective-permute-start.11
  55.4 0.7 collective-permute-done.5
  56.1 1.3 collective-permute-done.6
  57.5 1.6 collective-permute-done.10
  59.0 1.9 %collective-permute-done.11 = f16[6,32,512]{2,1,0:T(8,128)(2,1)S(1)} collective-permute-done((f16[6,32,512]{2,1,0:T(8,128)(2,1)S(1)}, f16[6,32,512]{2,1,0:T(8,128)(2,1)S(1)}, u32[]{:S(2)}, u32[]{:S(2)}) %collective-permute-start.11) | collective-permute-done | bytes 196640 | tf_op jit(solution)/shard_map/ppermute | solution.py:263
  61.0 0.5 collective-permute-start.12
  61.5 1.7 %collective-permute-start.9 = (f16[6,32,512]{2,1,0:T(8,128)(2,1)S(1)}, f16[6,32,512]{2,1,0:T(8,128)(2,1)S(1)}, u32[]{:S(2)}, u32[]{:S(2)}) collective-permute-start(f16[6,32,512]{2,1,0:T(8,128)(2,1)S(1)} %get-tuple-element.52), channel_id=1, source_target_pairs={{0,2},{1,3},{2,6},{3,7},{6,10},{7,11},{10,14},{11,15},{14,12},{15,... | collective-permute-start | bytes 589832 | tf_op jit(solution)/shard_map/ppermute | solution.py:263
  63.2 0.3 collective-permute-start.14
  63.5 3.4 %collective-permute-done.12 = f16[6,32,512]{2,1,0:T(8,128)(2,1)S(1)} collective-permute-done((f16[6,32,512]{2,1,0:T(8,128)(2,1)S(1)}, f16[6,32,512]{2,1,0:T(8,128)(2,1)S(1)}, u32[]{:S(2)}, u32[]{:S(2)}) %collective-permute-start.12) | collective-permute-done | bytes 196640 | tf_op jit(solution)/shard_map/ppermute | solution.py:263
  66.9 2.0 %collective-permute-done.9 = f16[6,32,512]{2,1,0:T(8,128)(2,1)S(1)} collective-permute-done((f16[6,32,512]{2,1,0:T(8,128)(2,1)S(1)}, f16[6,32,512]{2,1,0:T(8,128)(2,1)S(1)}, u32[]{:S(2)}, u32[]{:S(2)}) %collective-permute-start.9) | collective-permute-done | bytes 196640 | tf_op jit(solution)/shard_map/ppermute | solution.py:263
  68.9 0.2 fusion.30
  69.1 1.7 %collective-permute-start.13 = (f16[6,32,512]{2,1,0:T(8,128)(2,1)S(1)}, f16[6,32,512]{2,1,0:T(8,128)(2,1)S(1)}, u32[]{:S(2)}, u32[]{:S(2)}) collective-permute-start(f16[6,32,512]{2,1,0:T(8,128)(2,1)S(1)} %get-tuple-element.51), channel_id=1, source_target_pairs={{0,2},{1,3},{2,6},{3,7},{6,10},{7,11},{10,14},{11,15},{14,12},{15,... | collective-permute-start | bytes 589832 | tf_op jit(solution)/shard_map/ppermute | solution.py:263
  70.8 4.0 %collective-permute-done.13 = f16[6,32,512]{2,1,0:T(8,128)(2,1)S(1)} collective-permute-done((f16[6,32,512]{2,1,0:T(8,128)(2,1)S(1)}, f16[6,32,512]{2,1,0:T(8,128)(2,1)S(1)}, u32[]{:S(2)}, u32[]{:S(2)}) %collective-permute-start.13) | collective-permute-done | bytes 196640 | tf_op jit(solution)/shard_map/ppermute | solution.py:263
  74.9 0.1 fusion.5
  75.1 0.3 fusion.4
  75.4 0.2 divide_convert_fusion
  75.7 1.7 %collective-permute-start.16 = (bf16[6,64,512]{2,1,0:T(8,128)(2,1)S(1)}, bf16[6,64,512]{2,1,0:T(8,128)(2,1)S(1)}, u32[]{:S(2)}, u32[]{:S(2)}) collective-permute-start(bf16[6,64,512]{2,1,0:T(8,128)(2,1)S(1)} %divide_convert_fusion), channel_id=1, source_target_pairs={{0,2},{1,3},{2,6},{3,7},{6,10},{7,11},{10,14},{11,15},{14,12},{15,... | collective-permute-start | bytes 1179656 | tf_op jit(solution)/shard_map/ppermute | solution.py:263
  77.4 0.4 collective-permute-start.18
  78.0 0.8 broadcast_in_dim.59
  78.8 0.2 fusion.6
  79.1 8.1 %collective-permute-done.16 = bf16[6,64,512]{2,1,0:T(8,128)(2,1)S(1)} collective-permute-done((bf16[6,64,512]{2,1,0:T(8,128)(2,1)S(1)}, bf16[6,64,512]{2,1,0:T(8,128)(2,1)S(1)}, u32[]{:S(2)}, u32[]{:S(2)}) %collective-permute-start.16) | collective-permute-done | bytes 393248 | tf_op jit(solution)/shard_map/ppermute | solution.py:263
  87.2 1.6 collective-permute-start.20
  88.8 0.2 collective-permute-start.19
  89.1 0.4 collective-permute-start.22
  89.5 9.2 %collective-permute-done.20 = bf16[6,64,512]{2,1,0:T(8,128)(2,1)S(1)} collective-permute-done((bf16[6,64,512]{2,1,0:T(8,128)(2,1)S(1)}, bf16[6,64,512]{2,1,0:T(8,128)(2,1)S(1)}, u32[]{:S(2)}, u32[]{:S(2)}) %collective-permute-start.20) | collective-permute-done | bytes 393248 | tf_op jit(solution)/shard_map/ppermute | solution.py:263
  98.7 1.6 collective-permute-start.24
  100.4 0.2 collective-permute-done.22
  100.6 0.4 collective-permute-start.26
  101.1 9.1 %collective-permute-done.24 = bf16[6,64,512]{2,1,0:T(8,128)(2,1)S(1)} collective-permute-done((bf16[6,64,512]{2,1,0:T(8,128)(2,1)S(1)}, bf16[6,64,512]{2,1,0:T(8,128)(2,1)S(1)}, u32[]{:S(2)}, u32[]{:S(2)}) %collective-permute-start.24) | collective-permute-done | bytes 393248 | tf_op jit(solution)/shard_map/ppermute | solution.py:263
  110.3 1.7 %collective-permute-start.28 = (bf16[6,32,512]{2,1,0:T(8,128)(2,1)S(1)}, bf16[6,32,512]{2,1,0:T(8,128)(2,1)S(1)}, u32[]{:S(2)}, u32[]{:S(2)}) collective-permute-start(bf16[6,32,512]{2,1,0:T(8,128)(2,1)S(1)} %slice.92), channel_id=1, source_target_pairs={{0,2},{1,3},{2,6},{3,7},{6,10},{7,11},{10,14},{11,15},{14,12},{15,... | collective-permute-start | bytes 589832 | tf_op jit(solution)/shard_map/ppermute | solution.py:263
  112.1 0.5 collective-permute-start.30
  112.6 0.5 collective-permute-start.27
  113.3 3.6 %collective-permute-done.28 = bf16[6,32,512]{2,1,0:T(8,128)(2,1)S(1)} collective-permute-done((bf16[6,32,512]{2,1,0:T(8,128)(2,1)S(1)}, bf16[6,32,512]{2,1,0:T(8,128)(2,1)S(1)}, u32[]{:S(2)}, u32[]{:S(2)}) %collective-permute-start.28) | collective-permute-done | bytes 196640 | tf_op jit(solution)/shard_map/ppermute | solution.py:263
  116.8 1.9 %collective-permute-done.30 = bf16[6,32,512]{2,1,0:T(8,128)(2,1)S(1)} collective-permute-done((bf16[6,32,512]{2,1,0:T(8,128)(2,1)S(1)}, bf16[6,32,512]{2,1,0:T(8,128)(2,1)S(1)}, u32[]{:S(2)}, u32[]{:S(2)}) %collective-permute-start.30) | collective-permute-done | bytes 196640 | tf_op jit(solution)/shard_map/ppermute | solution.py:263
  119.0 1.2 collective-permute-done.31
  120.2 6.0 %pair_window.1.pf_ref = bf16[12,48,512]{2,1,0:T(8,128)(2,1)S(1)} custom-call(s32[1]{0:T(128)} %bitcast.index_ref, s32[16]{0:T(128)S(1)} %copy-done.4, bf16[2,8,6,64,512]{4,3,2,1,0:T(8,128)(2,1)S(1)} %bitcast_dynamic-update-slice_fusion.13.p_ref), custom_call_target="tpu_custom_call" | custom-call | flops 2717908992 | bytes 6291456 | tf_op jit(solution)/shard_map/pair_window/pallas_call | solution.py:533
  126.3 5.6 %row_mix.1 = bf16[4,512,768]{2,1,0:T(8,128)(2,1)} custom-call(s32[1]{0:T(128)} %bitcast.index_ref, s32[16]{0:T(128)S(1)} %copy-done.4, bf16[2,8,6,64,512]{4,3,2,1,0:T(8,128)(2,1)S(1)} %bitcast_dynamic-update-slice_fusion.13.p_ref, bf16[12,512,256]{2,1,0:T(8,128)(2,1)S(1)} %copy-done.2), custom_call_target="tpu_custom_call" | custom-call | flops 1610612736 | bytes 12582912 | tf_op jit(solution)/shard_map/row_mix/pallas_call | solution.py:226
  131.8 32.7 %contact_head.1 = f32[32,512]{1,0:T(8,128)} custom-call(s32[1]{0:T(128)} %bitcast.index_ref, bf16[12,48,512]{2,1,0:T(8,128)(2,1)S(1)} %pair_window.1.pf_ref, bf16[48,256]{1,0:T(8,128)(2,1)S(1)} %mul.41.pair_ref, bf16[2,3,384,256]{3,2,1,0:T(8,128)(2,1)S(1)} %copy-done.6, bf16[2,3,512,256]{3,2,1,0:T(8,128)(2,1)S(1)} %copy-done.5, ...), custom_call_target="tpu_custom_call" | custom-call | flops 5469372416 | bytes 4194304 | tf_op jit(solution)/shard_map/contact_head/pallas_call | solution.py:558
  (72 shorter events, 1.5 us)
Async XLA Ops:
  9.4 1.7 %copy-start.3 = (bf16[4,512,768]{2,1,0:T(8,128)(2,1)}, bf16[4,512,768]{2,1,0:T(8,128)(2,1)S(1)}, u32[]{:S(2)}) copy-start(bf16[4,512,768]{2,1,0:T(8,128)(2,1)S(1)} %get-tuple-element.26.normed_ref) | copy-start | bytes 9437188
  11.1 6.5 %collective-permute-start = (bf16[2,6,512,256]{3,2,1,0:T(8,128)(2,1)}, bf16[2,6,512,256]{3,2,1,0:T(8,128)(2,1)S(1)}, u32[]{:S(2)}, u32[]{:S(2)}) collective-permute-start(bf16[2,6,512,256]{3,2,1,0:T(8,128)(2,1)} %get-tuple-element.27), channel_id=1, source_target_pairs={{0,1},{1,0},{2,3},{3,2},{4,5},{5,4},{6,7},{7,6},{8,9},{9,8},{10,11... | collective-permute-start | bytes 9437192 | tf_op jit(solution)/shard_map/ppermute | solution.py:266
  11.6 6.0 %copy-start.4 = (s32[16]{0:T(128)S(1)}, s32[16]{0:T(128)}, u32[]{:S(2)}) copy-start(s32[16]{0:T(128)} %constant.14.clone.table_ref) | copy-start | bytes 196
  21.9 2.7 %copy-start = (f32[8,6,64,512]{3,2,1,0:T(8,128)}, f32[8,6,64,512]{3,2,1,0:T(8,128)S(1)}, u32[]{:S(2)}) copy-start(f32[8,6,64,512]{3,2,1,0:T(8,128)S(1)} %scores.1) | copy-start | bytes 18874372
  24.6 3.6 %copy-start.7 = (bf16[4,9,64,64]{3,2,1,0:T(8,128)(2,1)S(1)}, bf16[4,9,64,64]{3,2,1,0:T(8,128)(2,1)}, u32[]{:S(2)}) copy-start(bf16[4,9,64,64]{3,2,1,0:T(8,128)(2,1)} %param.11) | copy-start | bytes 884740
  25.5 8.2 %collective-permute-start.1 = (f16[6,32,512]{2,1,0:T(8,128)(2,1)S(1)}, f16[6,32,512]{2,1,0:T(8,128)(2,1)S(1)}, u32[]{:S(2)}, u32[]{:S(2)}) collective-permute-start(f16[6,32,512]{2,1,0:T(8,128)(2,1)S(1)} %get-tuple-element.63), channel_id=1, source_target_pairs={{0,2},{1,3},{2,6},{3,7},{6,10},{7,11},{10,14},{11,15},{14,12},{15,... | collective-permute-start | bytes 589832 | tf_op jit(solution)/shard_map/ppermute | solution.py:263
  28.1 7.0 %collective-permute-start.2 = (f16[6,32,512]{2,1,0:T(8,128)(2,1)S(1)}, f16[6,32,512]{2,1,0:T(8,128)(2,1)S(1)}, u32[]{:S(2)}, u32[]{:S(2)}) collective-permute-start(f16[6,32,512]{2,1,0:T(8,128)(2,1)S(1)} %get-tuple-element.62), channel_id=1, source_target_pairs={{0,4},{1,5},{2,0},{3,1},{6,2},{7,3},{10,6},{11,7},{14,10},{15,11},... | collective-permute-start | bytes 589832 | tf_op jit(solution)/shard_map/ppermute | solution.py:263
  29.2 17.0 %slice-start = ((s8[6291456]{0:T(1024)(128)(4,1)}), s8[2097152]{0:T(1024)(128)(4,1)S(1)}, s32[]{:S(2)}) async-start(s8[6291456]{0:T(1024)(128)(4,1)} %bitcast.120), calls=%async_computation | async-start | bytes 4194304
  36.4 9.9 %collective-permute-start.3 = (f16[6,32,512]{2,1,0:T(8,128)(2,1)S(1)}, f16[6,32,512]{2,1,0:T(8,128)(2,1)S(1)}, u32[]{:S(2)}, u32[]{:S(2)}) collective-permute-start(f16[6,32,512]{2,1,0:T(8,128)(2,1)S(1)} %get-tuple-element.59), channel_id=1, source_target_pairs={{0,2},{1,3},{2,6},{3,7},{6,10},{7,11},{10,14},{11,15},{14,12},{15,... | collective-permute-start | bytes 589832 | tf_op jit(solution)/shard_map/ppermute | solution.py:263
  38.0 8.3 %slice-start.1 = ((s8[6291456]{0:T(1024)(128)(4,1)}), s8[4194304]{0:T(1024)(128)(4,1)S(1)}, s32[]{:S(2)}) async-start(s8[6291456]{0:T(1024)(128)(4,1)} %bitcast.120), calls=%async_computation.1 | async-start | bytes 8388608
  38.0 8.3 %collective-permute-start.4 = (f16[6,32,512]{2,1,0:T(8,128)(2,1)S(1)}, f16[6,32,512]{2,1,0:T(8,128)(2,1)S(1)}, u32[]{:S(2)}, u32[]{:S(2)}) collective-permute-start(f16[6,32,512]{2,1,0:T(8,128)(2,1)S(1)} %get-tuple-element.58), channel_id=1, source_target_pairs={{0,4},{1,5},{2,0},{3,1},{6,2},{7,3},{10,6},{11,7},{14,10},{15,11},... | collective-permute-start | bytes 589832 | tf_op jit(solution)/shard_map/ppermute | solution.py:263
  44.1 30.8 %copy-start.1 = (bf16[12,512,256]{2,1,0:T(8,128)(2,1)}, bf16[12,512,256]{2,1,0:T(8,128)(2,1)S(1)}, u32[]{:S(2)}) copy-start(bf16[12,512,256]{2,1,0:T(8,128)(2,1)S(1)} %value_project.1.v_ref) | copy-start | bytes 9437188
  44.1 33.6 %copy-start.8 = (bf16[64,12]{0,1:T(8,128)(2,1)S(1)}, bf16[64,12]{0,1:T(8,128)(2,1)}, u32[]{:S(2)}) copy-start(bf16[64,12]{0,1:T(8,128)(2,1)} %param.10) | copy-start | bytes 4612
  44.2 33.8 %copy-start.9 = (f32[64]{0:T(128)S(1)}, f32[64]{0:T(128)}, u32[]{:S(2)}) copy-start(f32[64]{0:T(128)} %param.12) | copy-start | bytes 772
  44.2 7.7 %collective-permute-start.7 = (f16[6,32,512]{2,1,0:T(8,128)(2,1)S(1)}, f16[6,32,512]{2,1,0:T(8,128)(2,1)S(1)}, u32[]{:S(2)}, u32[]{:S(2)}) collective-permute-start(f16[6,32,512]{2,1,0:T(8,128)(2,1)S(1)} %get-tuple-element.61), channel_id=1, source_target_pairs={{0,2},{1,3},{2,6},{3,7},{6,10},{7,11},{10,14},{11,15},{14,12},{15,... | collective-permute-start | bytes 589832 | tf_op jit(solution)/shard_map/ppermute | solution.py:263
  45.8 7.4 %collective-permute-start.8 = (f16[6,32,512]{2,1,0:T(8,128)(2,1)S(1)}, f16[6,32,512]{2,1,0:T(8,128)(2,1)S(1)}, u32[]{:S(2)}, u32[]{:S(2)}) collective-permute-start(f16[6,32,512]{2,1,0:T(8,128)(2,1)S(1)} %get-tuple-element.60), channel_id=1, source_target_pairs={{0,4},{1,5},{2,0},{3,1},{6,2},{7,3},{10,6},{11,7},{14,10},{15,11},... | collective-permute-start | bytes 589832 | tf_op jit(solution)/shard_map/ppermute | solution.py:263
  46.4 9.7 %collective-permute-start.5 = (f16[6,32,512]{2,1,0:T(8,128)(2,1)S(1)}, f16[6,32,512]{2,1,0:T(8,128)(2,1)S(1)}, u32[]{:S(2)}, u32[]{:S(2)}) collective-permute-start(f16[6,32,512]{2,1,0:T(8,128)(2,1)S(1)} %get-tuple-element.57), channel_id=1, source_target_pairs={{0,2},{1,3},{2,6},{3,7},{6,10},{7,11},{10,14},{11,15},{14,12},{15,... | collective-permute-start | bytes 589832 | tf_op jit(solution)/shard_map/ppermute | solution.py:263
  48.0 9.3 %collective-permute-start.6 = (f16[6,32,512]{2,1,0:T(8,128)(2,1)S(1)}, f16[6,32,512]{2,1,0:T(8,128)(2,1)S(1)}, u32[]{:S(2)}, u32[]{:S(2)}) collective-permute-start(f16[6,32,512]{2,1,0:T(8,128)(2,1)S(1)} %get-tuple-element.56), channel_id=1, source_target_pairs={{0,4},{1,5},{2,0},{3,1},{6,2},{7,3},{10,6},{11,7},{14,10},{15,11},... | collective-permute-start | bytes 589832 | tf_op jit(solution)/shard_map/ppermute | solution.py:263
  53.3 5.7 %collective-permute-start.10 = (f16[6,32,512]{2,1,0:T(8,128)(2,1)S(1)}, f16[6,32,512]{2,1,0:T(8,128)(2,1)S(1)}, u32[]{:S(2)}, u32[]{:S(2)}) collective-permute-start(f16[6,32,512]{2,1,0:T(8,128)(2,1)S(1)} %get-tuple-element.55), channel_id=1, source_target_pairs={{0,2},{1,3},{2,6},{3,7},{6,10},{7,11},{10,14},{11,15},{14,12},{15,... | collective-permute-start | bytes 589832 | tf_op jit(solution)/shard_map/ppermute | solution.py:263
  54.9 6.0 %collective-permute-start.11 = (f16[6,32,512]{2,1,0:T(8,128)(2,1)S(1)}, f16[6,32,512]{2,1,0:T(8,128)(2,1)S(1)}, u32[]{:S(2)}, u32[]{:S(2)}) collective-permute-start(f16[6,32,512]{2,1,0:T(8,128)(2,1)S(1)} %get-tuple-element.54), channel_id=1, source_target_pairs={{0,4},{1,5},{2,0},{3,1},{6,2},{7,3},{10,6},{11,7},{14,10},{15,11},... | collective-permute-start | bytes 589832 | tf_op jit(solution)/shard_map/ppermute | solution.py:263
  61.0 5.9 %collective-permute-start.12 = (f16[6,32,512]{2,1,0:T(8,128)(2,1)S(1)}, f16[6,32,512]{2,1,0:T(8,128)(2,1)S(1)}, u32[]{:S(2)}, u32[]{:S(2)}) collective-permute-start(f16[6,32,512]{2,1,0:T(8,128)(2,1)S(1)} %fusion.12), channel_id=1, source_target_pairs={{0,4},{1,5},{2,0},{3,1},{6,2},{7,3},{10,6},{11,7},{14,10},{15,11},... | collective-permute-start | bytes 589832 | tf_op jit(solution)/shard_map/ppermute | solution.py:263
  61.5 7.5 %collective-permute-start.9 = (f16[6,32,512]{2,1,0:T(8,128)(2,1)S(1)}, f16[6,32,512]{2,1,0:T(8,128)(2,1)S(1)}, u32[]{:S(2)}, u32[]{:S(2)}) collective-permute-start(f16[6,32,512]{2,1,0:T(8,128)(2,1)S(1)} %get-tuple-element.52), channel_id=1, source_target_pairs={{0,2},{1,3},{2,6},{3,7},{6,10},{7,11},{10,14},{11,15},{14,12},{15,... | collective-permute-start | bytes 589832 | tf_op jit(solution)/shard_map/ppermute | solution.py:263
  63.2 7.6 %collective-permute-start.14 = (f16[6,32,512]{2,1,0:T(8,128)(2,1)S(1)}, f16[6,32,512]{2,1,0:T(8,128)(2,1)S(1)}, u32[]{:S(2)}, u32[]{:S(2)}) collective-permute-start(f16[6,32,512]{2,1,0:T(8,128)(2,1)S(1)} %get-tuple-element.53), channel_id=1, source_target_pairs={{0,4},{1,5},{2,0},{3,1},{6,2},{7,3},{10,6},{11,7},{14,10},{15,11},... | collective-permute-start | bytes 589832 | tf_op jit(solution)/shard_map/ppermute | solution.py:263
  69.1 5.7 %collective-permute-start.13 = (f16[6,32,512]{2,1,0:T(8,128)(2,1)S(1)}, f16[6,32,512]{2,1,0:T(8,128)(2,1)S(1)}, u32[]{:S(2)}, u32[]{:S(2)}) collective-permute-start(f16[6,32,512]{2,1,0:T(8,128)(2,1)S(1)} %get-tuple-element.51), channel_id=1, source_target_pairs={{0,2},{1,3},{2,6},{3,7},{6,10},{7,11},{10,14},{11,15},{14,12},{15,... | collective-permute-start | bytes 589832 | tf_op jit(solution)/shard_map/ppermute | solution.py:263
  75.6 13.9 %collective-permute-start.15 = (bf16[6,64,512]{2,1,0:T(8,128)(2,1)S(1)}, bf16[6,64,512]{2,1,0:T(8,128)(2,1)S(1)}, u32[]{:S(2)}, u32[]{:S(2)}) collective-permute-start(bf16[6,64,512]{2,1,0:T(8,128)(2,1)S(1)} %divide_convert_fusion), channel_id=1, source_target_pairs={{0,1},{1,0},{2,3},{3,2},{4,5},{5,4},{6,7},{7,6},{8,9},{9,8},{10,11... | collective-permute-start | bytes 1179656 | tf_op jit(solution)/shard_map/ppermute | solution.py:266
  75.7 11.5 %collective-permute-start.16 = (bf16[6,64,512]{2,1,0:T(8,128)(2,1)S(1)}, bf16[6,64,512]{2,1,0:T(8,128)(2,1)S(1)}, u32[]{:S(2)}, u32[]{:S(2)}) collective-permute-start(bf16[6,64,512]{2,1,0:T(8,128)(2,1)S(1)} %divide_convert_fusion), channel_id=1, source_target_pairs={{0,2},{1,3},{2,6},{3,7},{6,10},{7,11},{10,14},{11,15},{14,12},{15,... | collective-permute-start | bytes 1179656 | tf_op jit(solution)/shard_map/ppermute | solution.py:263
  77.4 11.5 %collective-permute-start.18 = (bf16[6,64,512]{2,1,0:T(8,128)(2,1)S(1)}, bf16[6,64,512]{2,1,0:T(8,128)(2,1)S(1)}, u32[]{:S(2)}, u32[]{:S(2)}) collective-permute-start(bf16[6,64,512]{2,1,0:T(8,128)(2,1)S(1)} %divide_convert_fusion), channel_id=1, source_target_pairs={{0,4},{1,5},{2,0},{3,1},{6,2},{7,3},{10,6},{11,7},{14,10},{15,11},... | collective-permute-start | bytes 1179656 | tf_op jit(solution)/shard_map/ppermute | solution.py:263
  87.2 13.4 %collective-permute-start.17 = (bf16[6,64,512]{2,1,0:T(8,128)(2,1)S(1)}, bf16[6,64,512]{2,1,0:T(8,128)(2,1)S(1)}, u32[]{:S(2)}, u32[]{:S(2)}) collective-permute-start(bf16[6,64,512]{2,1,0:T(8,128)(2,1)S(1)} %collective-permute-done.16), channel_id=1, source_target_pairs={{0,1},{1,0},{2,3},{3,2},{4,5},{5,4},{6,7},{7,6},{8,9},{9,8},{10,11... | collective-permute-start | bytes 1179656 | tf_op jit(solution)/shard_map/ppermute | solution.py:266
  87.2 11.5 %collective-permute-start.20 = (bf16[6,64,512]{2,1,0:T(8,128)(2,1)S(1)}, bf16[6,64,512]{2,1,0:T(8,128)(2,1)S(1)}, u32[]{:S(2)}, u32[]{:S(2)}) collective-permute-start(bf16[6,64,512]{2,1,0:T(8,128)(2,1)S(1)} %collective-permute-done.16), channel_id=1, source_target_pairs={{0,2},{1,3},{2,6},{3,7},{6,10},{7,11},{10,14},{11,15},{14,12},{15,... | collective-permute-start | bytes 1179656 | tf_op jit(solution)/shard_map/ppermute | solution.py:263
  88.8 12.2 %collective-permute-start.19 = (bf16[6,64,512]{2,1,0:T(8,128)(2,1)S(1)}, bf16[6,64,512]{2,1,0:T(8,128)(2,1)S(1)}, u32[]{:S(2)}, u32[]{:S(2)}) collective-permute-start(bf16[6,64,512]{2,1,0:T(8,128)(2,1)S(1)} %collective-permute-done.18), channel_id=1, source_target_pairs={{0,1},{1,0},{2,3},{3,2},{4,5},{5,4},{6,7},{7,6},{8,9},{9,8},{10,11... | collective-permute-start | bytes 1179656 | tf_op jit(solution)/shard_map/ppermute | solution.py:266
  89.1 11.5 %collective-permute-start.22 = (bf16[6,64,512]{2,1,0:T(8,128)(2,1)S(1)}, bf16[6,64,512]{2,1,0:T(8,128)(2,1)S(1)}, u32[]{:S(2)}, u32[]{:S(2)}) collective-permute-start(bf16[6,64,512]{2,1,0:T(8,128)(2,1)S(1)} %collective-permute-done.18), channel_id=1, source_target_pairs={{0,4},{1,5},{2,0},{3,1},{6,2},{7,3},{10,6},{11,7},{14,10},{15,11},... | collective-permute-start | bytes 1179656 | tf_op jit(solution)/shard_map/ppermute | solution.py:263
  98.7 13.9 %collective-permute-start.21 = (bf16[6,64,512]{2,1,0:T(8,128)(2,1)S(1)}, bf16[6,64,512]{2,1,0:T(8,128)(2,1)S(1)}, u32[]{:S(2)}, u32[]{:S(2)}) collective-permute-start(bf16[6,64,512]{2,1,0:T(8,128)(2,1)S(1)} %collective-permute-done.20), channel_id=1, source_target_pairs={{0,1},{1,0},{2,3},{3,2},{4,5},{5,4},{6,7},{7,6},{8,9},{9,8},{10,11... | collective-permute-start | bytes 1179656 | tf_op jit(solution)/shard_map/ppermute | solution.py:266
  98.7 11.5 %collective-permute-start.24 = (bf16[6,64,512]{2,1,0:T(8,128)(2,1)S(1)}, bf16[6,64,512]{2,1,0:T(8,128)(2,1)S(1)}, u32[]{:S(2)}, u32[]{:S(2)}) collective-permute-start(bf16[6,64,512]{2,1,0:T(8,128)(2,1)S(1)} %collective-permute-done.20), channel_id=1, source_target_pairs={{0,2},{1,3},{2,6},{3,7},{6,10},{7,11},{10,14},{11,15},{14,12},{15,... | collective-permute-start | bytes 1179656 | tf_op jit(solution)/shard_map/ppermute | solution.py:263
  100.5 12.7 %collective-permute-start.23 = (bf16[6,64,512]{2,1,0:T(8,128)(2,1)S(1)}, bf16[6,64,512]{2,1,0:T(8,128)(2,1)S(1)}, u32[]{:S(2)}, u32[]{:S(2)}) collective-permute-start(bf16[6,64,512]{2,1,0:T(8,128)(2,1)S(1)} %collective-permute-done.22), channel_id=1, source_target_pairs={{0,1},{1,0},{2,3},{3,2},{4,5},{5,4},{6,7},{7,6},{8,9},{9,8},{10,11... | collective-permute-start | bytes 1179656 | tf_op jit(solution)/shard_map/ppermute | solution.py:266
  100.6 11.5 %collective-permute-start.26 = (bf16[6,64,512]{2,1,0:T(8,128)(2,1)S(1)}, bf16[6,64,512]{2,1,0:T(8,128)(2,1)S(1)}, u32[]{:S(2)}, u32[]{:S(2)}) collective-permute-start(bf16[6,64,512]{2,1,0:T(8,128)(2,1)S(1)} %collective-permute-done.22), channel_id=1, source_target_pairs={{0,4},{1,5},{2,0},{3,1},{6,2},{7,3},{10,6},{11,7},{14,10},{15,11},... | collective-permute-start | bytes 1179656 | tf_op jit(solution)/shard_map/ppermute | solution.py:263
  110.3 6.6 %collective-permute-start.28 = (bf16[6,32,512]{2,1,0:T(8,128)(2,1)S(1)}, bf16[6,32,512]{2,1,0:T(8,128)(2,1)S(1)}, u32[]{:S(2)}, u32[]{:S(2)}) collective-permute-start(bf16[6,32,512]{2,1,0:T(8,128)(2,1)S(1)} %slice.92), channel_id=1, source_target_pairs={{0,2},{1,3},{2,6},{3,7},{6,10},{7,11},{10,14},{11,15},{14,12},{15,... | collective-permute-start | bytes 589832 | tf_op jit(solution)/shard_map/ppermute | solution.py:263
  112.1 6.7 %collective-permute-start.30 = (bf16[6,32,512]{2,1,0:T(8,128)(2,1)S(1)}, bf16[6,32,512]{2,1,0:T(8,128)(2,1)S(1)}, u32[]{:S(2)}, u32[]{:S(2)}) collective-permute-start(bf16[6,32,512]{2,1,0:T(8,128)(2,1)S(1)} %slice.93), channel_id=1, source_target_pairs={{0,4},{1,5},{2,0},{3,1},{6,2},{7,3},{10,6},{11,7},{14,10},{15,11},... | collective-permute-start | bytes 589832 | tf_op jit(solution)/shard_map/ppermute | solution.py:263
  112.6 6.2 %collective-permute-start.25 = (bf16[6,64,512]{2,1,0:T(8,128)(2,1)S(1)}, bf16[6,64,512]{2,1,0:T(8,128)(2,1)S(1)}, u32[]{:S(2)}, u32[]{:S(2)}) collective-permute-start(bf16[6,64,512]{2,1,0:T(8,128)(2,1)S(1)} %collective-permute-done.24), channel_id=1, source_target_pairs={{0,1},{1,0},{2,3},{3,2},{4,5},{5,4},{6,7},{7,6},{8,9},{9,8},{10,11... | collective-permute-start | bytes 1179656 | tf_op jit(solution)/shard_map/ppermute | solution.py:266
  112.6 6.3 %collective-permute-start.27 = (bf16[6,64,512]{2,1,0:T(8,128)(2,1)S(1)}, bf16[6,64,512]{2,1,0:T(8,128)(2,1)S(1)}, u32[]{:S(2)}, u32[]{:S(2)}) collective-permute-start(bf16[6,64,512]{2,1,0:T(8,128)(2,1)S(1)} %collective-permute-done.26), channel_id=1, source_target_pairs={{0,1},{1,0},{2,3},{3,2},{4,5},{5,4},{6,7},{7,6},{8,9},{9,8},{10,11... | collective-permute-start | bytes 1179656 | tf_op jit(solution)/shard_map/ppermute | solution.py:266
  116.8 2.1 %collective-permute-start.29 = (bf16[6,32,512]{2,1,0:T(8,128)(2,1)S(1)}, bf16[6,32,512]{2,1,0:T(8,128)(2,1)S(1)}, u32[]{:S(2)}, u32[]{:S(2)}) collective-permute-start(bf16[6,32,512]{2,1,0:T(8,128)(2,1)S(1)} %collective-permute-done.28), channel_id=1, source_target_pairs={{0,1},{1,0},{2,3},{3,2},{4,5},{5,4},{6,7},{7,6},{8,9},{9,8},{10,11... | collective-permute-start | bytes 589832 | tf_op jit(solution)/shard_map/ppermute | solution.py:266
  118.8 1.4 collective-permute-start.31
  118.9 7.4 %copy-start.2 = (bf16[12,512,256]{2,1,0:T(8,128)(2,1)S(1)}, bf16[12,512,256]{2,1,0:T(8,128)(2,1)}, u32[]{:S(2)}) copy-start(bf16[12,512,256]{2,1,0:T(8,128)(2,1)} %copy-done.1) | copy-start | bytes 9437188
  126.2 5.6 %copy-start.5 = (bf16[2,3,512,256]{3,2,1,0:T(8,128)(2,1)S(1)}, bf16[2,3,512,256]{3,2,1,0:T(8,128)(2,1)}, u32[]{:S(2)}) copy-start(bf16[2,3,512,256]{3,2,1,0:T(8,128)(2,1)} %get-tuple-element.49.far_ref) | copy-start | bytes 4718596
  126.3 5.6 %copy-start.6 = (bf16[2,3,384,256]{3,2,1,0:T(8,128)(2,1)S(1)}, bf16[2,3,384,256]{3,2,1,0:T(8,128)(2,1)}, u32[]{:S(2)}) copy-start(bf16[2,3,384,256]{3,2,1,0:T(8,128)(2,1)} %get-tuple-element.48.near_ref) | copy-start | bytes 3538948

commit v3 on v2

--- a/solution.py
+++ b/solution.py
@@ -177,7 +177,19 @@
         cost_estimate=cost(flops, moved),
         name="own_project",
     )(index, depth_count, normed, qkv_weight, qkv_weight)
-    values = pl.pallas_call(
+    return sent, own, normed
+
+
+def value_projection(normed, qkv_weight, head_count):
+    seqs, residues, features = normed.shape
+    size = features // head_count
+    rows = 128 if residues % 128 == 0 else residues
+    steps = residues // rows
+    flops = 2 * seqs * residues * features * features
+    moved = 2 * (2 * seqs * residues * features + features * features)
+    bf16 = jnp.bfloat16
+    params = pltpu.CompilerParams(vmem_limit_bytes=48 << 20)
+    return pl.pallas_call(
         value_kernel,
         out_shape=jax.ShapeDtypeStruct((head_count, residues, seqs * size), bf16),
         grid=(steps,),
@@ -190,7 +202,6 @@
         cost_estimate=cost(flops, moved),
         name="value_project",
     )(normed, qkv_weight)
-    return sent, own, values
 
 
 def scores_of(own, other, index, table, depth_count, size):
@@ -266,7 +277,7 @@
         return lax.ppermute(value, "seq", [(i, i ^ 1) for i in range(self.devices)])
 
 
-def reduce_scatter(links, scores, side):
+def reduce_scatter(links, scores):
     chips, _, rows, _ = scores.shape
     half = rows // 2
     low, high = slice(0, half), slice(half, rows)
@@ -278,8 +289,6 @@
 
     moving = [None, None]
     gate = None
-    side = list(side)
-    done = []
     for far in range(deep, 0, -1):
         for group in range(2):
             if group == 1 and far == deep:
@@ -288,19 +297,13 @@
             if moving[group] is None:
                 sums = [share(way, part, far).astype(jnp.float16) for way, part in chain]
             else:
-                arrived = moving[group]
-                if gate is not None:
-                    arrived, _ = lax.optimization_barrier((arrived, gate))
-                if side:
-                    arrived, kept = lax.optimization_barrier((arrived, side.pop(0)))
-                    done.append(kept)
+                arrived, _ = lax.optimization_barrier((moving[group], gate))
                 sums = [
                     (value.astype(jnp.float32) + share(way, part, far)).astype(jnp.float16)
                     for value, (way, part) in zip(arrived, chain)
                 ]
             gate = sums
             moving[group] = [links.send(value, way) for value, (way, _) in zip(sums, chain)]
-    (low_ahead, high_back), (high_ahead, low_back) = moving if deep > 1 else (moving[0], (0.0, 0.0))
 
     def settle(part, *arrived):
         total = scores[0, :, part]
@@ -308,32 +311,34 @@
             total = total + value.astype(jnp.float32)
         return total
 
-    if deep > 1:
-        parts = [settle(low, low_ahead, low_back), settle(high, high_ahead, high_back)]
-    else:
-        parts = [settle(low, low_ahead), settle(high, high_back)]
-    return jnp.concatenate(parts, axis=1), done + side
-
-
-def all_gather(links, own, gathered):
+    (low_ahead, high_back), (high_ahead, low_back) = moving
+    parts = [settle(low, low_ahead, low_back), settle(high, high_ahead, high_back)]
+    return jnp.concatenate(parts, axis=1)
+
+
+def all_gather(links, own, side):
     chips = links.chips
-    half = own.shape[1] // 2
+    heads, rows, width = own.shape
+    half = rows // 2
     deep = chips // 2
-    pieces = [(0, 0, own)]
+    gathered = jnp.zeros((2, chips) + own.shape, own.dtype)
+    side = list(side)
+    done = []
+    batches = [(0, own)]
     ahead = back = own
     for far in range(1, deep):
         ahead = links.send(ahead, 1)
         back = links.send(back, -1)
-        pieces += [(chips - far, 0, ahead), (far, 0, back)]
-    pieces += [
-        (deep, 0, links.send(ahead[:, :half], 1)),
-        (deep, half, links.send(back[:, half:], -1)),
-    ]
-    swapped = [links.swap(value) for _, _, value in pieces]
-    for (far, row, value), other in zip(pieces, swapped):
-        for core, piece in enumerate((value, other)):
-            gathered = lax.dynamic_update_slice(gathered, piece[None, None], (core, far, 0, row, 0))
-    return gathered
+        batches += [(chips - far, ahead), (far, back)]
+        if side:
+            (ahead, back), kept = lax.optimization_barrier(((ahead, back), side.pop(0)))
+            done.append(kept)
+    batches.append((deep, [links.send(ahead[:, :half], 1), links.send(back[:, half:], -1)]))
+    for far, batch in batches:
+        piece = jnp.concatenate(batch, axis=1) if far == deep else batch
+        for core, value in enumerate((piece, links.swap(piece))):
+            gathered = lax.dynamic_update_slice(gathered, value[None, None], (core, far, 0, 0, 0))
+    return gathered, done + side
 
 
 ROWS = 4
@@ -383,9 +388,9 @@
         ref[2, m] = right.astype(bf16)
 
     def conv(ref, m, w_ref, which, dilation):
-        before = jnp.maximum(m - 1, 0)
-        after = jnp.minimum(m + 1, blocks - 1)
-        total = None
+        before = max(m - 1, 0)
+        after = min(m + 1, blocks - 1)
+        windows = []
         for col in range(3):
             low = ref[col, before, :, half:]
             high = ref[col, after, :, :half]
@@ -394,42 +399,42 @@
                 edge = [jnp.where(lane < size, high, low)]
             else:
                 edge = [low, high]
-            window = jnp.concatenate([ref[col, m]] + edge, axis=1)
-            part = jnp.dot(window, w_ref[which, col], preferred_element_type=jnp.float32)
-            total = part if total is None else total + part
-        return total
-
-    def start(m, carry):
+            windows += [ref[col, m]] + edge
+        window = jnp.concatenate(windows, axis=1)
+        weight = w_ref[which].reshape(window.shape[1], lanes)
+        return jnp.dot(window, weight, preferred_element_type=jnp.float32)
+
+    def start(m):
         hidden = lax.dot_general(
             pf_ref[m], pair_ref[...], (((0,), (0,)), ((), ())), preferred_element_type=jnp.float32
         )
         hid_ref[m] = hidden
         spread(u_ref, m, hidden, 1)
-        return carry
-
-    lax.fori_loop(0, blocks, start, 0)
-
-    def first(m, carry):
+
+    for m in range(blocks):
+        start(m)
+
+    def first(m):
         inner = masked(m, jnp.maximum(conv(u_ref, m, near_ref, 0, 1), 0.0))
         spread(v_ref, m, inner, 1)
-        return carry
-
-    lax.fori_loop(0, blocks, first, 0)
-
-    def second(m, carry):
+
+    for m in range(blocks):
+        first(m)
+
+    def second(m):
         hidden = masked(m, hid_ref[m] + conv(v_ref, m, near_ref, 1, 1))
         hid_ref[m] = hidden
         spread(u_ref, m, hidden, 2)
-        return carry
-
-    lax.fori_loop(1, blocks - 1, second, 0)
-
-    def third(m, carry):
+
+    for m in range(1, blocks - 1):
+        second(m)
+
+    def third(m):
         inner = masked(m, jnp.maximum(conv(u_ref, m, far_ref, 0, 2), 0.0))
         spread(v_ref, m, inner, 2)
-        return carry
-
-    lax.fori_loop(1, blocks - 1, third, 0)
+
+    for m in range(1, blocks - 1):
+        third(m)
 
     group = lax.broadcasted_iota(jnp.int32, (lanes, 128), 0) // size
     slot = lax.broadcasted_iota(jnp.int32, (lanes, 128), 1)
@@ -444,7 +449,9 @@
             weighed = weighed - coarse.astype(jnp.float32)
         return logits
 
-    logits = lax.fori_loop(2, blocks - 2, last, jnp.zeros((residues, 128), jnp.float32))
+    logits = jnp.zeros((residues, 128), jnp.float32)
+    for m in range(2, blocks - 2):
+        logits = last(m, logits)
     o_ref[...] = 1.0 / (1.0 + jnp.exp(-logits.T[: o_ref.shape[0]]))
 
 
@@ -576,16 +583,16 @@
     head_count = pair_weight.shape[1]
     size = features // head_count
     links = Links()
-    sent, own, values = projections(alignment, qkv_weight, links.index, depth_count, head_count)
+    sent, own, normed = projections(alignment, qkv_weight, links.index, depth_count, head_count)
     other = links.swap(sent)
     scores = scores_of(own, other, links.index, links.table, depth_count, size)
-    rows = residues // links.chips
-    room = jnp.zeros((2, links.chips, head_count // 2, rows, residues), jnp.bfloat16)
-    summed, (room, taps, values) = reduce_scatter(
-        links, scores, (room, spread_taps(conv_weight), values)
+    summed = reduce_scatter(links, scores)
+    probabilities = jax.nn.softmax(summed * (1.0 / LINK_SCALE), axis=-1).astype(jnp.bfloat16)
+    probabilities, normed, conv_weight = lax.optimization_barrier(
+        (probabilities, normed, conv_weight)
     )
-    probabilities = jax.nn.softmax(summed * (1.0 / LINK_SCALE), axis=-1).astype(jnp.bfloat16)
-    gathered = all_gather(links, probabilities, room)
+    values = value_projection(normed, qkv_weight, head_count)
+    gathered, (values, taps) = all_gather(links, probabilities, (values, spread_taps(conv_weight)))
     row_mix = row_mix_of(gathered, values, links.index, links.table, seqs, head_count)
     contacts = contact_head(links, gathered, pair_weight, taps, head_weight)
     return (row_mix, contacts)

time: 165 us -> 144 us (0.87)
  Pallas kernels: 71.4 us -> 58.1 us
  waiting for transfers between devices: 55.9 us -> 51.9 us
  local copies, waits for them, and re-layouts: 7.04 us -> 4.31 us
  other arithmetic: 3.62 us -> 1.93 us
    pallas_call x1, Pallas kernels: 32.7 us -> 19.7 us  [contact_call(): pl.pallas_call(contact_kernel, out_shape=jax.ShapeDtypeStruct((own_rows,...]
    ppermute x22, waiting for transfers between devices: 54.6 us -> 50.4 us  [send(): return lax.ppermute(value, 'seq', pairs)]
    unnamed x24 -> x15, local copies, waits for them, and re-layouts: 4.41 us -> 1.67 us
  transfers between devices with their start and end apart: 32 -> 31, of which waited for: 19 -> 20; matrix products, arithmetic and copies ran while one was open for 2% -> 2% of each run, Pallas kernels for 9% -> 10%
where the time goes in v3:
time: 144 us
  Pallas kernels  58.1 us (40%)
  waiting for transfers between devices  51.9 us (36%)
  starting transfers between devices  25.7 us (18%)
  local copies, waits for them, and re-layouts  4.31 us (3%)
  other arithmetic  1.93 us (1%)
  between operations  1.66 us (1%)
    ppermute x22, waiting for transfers between devices, send(): return lax.ppermute(value, 'seq', pairs)  50.4 us
    ppermute x22, starting transfers between devices, send(): return lax.ppermute(value, 'seq', pairs)  23.6 us
    pallas_call x1, Pallas kernels, contact_call(): pl.pallas_call(contact_kernel, out_shape=jax.ShapeDtypeStruct((own_rows,...  19.7 us
    pallas_call x1, Pallas kernels, projections(): pl.pallas_call(norm_send_kernel, out_shape=(jax.ShapeDtypeStruct(alignmen...  8.16 us
    pallas_call x1, Pallas kernels, projections(): pl.pallas_call(own_kernel, out_shape=qk_shape, grid_spec=pltpu.PrefetchSc...  6.01 us
    pallas_call x1, Pallas kernels, contact_head(): pl.pallas_call(window_kernel, out_shape=jax.ShapeDtypeStruct((blocks, ROW...  5.99 us
    pallas_call x1, Pallas kernels, row_mix_of(): pl.pallas_call(mix_kernel, out_shape=jax.ShapeDtypeStruct((seqs, residues...  5.57 us
    pallas_call x1, Pallas kernels, value_projection(): pl.pallas_call(value_kernel, out_shape=jax.ShapeDtypeStruct((head_count,...  5.48 us
  transfers between devices with their start and end apart: 31, of which 20 were waited for; matrix products, arithmetic and copies ran while one was open for 2% of the time, Pallas kernels for 10%

profile of v3, /device:TPU:0, one launch (start us, length us, event | category | flops | bytes accessed | tf_op | source)
XLA Modules:
  0.0 143.6 jit_solution(4522047210800194397)
XLA Ops:
  1.3 8.2 %norm_send.1 = (bf16[4,512,768]{2,1,0:T(8,128)(2,1)S(1)}, bf16[2,6,512,256]{3,2,1,0:T(8,128)(2,1)}) custom-call(s32[1]{0:T(128)} %bitcast.index_ref, s32[1]{0:T(128)S(6)} %copy.26.depth_ref, bf16[4,512,768]{2,1,0:T(8,128)(2,1)} %x_ref.1, bf16[768,2304]{1,0:T(8,128)(2,1)} %w_ref.1, bf16[768,2304]{1,0:T(8,128)(2,1)} %w_ref.1), custom_call_target="tpu_custom_call" | custom-call | flops 2415919104 | bytes 10616832 | tf_op jit(solution)/shard_map/norm_send/pallas_call | solution.py:154
  9.4 1.6 %copy-done = bf16[4,512,768]{2,1,0:T(8,128)(2,1)} copy-done((bf16[4,512,768]{2,1,0:T(8,128)(2,1)}, bf16[4,512,768]{2,1,0:T(8,128)(2,1)S(1)}, u32[]{:S(2)}) %copy-start) | copy-done | bytes 3145752
  11.1 0.5 collective-permute-start
  11.5 6.0 %own_project.1.own_ref = bf16[2,6,512,256]{3,2,1,0:T(8,128)(2,1)S(1)} custom-call(s32[1]{0:T(128)} %bitcast.index_ref, s32[1]{0:T(128)S(6)} %copy.26.depth_ref, bf16[4,512,768]{2,1,0:T(8,128)(2,1)} %copy-done, bf16[768,2304]{1,0:T(8,128)(2,1)} %w_ref.1, bf16[768,2304]{1,0:T(8,128)(2,1)} %w_ref.1), custom_call_target="tpu_custom_call" | custom-call | flops 2415919104 | bytes 7471104 | tf_op jit(solution)/shard_map/own_project/pallas_call | solution.py:167
  17.6 4.2 %scores.1 = f32[8,6,64,512]{3,2,1,0:T(8,128)S(1)} custom-call(s32[1]{0:T(128)} %bitcast.index_ref, s32[16]{0:T(128)S(1)} %copy-done.1, s32[1]{0:T(128)S(6)} %copy.26.depth_ref, bf16[2,6,512,256]{3,2,1,0:T(8,128)(2,1)S(1)} %own_project.1.own_ref, bf16[2,6,512,256]{3,2,1,0:T(8,128)(2,1)S(1)} %collective-permute-done.other_ref), custom_call_target="tpu_custom_call" | custom-call | flops 1610612736 | bytes 12582912 | tf_op jit(solution)/shard_map/scores/pallas_call | solution.py:212
  21.8 0.7 convert.6
  22.5 0.2 slice_bitcast_fusion.12
  22.7 2.6 %collective-permute-start.1 = (f16[6,32,512]{2,1,0:T(8,128)(2,1)S(1)}, f16[6,32,512]{2,1,0:T(8,128)(2,1)S(1)}, u32[]{:S(2)}, u32[]{:S(2)}) collective-permute-start(f16[6,32,512]{2,1,0:T(8,128)(2,1)S(1)} %get-tuple-element.63), channel_id=1, source_target_pairs={{0,2},{1,3},{2,6},{3,7},{6,10},{7,11},{10,14},{11,15},{14,12},{15,... | collective-permute-start | bytes 589832 | tf_op jit(solution)/shard_map/ppermute | solution.py:274
  25.4 5.5 %collective-permute-done.1 = f16[6,32,512]{2,1,0:T(8,128)(2,1)S(1)} collective-permute-done((f16[6,32,512]{2,1,0:T(8,128)(2,1)S(1)}, f16[6,32,512]{2,1,0:T(8,128)(2,1)S(1)}, u32[]{:S(2)}, u32[]{:S(2)}) %collective-permute-start.1) | collective-permute-done | bytes 196640 | tf_op jit(solution)/shard_map/ppermute | solution.py:274
  30.9 1.4 collective-permute-done.2
  32.4 0.1 fusion.26
  32.5 1.6 %collective-permute-start.3 = (f16[6,32,512]{2,1,0:T(8,128)(2,1)S(1)}, f16[6,32,512]{2,1,0:T(8,128)(2,1)S(1)}, u32[]{:S(2)}, u32[]{:S(2)}) collective-permute-start(f16[6,32,512]{2,1,0:T(8,128)(2,1)S(1)} %get-tuple-element.59), channel_id=1, source_target_pairs={{0,2},{1,3},{2,6},{3,7},{6,10},{7,11},{10,14},{11,15},{14,12},{15,... | collective-permute-start | bytes 589832 | tf_op jit(solution)/shard_map/ppermute | solution.py:274
  34.1 0.5 collective-permute-start.4
  34.6 1.6 %collective-permute-start.7 = (f16[6,32,512]{2,1,0:T(8,128)(2,1)S(1)}, f16[6,32,512]{2,1,0:T(8,128)(2,1)S(1)}, u32[]{:S(2)}, u32[]{:S(2)}) collective-permute-start(f16[6,32,512]{2,1,0:T(8,128)(2,1)S(1)} %get-tuple-element.61), channel_id=1, source_target_pairs={{0,2},{1,3},{2,6},{3,7},{6,10},{7,11},{10,14},{11,15},{14,12},{15,... | collective-permute-start | bytes 589832 | tf_op jit(solution)/shard_map/ppermute | solution.py:274
  36.2 0.5 collective-permute-start.8
  36.6 3.8 %collective-permute-done.3 = f16[6,32,512]{2,1,0:T(8,128)(2,1)S(1)} collective-permute-done((f16[6,32,512]{2,1,0:T(8,128)(2,1)S(1)}, f16[6,32,512]{2,1,0:T(8,128)(2,1)S(1)}, u32[]{:S(2)}, u32[]{:S(2)}) %collective-permute-start.3) | collective-permute-done | bytes 196640 | tf_op jit(solution)/shard_map/ppermute | solution.py:274
  40.4 1.6 %collective-permute-done.4 = f16[6,32,512]{2,1,0:T(8,128)(2,1)S(1)} collective-permute-done((f16[6,32,512]{2,1,0:T(8,128)(2,1)S(1)}, f16[6,32,512]{2,1,0:T(8,128)(2,1)S(1)}, u32[]{:S(2)}, u32[]{:S(2)}) %collective-permute-start.4) | collective-permute-done | bytes 196640 | tf_op jit(solution)/shard_map/ppermute | solution.py:274
  42.0 0.1 fusion.22
  42.1 1.6 %collective-permute-start.5 = (f16[6,32,512]{2,1,0:T(8,128)(2,1)S(1)}, f16[6,32,512]{2,1,0:T(8,128)(2,1)S(1)}, u32[]{:S(2)}, u32[]{:S(2)}) collective-permute-start(f16[6,32,512]{2,1,0:T(8,128)(2,1)S(1)} %get-tuple-element.57), channel_id=1, source_target_pairs={{0,2},{1,3},{2,6},{3,7},{6,10},{7,11},{10,14},{11,15},{14,12},{15,... | collective-permute-start | bytes 589832 | tf_op jit(solution)/shard_map/ppermute | solution.py:274
  43.7 0.4 collective-permute-start.6
  44.2 0.4 collective-permute-done.7
  44.6 1.6 %collective-permute-done.8 = f16[6,32,512]{2,1,0:T(8,128)(2,1)S(1)} collective-permute-done((f16[6,32,512]{2,1,0:T(8,128)(2,1)S(1)}, f16[6,32,512]{2,1,0:T(8,128)(2,1)S(1)}, u32[]{:S(2)}, u32[]{:S(2)}) %collective-permute-start.8) | collective-permute-done | bytes 196640 | tf_op jit(solution)/shard_map/ppermute | solution.py:274
  46.2 0.1 fusion.18
  46.3 1.6 %collective-permute-start.10 = (f16[6,32,512]{2,1,0:T(8,128)(2,1)S(1)}, f16[6,32,512]{2,1,0:T(8,128)(2,1)S(1)}, u32[]{:S(2)}, u32[]{:S(2)}) collective-permute-start(f16[6,32,512]{2,1,0:T(8,128)(2,1)S(1)} %get-tuple-element.55), channel_id=1, source_target_pairs={{0,2},{1,3},{2,6},{3,7},{6,10},{7,11},{10,14},{11,15},{14,12},{15,... | collective-permute-start | bytes 589832 | tf_op jit(solution)/shard_map/ppermute | solution.py:274
  48.0 0.4 collective-permute-start.11
  48.4 1.1 collective-permute-done.5
  49.5 1.3 collective-permute-done.6
  50.8 0.1 fusion.16
  50.9 1.1 collective-permute-done.10
  52.1 2.3 %collective-permute-done.11 = f16[6,32,512]{2,1,0:T(8,128)(2,1)S(1)} collective-permute-done((f16[6,32,512]{2,1,0:T(8,128)(2,1)S(1)}, f16[6,32,512]{2,1,0:T(8,128)(2,1)S(1)}, u32[]{:S(2)}, u32[]{:S(2)}) %collective-permute-start.11) | collective-permute-done | bytes 196640 | tf_op jit(solution)/shard_map/ppermute | solution.py:274
  54.4 0.5 collective-permute-start.12
  54.9 1.6 %collective-permute-start.9 = (f16[6,32,512]{2,1,0:T(8,128)(2,1)S(1)}, f16[6,32,512]{2,1,0:T(8,128)(2,1)S(1)}, u32[]{:S(2)}, u32[]{:S(2)}) collective-permute-start(f16[6,32,512]{2,1,0:T(8,128)(2,1)S(1)} %get-tuple-element.52), channel_id=1, source_target_pairs={{0,2},{1,3},{2,6},{3,7},{6,10},{7,11},{10,14},{11,15},{14,12},{15,... | collective-permute-start | bytes 589832 | tf_op jit(solution)/shard_map/ppermute | solution.py:274
  56.4 0.4 collective-permute-start.14
  56.9 3.2 %collective-permute-done.12 = f16[6,32,512]{2,1,0:T(8,128)(2,1)S(1)} collective-permute-done((f16[6,32,512]{2,1,0:T(8,128)(2,1)S(1)}, f16[6,32,512]{2,1,0:T(8,128)(2,1)S(1)}, u32[]{:S(2)}, u32[]{:S(2)}) %collective-permute-start.12) | collective-permute-done | bytes 196640 | tf_op jit(solution)/shard_map/ppermute | solution.py:274
  60.1 2.5 %collective-permute-done.9 = f16[6,32,512]{2,1,0:T(8,128)(2,1)S(1)} collective-permute-done((f16[6,32,512]{2,1,0:T(8,128)(2,1)S(1)}, f16[6,32,512]{2,1,0:T(8,128)(2,1)S(1)}, u32[]{:S(2)}, u32[]{:S(2)}) %collective-permute-start.9) | collective-permute-done | bytes 196640 | tf_op jit(solution)/shard_map/ppermute | solution.py:274
  62.6 0.2 fusion.30
  62.8 1.6 %collective-permute-start.13 = (f16[6,32,512]{2,1,0:T(8,128)(2,1)S(1)}, f16[6,32,512]{2,1,0:T(8,128)(2,1)S(1)}, u32[]{:S(2)}, u32[]{:S(2)}) collective-permute-start(f16[6,32,512]{2,1,0:T(8,128)(2,1)S(1)} %get-tuple-element.51), channel_id=1, source_target_pairs={{0,2},{1,3},{2,6},{3,7},{6,10},{7,11},{10,14},{11,15},{14,12},{15,... | collective-permute-start | bytes 589832 | tf_op jit(solution)/shard_map/ppermute | solution.py:274
  64.4 4.1 %collective-permute-done.13 = f16[6,32,512]{2,1,0:T(8,128)(2,1)S(1)} collective-permute-done((f16[6,32,512]{2,1,0:T(8,128)(2,1)S(1)}, f16[6,32,512]{2,1,0:T(8,128)(2,1)S(1)}, u32[]{:S(2)}, u32[]{:S(2)}) %collective-permute-start.13) | collective-permute-done | bytes 196640 | tf_op jit(solution)/shard_map/ppermute | solution.py:274
  68.6 0.3 fusion.5
  69.0 1.6 %collective-permute-start.16 = (bf16[6,64,512]{2,1,0:T(8,128)(2,1)S(1)}, bf16[6,64,512]{2,1,0:T(8,128)(2,1)S(1)}, u32[]{:S(2)}, u32[]{:S(2)}) collective-permute-start(bf16[6,64,512]{2,1,0:T(8,128)(2,1)S(1)} %fusion.5), channel_id=1, source_target_pairs={{0,2},{1,3},{2,6},{3,7},{6,10},{7,11},{10,14},{11,15},{14,12},{15,... | collective-permute-start | bytes 1179656 | tf_op jit(solution)/shard_map/ppermute | solution.py:274
  70.6 0.4 collective-permute-start.18
  71.3 1.0 copy.9
  72.4 2.9 %spread_taps.1 = (bf16[2,3,384,256]{3,2,1,0:T(8,128)(2,1)}, bf16[2,3,512,256]{3,2,1,0:T(8,128)(2,1)}) custom-call(bf16[36,64,64]{2,1,0:T(8,128)(2,1)} %bitcast.115), custom_call_target="tpu_custom_call" | custom-call | bytes 6291456 | tf_op jit(solution)/shard_map/spread_taps/pallas_call | solution.py:461
  75.3 0.8 dynamic_update_slice.48
  76.1 5.5 %value_project.1.v_ref = bf16[12,512,256]{2,1,0:T(8,128)(2,1)S(1)} custom-call(bf16[4,512,768]{2,1,0:T(8,128)(2,1)} %copy-done, bf16[768,2304]{1,0:T(8,128)(2,1)} %w_ref.1), custom_call_target="tpu_custom_call" | custom-call | flops 2415919104 | bytes 7471104 | tf_op jit(solution)/shard_map/value_project/pallas_call | solution.py:192
  81.6 0.2 collective-permute-done.18
  81.8 1.4 collective-permute-start.20
  83.2 0.6 collective-permute-start.22
  83.8 0.5 collective-permute-start.19
  84.4 8.1 %collective-permute-done.20 = bf16[6,64,512]{2,1,0:T(8,128)(2,1)S(1)} collective-permute-done((bf16[6,64,512]{2,1,0:T(8,128)(2,1)S(1)}, bf16[6,64,512]{2,1,0:T(8,128)(2,1)S(1)}, u32[]{:S(2)}, u32[]{:S(2)}) %collective-permute-start.20) | collective-permute-done | bytes 393248 | tf_op jit(solution)/shard_map/ppermute | solution.py:274
  92.5 1.3 collective-permute-done.22
  93.8 0.9 collective-permute-start.24
  94.7 1.1 collective-permute-start.26
  95.9 0.5 collective-permute-start.23
  96.5 7.0 %collective-permute-done.24 = bf16[6,64,512]{2,1,0:T(8,128)(2,1)S(1)} collective-permute-done((bf16[6,64,512]{2,1,0:T(8,128)(2,1)S(1)}, bf16[6,64,512]{2,1,0:T(8,128)(2,1)S(1)}, u32[]{:S(2)}, u32[]{:S(2)}) %collective-permute-start.24) | collective-permute-done | bytes 393248 | tf_op jit(solution)/shard_map/ppermute | solution.py:274
  103.6 1.0 collective-permute-start.28
  104.5 1.4 collective-permute-start.29
  105.9 0.5 collective-permute-start.27
  106.6 2.7 %collective-permute-done.28 = bf16[6,32,512]{2,1,0:T(8,128)(2,1)S(1)} collective-permute-done((bf16[6,32,512]{2,1,0:T(8,128)(2,1)S(1)}, bf16[6,32,512]{2,1,0:T(8,128)(2,1)S(1)}, u32[]{:S(2)}, u32[]{:S(2)}) %collective-permute-start.28) | collective-permute-done | bytes 196640 | tf_op jit(solution)/shard_map/ppermute | solution.py:274
  109.3 1.1 collective-permute-done.29
  110.7 1.5 %collective-permute-done.30 = bf16[6,64,512]{2,1,0:T(8,128)(2,1)S(1)} collective-permute-done((bf16[6,64,512]{2,1,0:T(8,128)(2,1)S(1)}, bf16[6,64,512]{2,1,0:T(8,128)(2,1)S(1)}, u32[]{:S(2)}, u32[]{:S(2)}) %collective-permute-start.30) | collective-permute-done | bytes 393248 | tf_op jit(solution)/shard_map/ppermute | solution.py:277
  112.3 6.0 %pair_window.1.pf_ref = bf16[12,48,512]{2,1,0:T(8,128)(2,1)S(1)} custom-call(s32[1]{0:T(128)} %bitcast.index_ref, s32[16]{0:T(128)S(1)} %copy-done.1, bf16[2,8,6,64,512]{4,3,2,1,0:T(8,128)(2,1)S(1)} %bitcast_dynamic-update-slice_fusion.p_ref), custom_call_target="tpu_custom_call" | custom-call | flops 2717908992 | bytes 6291456 | tf_op jit(solution)/shard_map/pair_window/pallas_call | solution.py:540
  118.3 5.6 %row_mix.1 = bf16[4,512,768]{2,1,0:T(8,128)(2,1)} custom-call(s32[1]{0:T(128)} %bitcast.index_ref, s32[16]{0:T(128)S(1)} %copy-done.1, bf16[2,8,6,64,512]{4,3,2,1,0:T(8,128)(2,1)S(1)} %bitcast_dynamic-update-slice_fusion.p_ref, bf16[12,512,256]{2,1,0:T(8,128)(2,1)S(1)} %value_project.1.v_ref), custom_call_target="tpu_custom_call" | custom-call | flops 1610612736 | bytes 12582912 | tf_op jit(solution)/shard_map/row_mix/pallas_call | solution.py:237
  123.9 19.7 %contact_head.1 = f32[32,512]{1,0:T(8,128)} custom-call(s32[1]{0:T(128)} %bitcast.index_ref, bf16[12,48,512]{2,1,0:T(8,128)(2,1)S(1)} %pair_window.1.pf_ref, bf16[48,256]{1,0:T(8,128)(2,1)S(1)} %mul.28.pair_ref, bf16[2,3,384,256]{3,2,1,0:T(8,128)(2,1)S(1)} %copy-done.3, bf16[2,3,512,256]{3,2,1,0:T(8,128)(2,1)S(1)} %copy-done.2, ...), custom_call_target="tpu_custom_call" | custom-call | flops 5469372416 | bytes 4194304 | tf_op jit(solution)/shard_map/contact_head/pallas_call | solution.py:565
  (56 shorter events, 1.2 us)
Async XLA Ops:
  9.4 1.6 %copy-start = (bf16[4,512,768]{2,1,0:T(8,128)(2,1)}, bf16[4,512,768]{2,1,0:T(8,128)(2,1)S(1)}, u32[]{:S(2)}) copy-start(bf16[4,512,768]{2,1,0:T(8,128)(2,1)S(1)} %get-tuple-element.39.normed_ref) | copy-start | bytes 9437188
  11.1 6.5 %collective-permute-start = (bf16[2,6,512,256]{3,2,1,0:T(8,128)(2,1)}, bf16[2,6,512,256]{3,2,1,0:T(8,128)(2,1)S(1)}, u32[]{:S(2)}, u32[]{:S(2)}) collective-permute-start(bf16[2,6,512,256]{3,2,1,0:T(8,128)(2,1)} %get-tuple-element.27), channel_id=1, source_target_pairs={{0,1},{1,0},{2,3},{3,2},{4,5},{5,4},{6,7},{7,6},{8,9},{9,8},{10,11... | collective-permute-start | bytes 9437192 | tf_op jit(solution)/shard_map/ppermute | solution.py:277
  11.5 6.0 %copy-start.1 = (s32[16]{0:T(128)S(1)}, s32[16]{0:T(128)}, u32[]{:S(2)}) copy-start(s32[16]{0:T(128)} %constant.13.clone.table_ref) | copy-start | bytes 196
  22.7 8.2 %collective-permute-start.1 = (f16[6,32,512]{2,1,0:T(8,128)(2,1)S(1)}, f16[6,32,512]{2,1,0:T(8,128)(2,1)S(1)}, u32[]{:S(2)}, u32[]{:S(2)}) collective-permute-start(f16[6,32,512]{2,1,0:T(8,128)(2,1)S(1)} %get-tuple-element.63), channel_id=1, source_target_pairs={{0,2},{1,3},{2,6},{3,7},{6,10},{7,11},{10,14},{11,15},{14,12},{15,... | collective-permute-start | bytes 589832 | tf_op jit(solution)/shard_map/ppermute | solution.py:274
  25.3 7.0 %collective-permute-start.2 = (f16[6,32,512]{2,1,0:T(8,128)(2,1)S(1)}, f16[6,32,512]{2,1,0:T(8,128)(2,1)S(1)}, u32[]{:S(2)}, u32[]{:S(2)}) collective-permute-start(f16[6,32,512]{2,1,0:T(8,128)(2,1)S(1)} %get-tuple-element.62), channel_id=1, source_target_pairs={{0,4},{1,5},{2,0},{3,1},{6,2},{7,3},{10,6},{11,7},{14,10},{15,11},... | collective-permute-start | bytes 589832 | tf_op jit(solution)/shard_map/ppermute | solution.py:274
  32.5 38.5 %copy-start.5 = (bf16[64,12]{0,1:T(8,128)(2,1)S(1)}, bf16[64,12]{0,1:T(8,128)(2,1)}, u32[]{:S(2)}) copy-start(bf16[64,12]{0,1:T(8,128)(2,1)} %param.10) | copy-start | bytes 4612
  32.5 38.7 %copy-start.6 = (f32[64]{0:T(128)S(1)}, f32[64]{0:T(128)}, u32[]{:S(2)}) copy-start(f32[64]{0:T(128)} %param.12) | copy-start | bytes 772
  32.5 38.8 %copy-start.4 = (bf16[4,9,64,64]{3,2,1,0:T(8,128)(2,1)S(1)}, bf16[4,9,64,64]{3,2,1,0:T(8,128)(2,1)}, u32[]{:S(2)}) copy-start(bf16[4,9,64,64]{3,2,1,0:T(8,128)(2,1)} %param.11) | copy-start | bytes 884740
  32.5 7.9 %collective-permute-start.3 = (f16[6,32,512]{2,1,0:T(8,128)(2,1)S(1)}, f16[6,32,512]{2,1,0:T(8,128)(2,1)S(1)}, u32[]{:S(2)}, u32[]{:S(2)}) collective-permute-start(f16[6,32,512]{2,1,0:T(8,128)(2,1)S(1)} %get-tuple-element.59), channel_id=1, source_target_pairs={{0,2},{1,3},{2,6},{3,7},{6,10},{7,11},{10,14},{11,15},{14,12},{15,... | collective-permute-start | bytes 589832 | tf_op jit(solution)/shard_map/ppermute | solution.py:274
  34.1 7.8 %collective-permute-start.4 = (f16[6,32,512]{2,1,0:T(8,128)(2,1)S(1)}, f16[6,32,512]{2,1,0:T(8,128)(2,1)S(1)}, u32[]{:S(2)}, u32[]{:S(2)}) collective-permute-start(f16[6,32,512]{2,1,0:T(8,128)(2,1)S(1)} %get-tuple-element.58), channel_id=1, source_target_pairs={{0,4},{1,5},{2,0},{3,1},{6,2},{7,3},{10,6},{11,7},{14,10},{15,11},... | collective-permute-start | bytes 589832 | tf_op jit(solution)/shard_map/ppermute | solution.py:274
  34.6 10.0 %collective-permute-start.7 = (f16[6,32,512]{2,1,0:T(8,128)(2,1)S(1)}, f16[6,32,512]{2,1,0:T(8,128)(2,1)S(1)}, u32[]{:S(2)}, u32[]{:S(2)}) collective-permute-start(f16[6,32,512]{2,1,0:T(8,128)(2,1)S(1)} %get-tuple-element.61), channel_id=1, source_target_pairs={{0,2},{1,3},{2,6},{3,7},{6,10},{7,11},{10,14},{11,15},{14,12},{15,... | collective-permute-start | bytes 589832 | tf_op jit(solution)/shard_map/ppermute | solution.py:274
  36.2 10.0 %collective-permute-start.8 = (f16[6,32,512]{2,1,0:T(8,128)(2,1)S(1)}, f16[6,32,512]{2,1,0:T(8,128)(2,1)S(1)}, u32[]{:S(2)}, u32[]{:S(2)}) collective-permute-start(f16[6,32,512]{2,1,0:T(8,128)(2,1)S(1)} %get-tuple-element.60), channel_id=1, source_target_pairs={{0,4},{1,5},{2,0},{3,1},{6,2},{7,3},{10,6},{11,7},{14,10},{15,11},... | collective-permute-start | bytes 589832 | tf_op jit(solution)/shard_map/ppermute | solution.py:274
  42.1 7.4 %collective-permute-start.5 = (f16[6,32,512]{2,1,0:T(8,128)(2,1)S(1)}, f16[6,32,512]{2,1,0:T(8,128)(2,1)S(1)}, u32[]{:S(2)}, u32[]{:S(2)}) collective-permute-start(f16[6,32,512]{2,1,0:T(8,128)(2,1)S(1)} %get-tuple-element.57), channel_id=1, source_target_pairs={{0,2},{1,3},{2,6},{3,7},{6,10},{7,11},{10,14},{11,15},{14,12},{15,... | collective-permute-start | bytes 589832 | tf_op jit(solution)/shard_map/ppermute | solution.py:274
  43.7 7.0 %collective-permute-start.6 = (f16[6,32,512]{2,1,0:T(8,128)(2,1)S(1)}, f16[6,32,512]{2,1,0:T(8,128)(2,1)S(1)}, u32[]{:S(2)}, u32[]{:S(2)}) collective-permute-start(f16[6,32,512]{2,1,0:T(8,128)(2,1)S(1)} %get-tuple-element.56), channel_id=1, source_target_pairs={{0,4},{1,5},{2,0},{3,1},{6,2},{7,3},{10,6},{11,7},{14,10},{15,11},... | collective-permute-start | bytes 589832 | tf_op jit(solution)/shard_map/ppermute | solution.py:274
  46.3 5.7 %collective-permute-start.10 = (f16[6,32,512]{2,1,0:T(8,128)(2,1)S(1)}, f16[6,32,512]{2,1,0:T(8,128)(2,1)S(1)}, u32[]{:S(2)}, u32[]{:S(2)}) collective-permute-start(f16[6,32,512]{2,1,0:T(8,128)(2,1)S(1)} %get-tuple-element.55), channel_id=1, source_target_pairs={{0,2},{1,3},{2,6},{3,7},{6,10},{7,11},{10,14},{11,15},{14,12},{15,... | collective-permute-start | bytes 589832 | tf_op jit(solution)/shard_map/ppermute | solution.py:274
  48.0 6.3 %collective-permute-start.11 = (f16[6,32,512]{2,1,0:T(8,128)(2,1)S(1)}, f16[6,32,512]{2,1,0:T(8,128)(2,1)S(1)}, u32[]{:S(2)}, u32[]{:S(2)}) collective-permute-start(f16[6,32,512]{2,1,0:T(8,128)(2,1)S(1)} %get-tuple-element.54), channel_id=1, source_target_pairs={{0,4},{1,5},{2,0},{3,1},{6,2},{7,3},{10,6},{11,7},{14,10},{15,11},... | collective-permute-start | bytes 589832 | tf_op jit(solution)/shard_map/ppermute | solution.py:274
  54.4 5.7 %collective-permute-start.12 = (f16[6,32,512]{2,1,0:T(8,128)(2,1)S(1)}, f16[6,32,512]{2,1,0:T(8,128)(2,1)S(1)}, u32[]{:S(2)}, u32[]{:S(2)}) collective-permute-start(f16[6,32,512]{2,1,0:T(8,128)(2,1)S(1)} %fusion.12), channel_id=1, source_target_pairs={{0,4},{1,5},{2,0},{3,1},{6,2},{7,3},{10,6},{11,7},{14,10},{15,11},... | collective-permute-start | bytes 589832 | tf_op jit(solution)/shard_map/ppermute | solution.py:274
  54.9 7.7 %collective-permute-start.9 = (f16[6,32,512]{2,1,0:T(8,128)(2,1)S(1)}, f16[6,32,512]{2,1,0:T(8,128)(2,1)S(1)}, u32[]{:S(2)}, u32[]{:S(2)}) collective-permute-start(f16[6,32,512]{2,1,0:T(8,128)(2,1)S(1)} %get-tuple-element.52), channel_id=1, source_target_pairs={{0,2},{1,3},{2,6},{3,7},{6,10},{7,11},{10,14},{11,15},{14,12},{15,... | collective-permute-start | bytes 589832 | tf_op jit(solution)/shard_map/ppermute | solution.py:274
  56.4 8.0 %collective-permute-start.14 = (f16[6,32,512]{2,1,0:T(8,128)(2,1)S(1)}, f16[6,32,512]{2,1,0:T(8,128)(2,1)S(1)}, u32[]{:S(2)}, u32[]{:S(2)}) collective-permute-start(f16[6,32,512]{2,1,0:T(8,128)(2,1)S(1)} %get-tuple-element.53), channel_id=1, source_target_pairs={{0,4},{1,5},{2,0},{3,1},{6,2},{7,3},{10,6},{11,7},{14,10},{15,11},... | collective-permute-start | bytes 589832 | tf_op jit(solution)/shard_map/ppermute | solution.py:274
  62.8 5.7 %collective-permute-start.13 = (f16[6,32,512]{2,1,0:T(8,128)(2,1)S(1)}, f16[6,32,512]{2,1,0:T(8,128)(2,1)S(1)}, u32[]{:S(2)}, u32[]{:S(2)}) collective-permute-start(f16[6,32,512]{2,1,0:T(8,128)(2,1)S(1)} %get-tuple-element.51), channel_id=1, source_target_pairs={{0,2},{1,3},{2,6},{3,7},{6,10},{7,11},{10,14},{11,15},{14,12},{15,... | collective-permute-start | bytes 589832 | tf_op jit(solution)/shard_map/ppermute | solution.py:274
  68.9 15.4 %collective-permute-start.15 = (bf16[6,64,512]{2,1,0:T(8,128)(2,1)S(1)}, bf16[6,64,512]{2,1,0:T(8,128)(2,1)S(1)}, u32[]{:S(2)}, u32[]{:S(2)}) collective-permute-start(bf16[6,64,512]{2,1,0:T(8,128)(2,1)S(1)} %fusion.5), channel_id=1, source_target_pairs={{0,1},{1,0},{2,3},{3,2},{4,5},{5,4},{6,7},{7,6},{8,9},{9,8},{10,11... | collective-permute-start | bytes 1179656 | tf_op jit(solution)/shard_map/ppermute | solution.py:277
  69.0 12.6 %collective-permute-start.16 = (bf16[6,64,512]{2,1,0:T(8,128)(2,1)S(1)}, bf16[6,64,512]{2,1,0:T(8,128)(2,1)S(1)}, u32[]{:S(2)}, u32[]{:S(2)}) collective-permute-start(bf16[6,64,512]{2,1,0:T(8,128)(2,1)S(1)} %fusion.5), channel_id=1, source_target_pairs={{0,2},{1,3},{2,6},{3,7},{6,10},{7,11},{10,14},{11,15},{14,12},{15,... | collective-permute-start | bytes 1179656 | tf_op jit(solution)/shard_map/ppermute | solution.py:274
  70.6 11.2 %collective-permute-start.18 = (bf16[6,64,512]{2,1,0:T(8,128)(2,1)S(1)}, bf16[6,64,512]{2,1,0:T(8,128)(2,1)S(1)}, u32[]{:S(2)}, u32[]{:S(2)}) collective-permute-start(bf16[6,64,512]{2,1,0:T(8,128)(2,1)S(1)} %fusion.5), channel_id=1, source_target_pairs={{0,4},{1,5},{2,0},{3,1},{6,2},{7,3},{10,6},{11,7},{14,10},{15,11},... | collective-permute-start | bytes 1179656 | tf_op jit(solution)/shard_map/ppermute | solution.py:274
  81.8 10.8 %collective-permute-start.20 = (bf16[6,64,512]{2,1,0:T(8,128)(2,1)S(1)}, bf16[6,64,512]{2,1,0:T(8,128)(2,1)S(1)}, u32[]{:S(2)}, u32[]{:S(2)}) collective-permute-start(bf16[6,64,512]{2,1,0:T(8,128)(2,1)S(1)} %collective-permute-done.16), channel_id=1, source_target_pairs={{0,2},{1,3},{2,6},{3,7},{6,10},{7,11},{10,14},{11,15},{14,12},{15,... | collective-permute-start | bytes 1179656 | tf_op jit(solution)/shard_map/ppermute | solution.py:274
  83.2 10.6 %collective-permute-start.22 = (bf16[6,64,512]{2,1,0:T(8,128)(2,1)S(1)}, bf16[6,64,512]{2,1,0:T(8,128)(2,1)S(1)}, u32[]{:S(2)}, u32[]{:S(2)}) collective-permute-start(bf16[6,64,512]{2,1,0:T(8,128)(2,1)S(1)} %collective-permute-done.18), channel_id=1, source_target_pairs={{0,4},{1,5},{2,0},{3,1},{6,2},{7,3},{10,6},{11,7},{14,10},{15,11},... | collective-permute-start | bytes 1179656 | tf_op jit(solution)/shard_map/ppermute | solution.py:274
  83.8 12.1 %collective-permute-start.17 = (bf16[6,64,512]{2,1,0:T(8,128)(2,1)S(1)}, bf16[6,64,512]{2,1,0:T(8,128)(2,1)S(1)}, u32[]{:S(2)}, u32[]{:S(2)}) collective-permute-start(bf16[6,64,512]{2,1,0:T(8,128)(2,1)S(1)} %collective-permute-done.16), channel_id=1, source_target_pairs={{0,1},{1,0},{2,3},{3,2},{4,5},{5,4},{6,7},{7,6},{8,9},{9,8},{10,11... | collective-permute-start | bytes 1179656 | tf_op jit(solution)/shard_map/ppermute | solution.py:277
  83.8 12.6 %collective-permute-start.19 = (bf16[6,64,512]{2,1,0:T(8,128)(2,1)S(1)}, bf16[6,64,512]{2,1,0:T(8,128)(2,1)S(1)}, u32[]{:S(2)}, u32[]{:S(2)}) collective-permute-start(bf16[6,64,512]{2,1,0:T(8,128)(2,1)S(1)} %collective-permute-done.18), channel_id=1, source_target_pairs={{0,1},{1,0},{2,3},{3,2},{4,5},{5,4},{6,7},{7,6},{8,9},{9,8},{10,11... | collective-permute-start | bytes 1179656 | tf_op jit(solution)/shard_map/ppermute | solution.py:277
  93.8 9.7 %collective-permute-start.24 = (bf16[6,64,512]{2,1,0:T(8,128)(2,1)S(1)}, bf16[6,64,512]{2,1,0:T(8,128)(2,1)S(1)}, u32[]{:S(2)}, u32[]{:S(2)}) collective-permute-start(bf16[6,64,512]{2,1,0:T(8,128)(2,1)S(1)} %collective-permute-done.20), channel_id=1, source_target_pairs={{0,2},{1,3},{2,6},{3,7},{6,10},{7,11},{10,14},{11,15},{14,12},{15,... | collective-permute-start | bytes 1179656 | tf_op jit(solution)/shard_map/ppermute | solution.py:274
  94.7 9.8 %collective-permute-start.26 = (bf16[6,64,512]{2,1,0:T(8,128)(2,1)S(1)}, bf16[6,64,512]{2,1,0:T(8,128)(2,1)S(1)}, u32[]{:S(2)}, u32[]{:S(2)}) collective-permute-start(bf16[6,64,512]{2,1,0:T(8,128)(2,1)S(1)} %collective-permute-done.22), channel_id=1, source_target_pairs={{0,4},{1,5},{2,0},{3,1},{6,2},{7,3},{10,6},{11,7},{14,10},{15,11},... | collective-permute-start | bytes 1179656 | tf_op jit(solution)/shard_map/ppermute | solution.py:274
  95.8 10.0 %collective-permute-start.21 = (bf16[6,64,512]{2,1,0:T(8,128)(2,1)S(1)}, bf16[6,64,512]{2,1,0:T(8,128)(2,1)S(1)}, u32[]{:S(2)}, u32[]{:S(2)}) collective-permute-start(bf16[6,64,512]{2,1,0:T(8,128)(2,1)S(1)} %collective-permute-done.20), channel_id=1, source_target_pairs={{0,1},{1,0},{2,3},{3,2},{4,5},{5,4},{6,7},{7,6},{8,9},{9,8},{10,11... | collective-permute-start | bytes 1179656 | tf_op jit(solution)/shard_map/ppermute | solution.py:277
  95.9 10.6 %collective-permute-start.23 = (bf16[6,64,512]{2,1,0:T(8,128)(2,1)S(1)}, bf16[6,64,512]{2,1,0:T(8,128)(2,1)S(1)}, u32[]{:S(2)}, u32[]{:S(2)}) collective-permute-start(bf16[6,64,512]{2,1,0:T(8,128)(2,1)S(1)} %collective-permute-done.22), channel_id=1, source_target_pairs={{0,1},{1,0},{2,3},{3,2},{4,5},{5,4},{6,7},{7,6},{8,9},{9,8},{10,11... | collective-permute-start | bytes 1179656 | tf_op jit(solution)/shard_map/ppermute | solution.py:277
  103.6 5.7 %collective-permute-start.28 = (bf16[6,32,512]{2,1,0:T(8,128)(2,1)S(1)}, bf16[6,32,512]{2,1,0:T(8,128)(2,1)S(1)}, u32[]{:S(2)}, u32[]{:S(2)}) collective-permute-start(bf16[6,32,512]{2,1,0:T(8,128)(2,1)S(1)} %slice.92), channel_id=1, source_target_pairs={{0,2},{1,3},{2,6},{3,7},{6,10},{7,11},{10,14},{11,15},{14,12},{15,... | collective-permute-start | bytes 589832 | tf_op jit(solution)/shard_map/ppermute | solution.py:274
  104.5 5.9 %collective-permute-start.29 = (bf16[6,32,512]{2,1,0:T(8,128)(2,1)S(1)}, bf16[6,32,512]{2,1,0:T(8,128)(2,1)S(1)}, u32[]{:S(2)}, u32[]{:S(2)}) collective-permute-start(bf16[6,32,512]{2,1,0:T(8,128)(2,1)S(1)} %slice.93), channel_id=1, source_target_pairs={{0,4},{1,5},{2,0},{3,1},{6,2},{7,3},{10,6},{11,7},{14,10},{15,11},... | collective-permute-start | bytes 589832 | tf_op jit(solution)/shard_map/ppermute | solution.py:274
  105.9 4.6 %collective-permute-start.25 = (bf16[6,64,512]{2,1,0:T(8,128)(2,1)S(1)}, bf16[6,64,512]{2,1,0:T(8,128)(2,1)S(1)}, u32[]{:S(2)}, u32[]{:S(2)}) collective-permute-start(bf16[6,64,512]{2,1,0:T(8,128)(2,1)S(1)} %collective-permute-done.24), channel_id=1, source_target_pairs={{0,1},{1,0},{2,3},{3,2},{4,5},{5,4},{6,7},{7,6},{8,9},{9,8},{10,11... | collective-permute-start | bytes 1179656 | tf_op jit(solution)/shard_map/ppermute | solution.py:277
  105.9 4.7 %collective-permute-start.27 = (bf16[6,64,512]{2,1,0:T(8,128)(2,1)S(1)}, bf16[6,64,512]{2,1,0:T(8,128)(2,1)S(1)}, u32[]{:S(2)}, u32[]{:S(2)}) collective-permute-start(bf16[6,64,512]{2,1,0:T(8,128)(2,1)S(1)} %collective-permute-done.26), channel_id=1, source_target_pairs={{0,1},{1,0},{2,3},{3,2},{4,5},{5,4},{6,7},{7,6},{8,9},{9,8},{10,11... | collective-permute-start | bytes 1179656 | tf_op jit(solution)/shard_map/ppermute | solution.py:277
  110.4 1.8 %collective-permute-start.30 = (bf16[6,64,512]{2,1,0:T(8,128)(2,1)S(1)}, bf16[6,64,512]{2,1,0:T(8,128)(2,1)S(1)}, u32[]{:S(2)}, u32[]{:S(2)}) collective-permute-start(bf16[6,64,512]{2,1,0:T(8,128)(2,1)S(1)} %constant_dynamic-update-slice_fusion), channel_id=1, source_target_pairs={{0,1},{1,0},{2,3},{3,2},{4,5},{5,4},{6,7},{7,6},{8,9},{9,8},{10,11... | collective-permute-start | bytes 1179656 | tf_op jit(solution)/shard_map/ppermute | solution.py:277
  118.3 5.6 %copy-start.2 = (bf16[2,3,512,256]{3,2,1,0:T(8,128)(2,1)S(1)}, bf16[2,3,512,256]{3,2,1,0:T(8,128)(2,1)}, u32[]{:S(2)}) copy-start(bf16[2,3,512,256]{3,2,1,0:T(8,128)(2,1)} %get-tuple-element.49.far_ref) | copy-start | bytes 4718596
  118.3 5.6 %copy-start.3 = (bf16[2,3,384,256]{3,2,1,0:T(8,128)(2,1)S(1)}, bf16[2,3,384,256]{3,2,1,0:T(8,128)(2,1)}, u32[]{:S(2)}) copy-start(bf16[2,3,384,256]{3,2,1,0:T(8,128)(2,1)} %get-tuple-element.48.near_ref) | copy-start | bytes 3538948

commit v4 on v3

--- a/solution.py
+++ b/solution.py
@@ -46,47 +46,54 @@
     return table_ref[chips + lax.rem(place + ahead, chips)]
 
 
+def rows_here(ref_rows):
+    return pl.ds(pl.multiple_of(pl.program_id(0) * ref_rows, ref_rows), ref_rows)
+
+
 def norm_send_kernel(index_ref, depth_ref, x_ref, wq_ref, wk_ref, normed_ref, qk_ref):
     seqs, rows, width = x_ref.shape
-    size = qk_ref.shape[3] // seqs
     values = x_ref[...].reshape(seqs * rows, width).astype(jnp.float32)
     average = jnp.mean(values, axis=-1, keepdims=True)
     centered = values - average
     variance = jnp.mean(centered * centered, axis=-1, keepdims=True)
     normed = (centered * lax.rsqrt(variance + EPSILON)).astype(jnp.bfloat16)
-    normed_ref[...] = normed.reshape(seqs, rows, width)
-    project(index_ref, depth_ref, normed, wq_ref, wk_ref, qk_ref, seqs, rows, size)
-
-
-def own_kernel(index_ref, depth_ref, normed_ref, wq_ref, wk_ref, qk_ref):
-    seqs, rows, width = normed_ref.shape
+    normed_ref[:, rows_here(rows), :] = normed.reshape(seqs, rows, width)
+    project(index_ref, depth_ref, normed, wq_ref, wk_ref, qk_ref, seqs, rows)
+
+
+def own_kernel(rows, index_ref, depth_ref, normed_ref, wq_ref, wk_ref, qk_ref):
+    seqs, _, width = normed_ref.shape
+    normed = normed_ref[:, rows_here(rows), :].reshape(seqs * rows, width)
+    project(index_ref, depth_ref, normed, wq_ref, wk_ref, qk_ref, seqs, rows)
+
+
+def project(index_ref, depth_ref, normed, wq_ref, wk_ref, qk_ref, seqs, rows):
     size = qk_ref.shape[3] // seqs
-    normed = normed_ref[...].reshape(seqs * rows, width)
-    project(index_ref, depth_ref, normed, wq_ref, wk_ref, qk_ref, seqs, rows, size)
-
-
-def project(index_ref, depth_ref, normed, wq_ref, wk_ref, qk_ref, seqs, rows, size):
-    q = jnp.dot(normed, wq_ref[...], preferred_element_type=jnp.float32).astype(jnp.bfloat16)
+    here = rows_here(rows)
+    weight = jnp.concatenate([wq_ref[...], wk_ref[...]], axis=1)
+    both = jnp.dot(normed, weight, preferred_element_type=jnp.float32).astype(jnp.bfloat16)
+    q, k = both[:, : weight.shape[1] // 2], both[:, weight.shape[1] // 2 :]
     for head, block in enumerate(head_major(q, seqs, rows, size)):
         lane = lax.broadcasted_iota(jnp.int32, block.shape, 1)
         in_use = (depth_ref[0] - index_ref[0] * seqs) * size
-        qk_ref[0, head] = jnp.where(lane < in_use, block, jnp.zeros_like(block))
-    k = jnp.dot(normed, wk_ref[...], preferred_element_type=jnp.float32).astype(jnp.bfloat16)
+        qk_ref[0, head, here, :] = jnp.where(lane < in_use, block, jnp.zeros_like(block))
     for head, block in enumerate(head_major(k, seqs, rows, size)):
-        qk_ref[1, head] = block
-
-
-def value_kernel(normed_ref, w_ref, v_ref):
-    seqs, rows, width = normed_ref.shape
+        qk_ref[1, head, here, :] = block
+
+
+def value_kernel(rows, normed_ref, w_ref, v_ref):
+    seqs, _, width = normed_ref.shape
     size = v_ref.shape[2] // seqs
-    normed = normed_ref[...].reshape(seqs * rows, width)
+    here = rows_here(rows)
+    normed = normed_ref[:, here, :].reshape(seqs * rows, width)
     v = jnp.dot(normed, w_ref[...], preferred_element_type=jnp.float32).astype(jnp.bfloat16)
     for head, block in enumerate(head_major(v, seqs, rows, size)):
-        v_ref[head] = block
+        v_ref[head, here, :] = block
 
 
 def score_kernel(size, index_ref, table_ref, depth_ref, own_ref, other_ref, s_ref):
     chips, _, rows, residues = s_ref.shape
+    here = pl.program_id(0)
     depth = jnp.full((1, residues), depth_ref[0], jnp.int32).astype(jnp.float32)
     scale = size**-0.5 / jnp.sqrt(depth) * LINK_SCALE
     places = [
@@ -95,24 +102,31 @@
     ]
     total = None
     for ref in (own_ref, other_ref):
-        q = jnp.concatenate([ref[0, 0, place, :] for place in places], axis=0)
+        q = jnp.concatenate([ref[0, here, place, :] for place in places], axis=0)
         part = lax.dot_general(
-            q, ref[1, 0], (((1,), (1,)), ((), ())), preferred_element_type=jnp.float32
+            q, ref[1, here], (((1,), (1,)), ((), ())), preferred_element_type=jnp.float32
         )
         total = part if total is None else total + part
     total = total * scale
-    s_ref[...] = total.reshape(chips, 1, rows, total.shape[1])
+    s_ref[:, here] = total.reshape(chips, rows, total.shape[1])
 
 
 def mix_kernel(index_ref, table_ref, p_ref, v_ref, o_ref):
     seqs = o_ref.shape[0]
     size = v_ref.shape[2] // seqs
-    _, chips, _, rows, residues = p_ref.shape
+    _, chips, heads, rows, residues = p_ref.shape
+    pairs = heads // 2
+    step = pl.program_id(0)
+    side = lax.div(step, pairs)
+    first = 2 * lax.rem(step, pairs)
+    start = lax.rem(index_ref[0] + side, 2) * heads + first
     mixed = []
-    for head in range(v_ref.shape[0]):
-        probs = p_ref[0, :, head].reshape(chips * rows, residues)
+    for head in range(2):
+        probs = p_ref[side, :, first + head].reshape(chips * rows, residues)
         mixed.append(
-            jnp.dot(probs, v_ref[head], preferred_element_type=jnp.float32).astype(jnp.bfloat16)
+            jnp.dot(probs, v_ref[start + head], preferred_element_type=jnp.float32).astype(
+                jnp.bfloat16
+            )
         )
     places = [
         pl.ds(pl.multiple_of(ring_place(index_ref, table_ref, ahead) * rows, rows), rows)
@@ -134,12 +148,12 @@
     seqs, residues, features = alignment.shape
     heads = head_count // 2
     size = features // head_count
-    rows = 128 if residues % 128 == 0 else residues
+    rows = 256 if residues % 256 == 0 else residues
     cols = heads * size
     steps = residues // rows
     bf16 = jnp.bfloat16
     x_spec = pl.BlockSpec((seqs, rows, features), lambda i, *_: (0, i, 0))
-    qk_spec = pl.BlockSpec((2, heads, rows, seqs * size), lambda i, *_: (0, 0, i, 0))
+    vmem = pl.BlockSpec(memory_space=pltpu.VMEM)
     qk_shape = jax.ShapeDtypeStruct((2, heads, residues, seqs * size), bf16)
     params = pltpu.CompilerParams(vmem_limit_bytes=48 << 20)
 
@@ -158,20 +172,20 @@
             num_scalar_prefetch=2,
             grid=(steps,),
             in_specs=[x_spec] + weight_specs(lambda half: 1 - half),
-            out_specs=[x_spec, qk_spec],
+            out_specs=[vmem, vmem],
         ),
         compiler_params=params,
         cost_estimate=cost(flops, moved + 2 * alignment.size),
         name="norm_send",
     )(index, depth_count, alignment, qkv_weight, qkv_weight)
     own = pl.pallas_call(
-        own_kernel,
+        functools.partial(own_kernel, rows),
         out_shape=qk_shape,
         grid_spec=pltpu.PrefetchScalarGridSpec(
             num_scalar_prefetch=2,
             grid=(steps,),
-            in_specs=[x_spec] + weight_specs(lambda half: half),
-            out_specs=qk_spec,
+            in_specs=[vmem] + weight_specs(lambda half: half),
+            out_specs=vmem,
         ),
         compiler_params=params,
         cost_estimate=cost(flops, moved),
@@ -183,21 +197,21 @@
 def value_projection(normed, qkv_weight, head_count):
     seqs, residues, features = normed.shape
     size = features // head_count
-    rows = 128 if residues % 128 == 0 else residues
+    rows = 256 if residues % 256 == 0 else residues
     steps = residues // rows
     flops = 2 * seqs * residues * features * features
     moved = 2 * (2 * seqs * residues * features + features * features)
     bf16 = jnp.bfloat16
     params = pltpu.CompilerParams(vmem_limit_bytes=48 << 20)
     return pl.pallas_call(
-        value_kernel,
+        functools.partial(value_kernel, rows),
         out_shape=jax.ShapeDtypeStruct((head_count, residues, seqs * size), bf16),
         grid=(steps,),
         in_specs=[
-            pl.BlockSpec((seqs, rows, features), lambda i: (0, i, 0)),
+            pl.BlockSpec(memory_space=pltpu.VMEM),
             pl.BlockSpec((features, features), lambda i: (0, 2)),
         ],
-        out_specs=pl.BlockSpec((head_count, rows, seqs * size), lambda i: (0, i, 0)),
+        out_specs=pl.BlockSpec(memory_space=pltpu.VMEM),
         compiler_params=params,
         cost_estimate=cost(flops, moved),
         name="value_project",
@@ -208,7 +222,7 @@
     _, heads, residues, inner = own.shape
     chips = table.shape[0] // 2
     rows = residues // chips
-    spec = pl.BlockSpec((2, 1, residues, inner), lambda h, *_: (0, h, 0, 0))
+    spec = pl.BlockSpec(memory_space=pltpu.VMEM)
     return pl.pallas_call(
         functools.partial(score_kernel, size),
         out_shape=jax.ShapeDtypeStruct((chips, heads, rows, residues), jnp.float32),
@@ -216,7 +230,7 @@
             num_scalar_prefetch=3,
             grid=(heads,),
             in_specs=[spec, spec],
-            out_specs=pl.BlockSpec((chips, 1, rows, residues), lambda h, *_: (0, h, 0, 0)),
+            out_specs=spec,
         ),
         compiler_params=pltpu.CompilerParams(vmem_limit_bytes=32 << 20),
         cost_estimate=cost(4 * heads * residues * residues * inner, 4 * own.size + 4 * heads * residues**2),
@@ -240,13 +254,7 @@
         grid_spec=pltpu.PrefetchScalarGridSpec(
             num_scalar_prefetch=2,
             grid=(2 * pairs,),
-            in_specs=[
-                pl.BlockSpec(
-                    (1, chips, 2, rows, residues),
-                    lambda g, *_: (lax.div(g, pairs), 0, lax.rem(g, pairs), 0, 0),
-                ),
-                pl.BlockSpec((2, residues, inner), lambda g, index, _: (pair_at(g, index), 0, 0)),
-            ],
+            in_specs=[pl.BlockSpec(memory_space=pltpu.VMEM)] * 2,
             out_specs=pl.BlockSpec(
                 (seqs, residues, 2 * size), lambda g, index, _: (0, 0, pair_at(g, index))
             ),

time: 144 us -> 141 us (0.979)
  Pallas kernels: 58.1 us -> 55.3 us
  transfers between devices with their start and end apart: 31 -> 31, of which waited for: 20 -> 21; matrix products, arithmetic and copies ran while one was open for 2% -> 2% of each run, Pallas kernels for 10% -> 9%
where the time goes in v4:
time: 141 us
  Pallas kernels  55.3 us (39%)
  waiting for transfers between devices  51.4 us (36%)
  starting transfers between devices  26.3 us (19%)
  local copies, waits for them, and re-layouts  4.31 us (3%)
  other arithmetic  1.93 us (1%)
  between operations  1.65 us (1%)
    ppermute x22, waiting for transfers between devices, send(): return lax.ppermute(value, 'seq', pairs)  49.5 us
    ppermute x22, starting transfers between devices, send(): return lax.ppermute(value, 'seq', pairs)  24.2 us
    pallas_call x1, Pallas kernels, contact_call(): pl.pallas_call(contact_kernel, out_shape=jax.ShapeDtypeStruct((own_rows,...  19.7 us
    pallas_call x1, Pallas kernels, projections(): pl.pallas_call(norm_send_kernel, out_shape=(jax.ShapeDtypeStruct(alignmen...  7.74 us
    pallas_call x1, Pallas kernels, contact_head(): pl.pallas_call(window_kernel, out_shape=jax.ShapeDtypeStruct((blocks, ROW...  5.99 us
    pallas_call x1, Pallas kernels, row_mix_of(): pl.pallas_call(mix_kernel, out_shape=jax.ShapeDtypeStruct((seqs, residues...  5.24 us
    pallas_call x1, Pallas kernels, value_projection(): pl.pallas_call(functools.partial(value_kernel, rows), out_shape=jax.Shape...  5.19 us
    pallas_call x1, Pallas kernels, projections(): pl.pallas_call(functools.partial(own_kernel, rows), out_shape=qk_shape, g...  5.18 us
  transfers between devices with their start and end apart: 31, of which 21 were waited for; matrix products, arithmetic and copies ran while one was open for 2% of the time, Pallas kernels for 9%

profile of v4, /device:TPU:0, one launch (start us, length us, event | category | flops | bytes accessed | tf_op | source)
XLA Modules:
  0.0 140.9 jit_solution(3104652474965981572)
XLA Ops:
  1.3 7.7 %norm_send.1 = (bf16[4,512,768]{2,1,0:T(8,128)(2,1)S(1)}, bf16[2,6,512,256]{3,2,1,0:T(8,128)(2,1)}) custom-call(s32[1]{0:T(128)} %bitcast.index_ref, s32[1]{0:T(128)S(6)} %copy.26.depth_ref, bf16[4,512,768]{2,1,0:T(8,128)(2,1)} %x_ref.1, bf16[768,2304]{1,0:T(8,128)(2,1)} %w_ref.1, bf16[768,2304]{1,0:T(8,128)(2,1)} %w_ref.1), custom_call_target="tpu_custom_call" | custom-call | flops 2415919104 | bytes 10616832 | tf_op jit(solution)/shard_map/norm_send/pallas_call | solution.py:168
  9.0 1.6 %copy-done = bf16[4,512,768]{2,1,0:T(8,128)(2,1)} copy-done((bf16[4,512,768]{2,1,0:T(8,128)(2,1)}, bf16[4,512,768]{2,1,0:T(8,128)(2,1)S(1)}, u32[]{:S(2)}) %copy-start) | copy-done | bytes 3145752
  10.6 0.5 collective-permute-start
  11.1 5.2 %own_project.1.own_ref = bf16[2,6,512,256]{3,2,1,0:T(8,128)(2,1)S(1)} custom-call(s32[1]{0:T(128)} %bitcast.index_ref, s32[1]{0:T(128)S(6)} %copy.26.depth_ref, bf16[4,512,768]{2,1,0:T(8,128)(2,1)} %copy-done, bf16[768,2304]{1,0:T(8,128)(2,1)} %w_ref.1, bf16[768,2304]{1,0:T(8,128)(2,1)} %w_ref.1), custom_call_target="tpu_custom_call" | custom-call | flops 2415919104 | bytes 7471104 | tf_op jit(solution)/shard_map/own_project/pallas_call | solution.py:181
  16.3 0.3 collective-permute-done.other_ref
  16.6 3.4 %scores.1 = f32[8,6,64,512]{3,2,1,0:T(8,128)S(1)} custom-call(s32[1]{0:T(128)} %bitcast.index_ref, s32[16]{0:T(128)S(1)} %copy-done.1, s32[1]{0:T(128)S(6)} %copy.26.depth_ref, bf16[2,6,512,256]{3,2,1,0:T(8,128)(2,1)S(1)} %own_project.1.own_ref, bf16[2,6,512,256]{3,2,1,0:T(8,128)(2,1)S(1)} %collective-permute-done.other_ref), custom_call_target="tpu_custom_call" | custom-call | flops 1610612736 | bytes 12582912 | tf_op jit(solution)/shard_map/scores/pallas_call | solution.py:226
  20.0 0.7 convert.6
  20.7 0.2 slice_bitcast_fusion.12
  20.9 2.9 %collective-permute-start.1 = (f16[6,32,512]{2,1,0:T(8,128)(2,1)S(1)}, f16[6,32,512]{2,1,0:T(8,128)(2,1)S(1)}, u32[]{:S(2)}, u32[]{:S(2)}) collective-permute-start(f16[6,32,512]{2,1,0:T(8,128)(2,1)S(1)} %get-tuple-element.63), channel_id=1, source_target_pairs={{0,2},{1,3},{2,6},{3,7},{6,10},{7,11},{10,14},{11,15},{14,12},{15,... | collective-permute-start | bytes 589832 | tf_op jit(solution)/shard_map/ppermute | solution.py:282
  24.0 5.1 %collective-permute-done.1 = f16[6,32,512]{2,1,0:T(8,128)(2,1)S(1)} collective-permute-done((f16[6,32,512]{2,1,0:T(8,128)(2,1)S(1)}, f16[6,32,512]{2,1,0:T(8,128)(2,1)S(1)}, u32[]{:S(2)}, u32[]{:S(2)}) %collective-permute-start.1) | collective-permute-done | bytes 196640 | tf_op jit(solution)/shard_map/ppermute | solution.py:282
  29.1 1.4 %collective-permute-done.2 = f16[6,32,512]{2,1,0:T(8,128)(2,1)S(1)} collective-permute-done((f16[6,32,512]{2,1,0:T(8,128)(2,1)S(1)}, f16[6,32,512]{2,1,0:T(8,128)(2,1)S(1)}, u32[]{:S(2)}, u32[]{:S(2)}) %collective-permute-start.2) | collective-permute-done | bytes 196640 | tf_op jit(solution)/shard_map/ppermute | solution.py:282
  30.5 0.1 fusion.26
  30.7 1.6 %collective-permute-start.3 = (f16[6,32,512]{2,1,0:T(8,128)(2,1)S(1)}, f16[6,32,512]{2,1,0:T(8,128)(2,1)S(1)}, u32[]{:S(2)}, u32[]{:S(2)}) collective-permute-start(f16[6,32,512]{2,1,0:T(8,128)(2,1)S(1)} %get-tuple-element.59), channel_id=1, source_target_pairs={{0,2},{1,3},{2,6},{3,7},{6,10},{7,11},{10,14},{11,15},{14,12},{15,... | collective-permute-start | bytes 589832 | tf_op jit(solution)/shard_map/ppermute | solution.py:282
  32.3 0.5 collective-permute-start.4
  32.8 1.6 %collective-permute-start.7 = (f16[6,32,512]{2,1,0:T(8,128)(2,1)S(1)}, f16[6,32,512]{2,1,0:T(8,128)(2,1)S(1)}, u32[]{:S(2)}, u32[]{:S(2)}) collective-permute-start(f16[6,32,512]{2,1,0:T(8,128)(2,1)S(1)} %get-tuple-element.61), channel_id=1, source_target_pairs={{0,2},{1,3},{2,6},{3,7},{6,10},{7,11},{10,14},{11,15},{14,12},{15,... | collective-permute-start | bytes 589832 | tf_op jit(solution)/shard_map/ppermute | solution.py:282
  34.4 0.5 collective-permute-start.8
  34.8 3.8 %collective-permute-done.3 = f16[6,32,512]{2,1,0:T(8,128)(2,1)S(1)} collective-permute-done((f16[6,32,512]{2,1,0:T(8,128)(2,1)S(1)}, f16[6,32,512]{2,1,0:T(8,128)(2,1)S(1)}, u32[]{:S(2)}, u32[]{:S(2)}) %collective-permute-start.3) | collective-permute-done | bytes 196640 | tf_op jit(solution)/shard_map/ppermute | solution.py:282
  38.6 1.3 collective-permute-done.4
  39.9 0.1 fusion.22
  40.1 1.6 %collective-permute-start.5 = (f16[6,32,512]{2,1,0:T(8,128)(2,1)S(1)}, f16[6,32,512]{2,1,0:T(8,128)(2,1)S(1)}, u32[]{:S(2)}, u32[]{:S(2)}) collective-permute-start(f16[6,32,512]{2,1,0:T(8,128)(2,1)S(1)} %get-tuple-element.57), channel_id=1, source_target_pairs={{0,2},{1,3},{2,6},{3,7},{6,10},{7,11},{10,14},{11,15},{14,12},{15,... | collective-permute-start | bytes 589832 | tf_op jit(solution)/shard_map/ppermute | solution.py:282
  41.7 0.4 collective-permute-start.6
  42.2 0.7 collective-permute-done.7
  42.8 1.3 collective-permute-done.8
  44.1 0.1 fusion.18
  44.3 1.6 %collective-permute-start.10 = (f16[6,32,512]{2,1,0:T(8,128)(2,1)S(1)}, f16[6,32,512]{2,1,0:T(8,128)(2,1)S(1)}, u32[]{:S(2)}, u32[]{:S(2)}) collective-permute-start(f16[6,32,512]{2,1,0:T(8,128)(2,1)S(1)} %get-tuple-element.55), channel_id=1, source_target_pairs={{0,2},{1,3},{2,6},{3,7},{6,10},{7,11},{10,14},{11,15},{14,12},{15,... | collective-permute-start | bytes 589832 | tf_op jit(solution)/shard_map/ppermute | solution.py:282
  45.9 0.5 collective-permute-start.11
  46.3 0.8 collective-permute-done.5
  47.1 1.3 collective-permute-done.6
  48.5 1.5 %collective-permute-done.10 = f16[6,32,512]{2,1,0:T(8,128)(2,1)S(1)} collective-permute-done((f16[6,32,512]{2,1,0:T(8,128)(2,1)S(1)}, f16[6,32,512]{2,1,0:T(8,128)(2,1)S(1)}, u32[]{:S(2)}, u32[]{:S(2)}) %collective-permute-start.10) | collective-permute-done | bytes 196640 | tf_op jit(solution)/shard_map/ppermute | solution.py:282
  50.0 3.1 %collective-permute-done.11 = f16[6,32,512]{2,1,0:T(8,128)(2,1)S(1)} collective-permute-done((f16[6,32,512]{2,1,0:T(8,128)(2,1)S(1)}, f16[6,32,512]{2,1,0:T(8,128)(2,1)S(1)}, u32[]{:S(2)}, u32[]{:S(2)}) %collective-permute-start.11) | collective-permute-done | bytes 196640 | tf_op jit(solution)/shard_map/ppermute | solution.py:282
  53.2 0.5 collective-permute-start.12
  53.7 1.6 %collective-permute-start.9 = (f16[6,32,512]{2,1,0:T(8,128)(2,1)S(1)}, f16[6,32,512]{2,1,0:T(8,128)(2,1)S(1)}, u32[]{:S(2)}, u32[]{:S(2)}) collective-permute-start(f16[6,32,512]{2,1,0:T(8,128)(2,1)S(1)} %get-tuple-element.52), channel_id=1, source_target_pairs={{0,2},{1,3},{2,6},{3,7},{6,10},{7,11},{10,14},{11,15},{14,12},{15,... | collective-permute-start | bytes 589832 | tf_op jit(solution)/shard_map/ppermute | solution.py:282
  55.3 0.4 collective-permute-start.14
  55.7 3.2 %collective-permute-done.12 = f16[6,32,512]{2,1,0:T(8,128)(2,1)S(1)} collective-permute-done((f16[6,32,512]{2,1,0:T(8,128)(2,1)S(1)}, f16[6,32,512]{2,1,0:T(8,128)(2,1)S(1)}, u32[]{:S(2)}, u32[]{:S(2)}) %collective-permute-start.12) | collective-permute-done | bytes 196640 | tf_op jit(solution)/shard_map/ppermute | solution.py:282
  58.9 1.6 %collective-permute-done.9 = f16[6,32,512]{2,1,0:T(8,128)(2,1)S(1)} collective-permute-done((f16[6,32,512]{2,1,0:T(8,128)(2,1)S(1)}, f16[6,32,512]{2,1,0:T(8,128)(2,1)S(1)}, u32[]{:S(2)}, u32[]{:S(2)}) %collective-permute-start.9) | collective-permute-done | bytes 196640 | tf_op jit(solution)/shard_map/ppermute | solution.py:282
  60.5 0.2 fusion.30
  60.7 1.9 %collective-permute-start.13 = (f16[6,32,512]{2,1,0:T(8,128)(2,1)S(1)}, f16[6,32,512]{2,1,0:T(8,128)(2,1)S(1)}, u32[]{:S(2)}, u32[]{:S(2)}) collective-permute-start(f16[6,32,512]{2,1,0:T(8,128)(2,1)S(1)} %get-tuple-element.51), channel_id=1, source_target_pairs={{0,2},{1,3},{2,6},{3,7},{6,10},{7,11},{10,14},{11,15},{14,12},{15,... | collective-permute-start | bytes 589832 | tf_op jit(solution)/shard_map/ppermute | solution.py:282
  62.6 3.8 %collective-permute-done.13 = f16[6,32,512]{2,1,0:T(8,128)(2,1)S(1)} collective-permute-done((f16[6,32,512]{2,1,0:T(8,128)(2,1)S(1)}, f16[6,32,512]{2,1,0:T(8,128)(2,1)S(1)}, u32[]{:S(2)}, u32[]{:S(2)}) %collective-permute-start.13) | collective-permute-done | bytes 196640 | tf_op jit(solution)/shard_map/ppermute | solution.py:282
  66.5 0.3 fusion.5
  66.9 1.9 %collective-permute-start.16 = (bf16[6,64,512]{2,1,0:T(8,128)(2,1)S(1)}, bf16[6,64,512]{2,1,0:T(8,128)(2,1)S(1)}, u32[]{:S(2)}, u32[]{:S(2)}) collective-permute-start(bf16[6,64,512]{2,1,0:T(8,128)(2,1)S(1)} %fusion.5), channel_id=1, source_target_pairs={{0,2},{1,3},{2,6},{3,7},{6,10},{7,11},{10,14},{11,15},{14,12},{15,... | collective-permute-start | bytes 1179656 | tf_op jit(solution)/shard_map/ppermute | solution.py:282
  68.8 0.2 collective-permute-start.18
  69.2 1.0 copy.9
  70.3 2.9 %spread_taps.1 = (bf16[2,3,384,256]{3,2,1,0:T(8,128)(2,1)}, bf16[2,3,512,256]{3,2,1,0:T(8,128)(2,1)}) custom-call(bf16[36,64,64]{2,1,0:T(8,128)(2,1)} %bitcast.115), custom_call_target="tpu_custom_call" | custom-call | bytes 6291456 | tf_op jit(solution)/shard_map/spread_taps/pallas_call | solution.py:469
  73.2 0.8 dynamic_update_slice.48
  74.0 5.2 %value_project.1.v_ref = bf16[12,512,256]{2,1,0:T(8,128)(2,1)S(1)} custom-call(bf16[4,512,768]{2,1,0:T(8,128)(2,1)} %copy-done, bf16[768,2304]{1,0:T(8,128)(2,1)} %w_ref.1), custom_call_target="tpu_custom_call" | custom-call | flops 2415919104 | bytes 7471104 | tf_op jit(solution)/shard_map/value_project/pallas_call | solution.py:206
  79.2 0.8 collective-permute-done.18
  80.0 1.1 collective-permute-start.20
  81.1 0.9 collective-permute-start.22
  82.0 0.5 collective-permute-start.19
  82.6 7.7 %collective-permute-done.20 = bf16[6,64,512]{2,1,0:T(8,128)(2,1)S(1)} collective-permute-done((bf16[6,64,512]{2,1,0:T(8,128)(2,1)S(1)}, bf16[6,64,512]{2,1,0:T(8,128)(2,1)S(1)}, u32[]{:S(2)}, u32[]{:S(2)}) %collective-permute-start.20) | collective-permute-done | bytes 393248 | tf_op jit(solution)/shard_map/ppermute | solution.py:282
  90.3 1.4 collective-permute-done.22
  91.7 0.7 collective-permute-start.24
  92.4 1.3 collective-permute-start.26
  93.8 0.5 collective-permute-start.23
  94.4 7.0 %collective-permute-done.24 = bf16[6,64,512]{2,1,0:T(8,128)(2,1)S(1)} collective-permute-done((bf16[6,64,512]{2,1,0:T(8,128)(2,1)S(1)}, bf16[6,64,512]{2,1,0:T(8,128)(2,1)S(1)}, u32[]{:S(2)}, u32[]{:S(2)}) %collective-permute-start.24) | collective-permute-done | bytes 393248 | tf_op jit(solution)/shard_map/ppermute | solution.py:282
  101.5 0.8 collective-permute-start.28
  102.2 1.6 %collective-permute-start.29 = (bf16[6,32,512]{2,1,0:T(8,128)(2,1)S(1)}, bf16[6,32,512]{2,1,0:T(8,128)(2,1)S(1)}, u32[]{:S(2)}, u32[]{:S(2)}) collective-permute-start(bf16[6,32,512]{2,1,0:T(8,128)(2,1)S(1)} %slice.93), channel_id=1, source_target_pairs={{0,4},{1,5},{2,0},{3,1},{6,2},{7,3},{10,6},{11,7},{14,10},{15,11},... | collective-permute-start | bytes 589832 | tf_op jit(solution)/shard_map/ppermute | solution.py:282
  103.8 0.5 collective-permute-start.27
  104.5 2.7 %collective-permute-done.28 = bf16[6,32,512]{2,1,0:T(8,128)(2,1)S(1)} collective-permute-done((bf16[6,32,512]{2,1,0:T(8,128)(2,1)S(1)}, bf16[6,32,512]{2,1,0:T(8,128)(2,1)S(1)}, u32[]{:S(2)}, u32[]{:S(2)}) %collective-permute-start.28) | collective-permute-done | bytes 196640 | tf_op jit(solution)/shard_map/ppermute | solution.py:282
  107.2 0.9 collective-permute-done.29
  108.4 1.5 %collective-permute-done.30 = bf16[6,64,512]{2,1,0:T(8,128)(2,1)S(1)} collective-permute-done((bf16[6,64,512]{2,1,0:T(8,128)(2,1)S(1)}, bf16[6,64,512]{2,1,0:T(8,128)(2,1)S(1)}, u32[]{:S(2)}, u32[]{:S(2)}) %collective-permute-start.30) | collective-permute-done | bytes 393248 | tf_op jit(solution)/shard_map/ppermute | solution.py:285
  110.0 6.0 %pair_window.1.pf_ref = bf16[12,48,512]{2,1,0:T(8,128)(2,1)S(1)} custom-call(s32[1]{0:T(128)} %bitcast.index_ref, s32[16]{0:T(128)S(1)} %copy-done.1, bf16[2,8,6,64,512]{4,3,2,1,0:T(8,128)(2,1)S(1)} %bitcast_dynamic-update-slice_fusion.p_ref), custom_call_target="tpu_custom_call" | custom-call | flops 2717908992 | bytes 6291456 | tf_op jit(solution)/shard_map/pair_window/pallas_call | solution.py:548
  116.0 5.2 %row_mix.1 = bf16[4,512,768]{2,1,0:T(8,128)(2,1)} custom-call(s32[1]{0:T(128)} %bitcast.index_ref, s32[16]{0:T(128)S(1)} %copy-done.1, bf16[2,8,6,64,512]{4,3,2,1,0:T(8,128)(2,1)S(1)} %bitcast_dynamic-update-slice_fusion.p_ref, bf16[12,512,256]{2,1,0:T(8,128)(2,1)S(1)} %value_project.1.v_ref), custom_call_target="tpu_custom_call" | custom-call | flops 1610612736 | bytes 12582912 | tf_op jit(solution)/shard_map/row_mix/pallas_call | solution.py:251
  121.2 19.7 %contact_head.1 = f32[32,512]{1,0:T(8,128)} custom-call(s32[1]{0:T(128)} %bitcast.index_ref, bf16[12,48,512]{2,1,0:T(8,128)(2,1)S(1)} %pair_window.1.pf_ref, bf16[48,256]{1,0:T(8,128)(2,1)S(1)} %mul.28.pair_ref, bf16[2,3,384,256]{3,2,1,0:T(8,128)(2,1)S(1)} %copy-done.3, bf16[2,3,512,256]{3,2,1,0:T(8,128)(2,1)S(1)} %copy-done.2, ...), custom_call_target="tpu_custom_call" | custom-call | flops 5469372416 | bytes 4194304 | tf_op jit(solution)/shard_map/contact_head/pallas_call | solution.py:573
  (56 shorter events, 1.4 us)
Async XLA Ops:
  9.0 1.6 %copy-start = (bf16[4,512,768]{2,1,0:T(8,128)(2,1)}, bf16[4,512,768]{2,1,0:T(8,128)(2,1)S(1)}, u32[]{:S(2)}) copy-start(bf16[4,512,768]{2,1,0:T(8,128)(2,1)S(1)} %get-tuple-element.39.normed_ref) | copy-start | bytes 9437188
  10.6 6.0 %collective-permute-start = (bf16[2,6,512,256]{3,2,1,0:T(8,128)(2,1)}, bf16[2,6,512,256]{3,2,1,0:T(8,128)(2,1)S(1)}, u32[]{:S(2)}, u32[]{:S(2)}) collective-permute-start(bf16[2,6,512,256]{3,2,1,0:T(8,128)(2,1)} %get-tuple-element.27), channel_id=1, source_target_pairs={{0,1},{1,0},{2,3},{3,2},{4,5},{5,4},{6,7},{7,6},{8,9},{9,8},{10,11... | collective-permute-start | bytes 9437192 | tf_op jit(solution)/shard_map/ppermute | solution.py:285
  11.1 5.5 %copy-start.1 = (s32[16]{0:T(128)S(1)}, s32[16]{0:T(128)}, u32[]{:S(2)}) copy-start(s32[16]{0:T(128)} %constant.13.clone.table_ref) | copy-start | bytes 196
  20.9 8.2 %collective-permute-start.1 = (f16[6,32,512]{2,1,0:T(8,128)(2,1)S(1)}, f16[6,32,512]{2,1,0:T(8,128)(2,1)S(1)}, u32[]{:S(2)}, u32[]{:S(2)}) collective-permute-start(f16[6,32,512]{2,1,0:T(8,128)(2,1)S(1)} %get-tuple-element.63), channel_id=1, source_target_pairs={{0,2},{1,3},{2,6},{3,7},{6,10},{7,11},{10,14},{11,15},{14,12},{15,... | collective-permute-start | bytes 589832 | tf_op jit(solution)/shard_map/ppermute | solution.py:282
  23.9 6.7 %collective-permute-start.2 = (f16[6,32,512]{2,1,0:T(8,128)(2,1)S(1)}, f16[6,32,512]{2,1,0:T(8,128)(2,1)S(1)}, u32[]{:S(2)}, u32[]{:S(2)}) collective-permute-start(f16[6,32,512]{2,1,0:T(8,128)(2,1)S(1)} %get-tuple-element.62), channel_id=1, source_target_pairs={{0,4},{1,5},{2,0},{3,1},{6,2},{7,3},{10,6},{11,7},{14,10},{15,11},... | collective-permute-start | bytes 589832 | tf_op jit(solution)/shard_map/ppermute | solution.py:282
  30.7 38.3 %copy-start.5 = (bf16[64,12]{0,1:T(8,128)(2,1)S(1)}, bf16[64,12]{0,1:T(8,128)(2,1)}, u32[]{:S(2)}) copy-start(bf16[64,12]{0,1:T(8,128)(2,1)} %param.10) | copy-start | bytes 4612
  30.7 38.5 %copy-start.6 = (f32[64]{0:T(128)S(1)}, f32[64]{0:T(128)}, u32[]{:S(2)}) copy-start(f32[64]{0:T(128)} %param.12) | copy-start | bytes 772
  30.7 38.5 %copy-start.4 = (bf16[4,9,64,64]{3,2,1,0:T(8,128)(2,1)S(1)}, bf16[4,9,64,64]{3,2,1,0:T(8,128)(2,1)}, u32[]{:S(2)}) copy-start(bf16[4,9,64,64]{3,2,1,0:T(8,128)(2,1)} %param.11) | copy-start | bytes 884740
  30.7 7.9 %collective-permute-start.3 = (f16[6,32,512]{2,1,0:T(8,128)(2,1)S(1)}, f16[6,32,512]{2,1,0:T(8,128)(2,1)S(1)}, u32[]{:S(2)}, u32[]{:S(2)}) collective-permute-start(f16[6,32,512]{2,1,0:T(8,128)(2,1)S(1)} %get-tuple-element.59), channel_id=1, source_target_pairs={{0,2},{1,3},{2,6},{3,7},{6,10},{7,11},{10,14},{11,15},{14,12},{15,... | collective-permute-start | bytes 589832 | tf_op jit(solution)/shard_map/ppermute | solution.py:282
  32.3 7.6 %collective-permute-start.4 = (f16[6,32,512]{2,1,0:T(8,128)(2,1)S(1)}, f16[6,32,512]{2,1,0:T(8,128)(2,1)S(1)}, u32[]{:S(2)}, u32[]{:S(2)}) collective-permute-start(f16[6,32,512]{2,1,0:T(8,128)(2,1)S(1)} %get-tuple-element.58), channel_id=1, source_target_pairs={{0,4},{1,5},{2,0},{3,1},{6,2},{7,3},{10,6},{11,7},{14,10},{15,11},... | collective-permute-start | bytes 589832 | tf_op jit(solution)/shard_map/ppermute | solution.py:282
  32.8 10.0 %collective-permute-start.7 = (f16[6,32,512]{2,1,0:T(8,128)(2,1)S(1)}, f16[6,32,512]{2,1,0:T(8,128)(2,1)S(1)}, u32[]{:S(2)}, u32[]{:S(2)}) collective-permute-start(f16[6,32,512]{2,1,0:T(8,128)(2,1)S(1)} %get-tuple-element.61), channel_id=1, source_target_pairs={{0,2},{1,3},{2,6},{3,7},{6,10},{7,11},{10,14},{11,15},{14,12},{15,... | collective-permute-start | bytes 589832 | tf_op jit(solution)/shard_map/ppermute | solution.py:282
  34.4 9.8 %collective-permute-start.8 = (f16[6,32,512]{2,1,0:T(8,128)(2,1)S(1)}, f16[6,32,512]{2,1,0:T(8,128)(2,1)S(1)}, u32[]{:S(2)}, u32[]{:S(2)}) collective-permute-start(f16[6,32,512]{2,1,0:T(8,128)(2,1)S(1)} %get-tuple-element.60), channel_id=1, source_target_pairs={{0,4},{1,5},{2,0},{3,1},{6,2},{7,3},{10,6},{11,7},{14,10},{15,11},... | collective-permute-start | bytes 589832 | tf_op jit(solution)/shard_map/ppermute | solution.py:282
  40.1 7.0 %collective-permute-start.5 = (f16[6,32,512]{2,1,0:T(8,128)(2,1)S(1)}, f16[6,32,512]{2,1,0:T(8,128)(2,1)S(1)}, u32[]{:S(2)}, u32[]{:S(2)}) collective-permute-start(f16[6,32,512]{2,1,0:T(8,128)(2,1)S(1)} %get-tuple-element.57), channel_id=1, source_target_pairs={{0,2},{1,3},{2,6},{3,7},{6,10},{7,11},{10,14},{11,15},{14,12},{15,... | collective-permute-start | bytes 589832 | tf_op jit(solution)/shard_map/ppermute | solution.py:282
  41.7 6.7 %collective-permute-start.6 = (f16[6,32,512]{2,1,0:T(8,128)(2,1)S(1)}, f16[6,32,512]{2,1,0:T(8,128)(2,1)S(1)}, u32[]{:S(2)}, u32[]{:S(2)}) collective-permute-start(f16[6,32,512]{2,1,0:T(8,128)(2,1)S(1)} %get-tuple-element.56), channel_id=1, source_target_pairs={{0,4},{1,5},{2,0},{3,1},{6,2},{7,3},{10,6},{11,7},{14,10},{15,11},... | collective-permute-start | bytes 589832 | tf_op jit(solution)/shard_map/ppermute | solution.py:282
  44.3 5.7 %collective-permute-start.10 = (f16[6,32,512]{2,1,0:T(8,128)(2,1)S(1)}, f16[6,32,512]{2,1,0:T(8,128)(2,1)S(1)}, u32[]{:S(2)}, u32[]{:S(2)}) collective-permute-start(f16[6,32,512]{2,1,0:T(8,128)(2,1)S(1)} %get-tuple-element.55), channel_id=1, source_target_pairs={{0,2},{1,3},{2,6},{3,7},{6,10},{7,11},{10,14},{11,15},{14,12},{15,... | collective-permute-start | bytes 589832 | tf_op jit(solution)/shard_map/ppermute | solution.py:282
  45.9 7.2 %collective-permute-start.11 = (f16[6,32,512]{2,1,0:T(8,128)(2,1)S(1)}, f16[6,32,512]{2,1,0:T(8,128)(2,1)S(1)}, u32[]{:S(2)}, u32[]{:S(2)}) collective-permute-start(f16[6,32,512]{2,1,0:T(8,128)(2,1)S(1)} %get-tuple-element.54), channel_id=1, source_target_pairs={{0,4},{1,5},{2,0},{3,1},{6,2},{7,3},{10,6},{11,7},{14,10},{15,11},... | collective-permute-start | bytes 589832 | tf_op jit(solution)/shard_map/ppermute | solution.py:282
  53.2 5.7 %collective-permute-start.12 = (f16[6,32,512]{2,1,0:T(8,128)(2,1)S(1)}, f16[6,32,512]{2,1,0:T(8,128)(2,1)S(1)}, u32[]{:S(2)}, u32[]{:S(2)}) collective-permute-start(f16[6,32,512]{2,1,0:T(8,128)(2,1)S(1)} %fusion.12), channel_id=1, source_target_pairs={{0,4},{1,5},{2,0},{3,1},{6,2},{7,3},{10,6},{11,7},{14,10},{15,11},... | collective-permute-start | bytes 589832 | tf_op jit(solution)/shard_map/ppermute | solution.py:282
  53.7 6.8 %collective-permute-start.9 = (f16[6,32,512]{2,1,0:T(8,128)(2,1)S(1)}, f16[6,32,512]{2,1,0:T(8,128)(2,1)S(1)}, u32[]{:S(2)}, u32[]{:S(2)}) collective-permute-start(f16[6,32,512]{2,1,0:T(8,128)(2,1)S(1)} %get-tuple-element.52), channel_id=1, source_target_pairs={{0,2},{1,3},{2,6},{3,7},{6,10},{7,11},{10,14},{11,15},{14,12},{15,... | collective-permute-start | bytes 589832 | tf_op jit(solution)/shard_map/ppermute | solution.py:282
  55.3 7.3 %collective-permute-start.14 = (f16[6,32,512]{2,1,0:T(8,128)(2,1)S(1)}, f16[6,32,512]{2,1,0:T(8,128)(2,1)S(1)}, u32[]{:S(2)}, u32[]{:S(2)}) collective-permute-start(f16[6,32,512]{2,1,0:T(8,128)(2,1)S(1)} %get-tuple-element.53), channel_id=1, source_target_pairs={{0,4},{1,5},{2,0},{3,1},{6,2},{7,3},{10,6},{11,7},{14,10},{15,11},... | collective-permute-start | bytes 589832 | tf_op jit(solution)/shard_map/ppermute | solution.py:282
  60.7 5.7 %collective-permute-start.13 = (f16[6,32,512]{2,1,0:T(8,128)(2,1)S(1)}, f16[6,32,512]{2,1,0:T(8,128)(2,1)S(1)}, u32[]{:S(2)}, u32[]{:S(2)}) collective-permute-start(f16[6,32,512]{2,1,0:T(8,128)(2,1)S(1)} %get-tuple-element.51), channel_id=1, source_target_pairs={{0,2},{1,3},{2,6},{3,7},{6,10},{7,11},{10,14},{11,15},{14,12},{15,... | collective-permute-start | bytes 589832 | tf_op jit(solution)/shard_map/ppermute | solution.py:282
  66.8 15.7 %collective-permute-start.15 = (bf16[6,64,512]{2,1,0:T(8,128)(2,1)S(1)}, bf16[6,64,512]{2,1,0:T(8,128)(2,1)S(1)}, u32[]{:S(2)}, u32[]{:S(2)}) collective-permute-start(bf16[6,64,512]{2,1,0:T(8,128)(2,1)S(1)} %fusion.5), channel_id=1, source_target_pairs={{0,1},{1,0},{2,3},{3,2},{4,5},{5,4},{6,7},{7,6},{8,9},{9,8},{10,11... | collective-permute-start | bytes 1179656 | tf_op jit(solution)/shard_map/ppermute | solution.py:285
  66.9 12.3 %collective-permute-start.16 = (bf16[6,64,512]{2,1,0:T(8,128)(2,1)S(1)}, bf16[6,64,512]{2,1,0:T(8,128)(2,1)S(1)}, u32[]{:S(2)}, u32[]{:S(2)}) collective-permute-start(bf16[6,64,512]{2,1,0:T(8,128)(2,1)S(1)} %fusion.5), channel_id=1, source_target_pairs={{0,2},{1,3},{2,6},{3,7},{6,10},{7,11},{10,14},{11,15},{14,12},{15,... | collective-permute-start | bytes 1179656 | tf_op jit(solution)/shard_map/ppermute | solution.py:282
  68.8 11.2 %collective-permute-start.18 = (bf16[6,64,512]{2,1,0:T(8,128)(2,1)S(1)}, bf16[6,64,512]{2,1,0:T(8,128)(2,1)S(1)}, u32[]{:S(2)}, u32[]{:S(2)}) collective-permute-start(bf16[6,64,512]{2,1,0:T(8,128)(2,1)S(1)} %fusion.5), channel_id=1, source_target_pairs={{0,4},{1,5},{2,0},{3,1},{6,2},{7,3},{10,6},{11,7},{14,10},{15,11},... | collective-permute-start | bytes 1179656 | tf_op jit(solution)/shard_map/ppermute | solution.py:282
  80.0 10.4 %collective-permute-start.20 = (bf16[6,64,512]{2,1,0:T(8,128)(2,1)S(1)}, bf16[6,64,512]{2,1,0:T(8,128)(2,1)S(1)}, u32[]{:S(2)}, u32[]{:S(2)}) collective-permute-start(bf16[6,64,512]{2,1,0:T(8,128)(2,1)S(1)} %collective-permute-done.16), channel_id=1, source_target_pairs={{0,2},{1,3},{2,6},{3,7},{6,10},{7,11},{10,14},{11,15},{14,12},{15,... | collective-permute-start | bytes 1179656 | tf_op jit(solution)/shard_map/ppermute | solution.py:282
  81.1 10.6 %collective-permute-start.22 = (bf16[6,64,512]{2,1,0:T(8,128)(2,1)S(1)}, bf16[6,64,512]{2,1,0:T(8,128)(2,1)S(1)}, u32[]{:S(2)}, u32[]{:S(2)}) collective-permute-start(bf16[6,64,512]{2,1,0:T(8,128)(2,1)S(1)} %collective-permute-done.18), channel_id=1, source_target_pairs={{0,4},{1,5},{2,0},{3,1},{6,2},{7,3},{10,6},{11,7},{14,10},{15,11},... | collective-permute-start | bytes 1179656 | tf_op jit(solution)/shard_map/ppermute | solution.py:282
  82.0 11.8 %collective-permute-start.17 = (bf16[6,64,512]{2,1,0:T(8,128)(2,1)S(1)}, bf16[6,64,512]{2,1,0:T(8,128)(2,1)S(1)}, u32[]{:S(2)}, u32[]{:S(2)}) collective-permute-start(bf16[6,64,512]{2,1,0:T(8,128)(2,1)S(1)} %collective-permute-done.16), channel_id=1, source_target_pairs={{0,1},{1,0},{2,3},{3,2},{4,5},{5,4},{6,7},{7,6},{8,9},{9,8},{10,11... | collective-permute-start | bytes 1179656 | tf_op jit(solution)/shard_map/ppermute | solution.py:285
  82.0 12.3 %collective-permute-start.19 = (bf16[6,64,512]{2,1,0:T(8,128)(2,1)S(1)}, bf16[6,64,512]{2,1,0:T(8,128)(2,1)S(1)}, u32[]{:S(2)}, u32[]{:S(2)}) collective-permute-start(bf16[6,64,512]{2,1,0:T(8,128)(2,1)S(1)} %collective-permute-done.18), channel_id=1, source_target_pairs={{0,1},{1,0},{2,3},{3,2},{4,5},{5,4},{6,7},{7,6},{8,9},{9,8},{10,11... | collective-permute-start | bytes 1179656 | tf_op jit(solution)/shard_map/ppermute | solution.py:285
  91.7 9.7 %collective-permute-start.24 = (bf16[6,64,512]{2,1,0:T(8,128)(2,1)S(1)}, bf16[6,64,512]{2,1,0:T(8,128)(2,1)S(1)}, u32[]{:S(2)}, u32[]{:S(2)}) collective-permute-start(bf16[6,64,512]{2,1,0:T(8,128)(2,1)S(1)} %collective-permute-done.20), channel_id=1, source_target_pairs={{0,2},{1,3},{2,6},{3,7},{6,10},{7,11},{10,14},{11,15},{14,12},{15,... | collective-permute-start | bytes 1179656 | tf_op jit(solution)/shard_map/ppermute | solution.py:282
  92.4 9.8 %collective-permute-start.26 = (bf16[6,64,512]{2,1,0:T(8,128)(2,1)S(1)}, bf16[6,64,512]{2,1,0:T(8,128)(2,1)S(1)}, u32[]{:S(2)}, u32[]{:S(2)}) collective-permute-start(bf16[6,64,512]{2,1,0:T(8,128)(2,1)S(1)} %collective-permute-done.22), channel_id=1, source_target_pairs={{0,4},{1,5},{2,0},{3,1},{6,2},{7,3},{10,6},{11,7},{14,10},{15,11},... | collective-permute-start | bytes 1179656 | tf_op jit(solution)/shard_map/ppermute | solution.py:282
  93.7 10.0 %collective-permute-start.21 = (bf16[6,64,512]{2,1,0:T(8,128)(2,1)S(1)}, bf16[6,64,512]{2,1,0:T(8,128)(2,1)S(1)}, u32[]{:S(2)}, u32[]{:S(2)}) collective-permute-start(bf16[6,64,512]{2,1,0:T(8,128)(2,1)S(1)} %collective-permute-done.20), channel_id=1, source_target_pairs={{0,1},{1,0},{2,3},{3,2},{4,5},{5,4},{6,7},{7,6},{8,9},{9,8},{10,11... | collective-permute-start | bytes 1179656 | tf_op jit(solution)/shard_map/ppermute | solution.py:285
  93.8 10.6 %collective-permute-start.23 = (bf16[6,64,512]{2,1,0:T(8,128)(2,1)S(1)}, bf16[6,64,512]{2,1,0:T(8,128)(2,1)S(1)}, u32[]{:S(2)}, u32[]{:S(2)}) collective-permute-start(bf16[6,64,512]{2,1,0:T(8,128)(2,1)S(1)} %collective-permute-done.22), channel_id=1, source_target_pairs={{0,1},{1,0},{2,3},{3,2},{4,5},{5,4},{6,7},{7,6},{8,9},{9,8},{10,11... | collective-permute-start | bytes 1179656 | tf_op jit(solution)/shard_map/ppermute | solution.py:285
  101.5 5.7 %collective-permute-start.28 = (bf16[6,32,512]{2,1,0:T(8,128)(2,1)S(1)}, bf16[6,32,512]{2,1,0:T(8,128)(2,1)S(1)}, u32[]{:S(2)}, u32[]{:S(2)}) collective-permute-start(bf16[6,32,512]{2,1,0:T(8,128)(2,1)S(1)} %slice.92), channel_id=1, source_target_pairs={{0,2},{1,3},{2,6},{3,7},{6,10},{7,11},{10,14},{11,15},{14,12},{15,... | collective-permute-start | bytes 589832 | tf_op jit(solution)/shard_map/ppermute | solution.py:282
  102.2 5.9 %collective-permute-start.29 = (bf16[6,32,512]{2,1,0:T(8,128)(2,1)S(1)}, bf16[6,32,512]{2,1,0:T(8,128)(2,1)S(1)}, u32[]{:S(2)}, u32[]{:S(2)}) collective-permute-start(bf16[6,32,512]{2,1,0:T(8,128)(2,1)S(1)} %slice.93), channel_id=1, source_target_pairs={{0,4},{1,5},{2,0},{3,1},{6,2},{7,3},{10,6},{11,7},{14,10},{15,11},... | collective-permute-start | bytes 589832 | tf_op jit(solution)/shard_map/ppermute | solution.py:282
  103.8 4.4 %collective-permute-start.25 = (bf16[6,64,512]{2,1,0:T(8,128)(2,1)S(1)}, bf16[6,64,512]{2,1,0:T(8,128)(2,1)S(1)}, u32[]{:S(2)}, u32[]{:S(2)}) collective-permute-start(bf16[6,64,512]{2,1,0:T(8,128)(2,1)S(1)} %collective-permute-done.24), channel_id=1, source_target_pairs={{0,1},{1,0},{2,3},{3,2},{4,5},{5,4},{6,7},{7,6},{8,9},{9,8},{10,11... | collective-permute-start | bytes 1179656 | tf_op jit(solution)/shard_map/ppermute | solution.py:285
  103.8 4.5 %collective-permute-start.27 = (bf16[6,64,512]{2,1,0:T(8,128)(2,1)S(1)}, bf16[6,64,512]{2,1,0:T(8,128)(2,1)S(1)}, u32[]{:S(2)}, u32[]{:S(2)}) collective-permute-start(bf16[6,64,512]{2,1,0:T(8,128)(2,1)S(1)} %collective-permute-done.26), channel_id=1, source_target_pairs={{0,1},{1,0},{2,3},{3,2},{4,5},{5,4},{6,7},{7,6},{8,9},{9,8},{10,11... | collective-permute-start | bytes 1179656 | tf_op jit(solution)/shard_map/ppermute | solution.py:285
  108.2 1.8 %collective-permute-start.30 = (bf16[6,64,512]{2,1,0:T(8,128)(2,1)S(1)}, bf16[6,64,512]{2,1,0:T(8,128)(2,1)S(1)}, u32[]{:S(2)}, u32[]{:S(2)}) collective-permute-start(bf16[6,64,512]{2,1,0:T(8,128)(2,1)S(1)} %constant_dynamic-update-slice_fusion), channel_id=1, source_target_pairs={{0,1},{1,0},{2,3},{3,2},{4,5},{5,4},{6,7},{7,6},{8,9},{9,8},{10,11... | collective-permute-start | bytes 1179656 | tf_op jit(solution)/shard_map/ppermute | solution.py:285
  116.0 5.3 %copy-start.2 = (bf16[2,3,512,256]{3,2,1,0:T(8,128)(2,1)S(1)}, bf16[2,3,512,256]{3,2,1,0:T(8,128)(2,1)}, u32[]{:S(2)}) copy-start(bf16[2,3,512,256]{3,2,1,0:T(8,128)(2,1)} %get-tuple-element.49.far_ref) | copy-start | bytes 4718596
  116.0 5.3 %copy-start.3 = (bf16[2,3,384,256]{3,2,1,0:T(8,128)(2,1)S(1)}, bf16[2,3,384,256]{3,2,1,0:T(8,128)(2,1)}, u32[]{:S(2)}) copy-start(bf16[2,3,384,256]{3,2,1,0:T(8,128)(2,1)} %get-tuple-element.48.near_ref) | copy-start | bytes 3538948

commit v5 on v4

--- a/solution.py
+++ b/solution.py
@@ -383,6 +383,8 @@
     lane_row = lax.broadcasted_iota(jnp.int32, (1, lanes), 1) // size
 
     def masked(m, values):
+        if 2 <= m < blocks - 2:
+            return values
         row = index_ref[0] * o_ref.shape[0] + ROWS * (m - 2) + lane_row
         return jnp.where((row >= 0) & (row < residues), values, 0.0)
 
@@ -519,7 +521,7 @@
         want = jnp.where((row >= 0) & (row < residues), head * 2048 + row, -1)
         return jnp.where(want == have, 1.0, 0.0).astype(jnp.bfloat16)
 
-    step = 3 if blocks % 3 == 0 else 1
+    step = blocks
     for block in range(0, blocks, step):
         by_col = lax.dot_general(
             picks(wide, left, step * taken, block * taken),

time: 141 us -> 139 us (0.986)
  Pallas kernels: 55.3 us -> 52.9 us
    pallas_call x1, Pallas kernels: 5.99 us -> 3.67 us  [contact_head(): pl.pallas_call(window_kernel, out_shape=jax.ShapeDtypeStruct((blocks, ROW...]
  transfers between devices with their start and end apart: 31 -> 31, of which waited for: 21 -> 21; matrix products, arithmetic and copies ran while one was open for 2% -> 2% of each run, Pallas kernels for 9% -> 10%
where the time goes in v5:
time: 139 us
  Pallas kernels  52.9 us (38%)
  waiting for transfers between devices  51.4 us (37%)
  starting transfers between devices  26.3 us (19%)
  local copies, waits for them, and re-layouts  4.31 us (3%)
  other arithmetic  1.93 us (1%)
  between operations  1.65 us (1%)
    ppermute x22, waiting for transfers between devices, send(): return lax.ppermute(value, 'seq', pairs)  49.5 us
    ppermute x22, starting transfers between devices, send(): return lax.ppermute(value, 'seq', pairs)  24.2 us
    pallas_call x1, Pallas kernels, contact_call(): pl.pallas_call(contact_kernel, out_shape=jax.ShapeDtypeStruct((own_rows,...  19.6 us
    pallas_call x1, Pallas kernels, projections(): pl.pallas_call(norm_send_kernel, out_shape=(jax.ShapeDtypeStruct(alignmen...  7.74 us
    pallas_call x1, Pallas kernels, row_mix_of(): pl.pallas_call(mix_kernel, out_shape=jax.ShapeDtypeStruct((seqs, residues...  5.25 us
    pallas_call x1, Pallas kernels, value_projection(): pl.pallas_call(functools.partial(value_kernel, rows), out_shape=jax.Shape...  5.19 us
    pallas_call x1, Pallas kernels, projections(): pl.pallas_call(functools.partial(own_kernel, rows), out_shape=qk_shape, g...  5.18 us
    pallas_call x1, Pallas kernels, contact_head(): pl.pallas_call(window_kernel, out_shape=jax.ShapeDtypeStruct((blocks, ROW...  3.67 us
  transfers between devices with their start and end apart: 31, of which 21 were waited for; matrix products, arithmetic and copies ran while one was open for 2% of the time, Pallas kernels for 10%

profile of v5, /device:TPU:0, one launch (start us, length us, event | category | flops | bytes accessed | tf_op | source)
XLA Modules:
  0.0 138.5 jit_solution(3394384612829325728)
XLA Ops:
  1.3 7.7 %norm_send.1 = (bf16[4,512,768]{2,1,0:T(8,128)(2,1)S(1)}, bf16[2,6,512,256]{3,2,1,0:T(8,128)(2,1)}) custom-call(s32[1]{0:T(128)} %bitcast.index_ref, s32[1]{0:T(128)S(6)} %copy.26.depth_ref, bf16[4,512,768]{2,1,0:T(8,128)(2,1)} %x_ref.1, bf16[768,2304]{1,0:T(8,128)(2,1)} %w_ref.1, bf16[768,2304]{1,0:T(8,128)(2,1)} %w_ref.1), custom_call_target="tpu_custom_call" | custom-call | flops 2415919104 | bytes 10616832 | tf_op jit(solution)/shard_map/norm_send/pallas_call | solution.py:168
  9.0 1.6 %copy-done = bf16[4,512,768]{2,1,0:T(8,128)(2,1)} copy-done((bf16[4,512,768]{2,1,0:T(8,128)(2,1)}, bf16[4,512,768]{2,1,0:T(8,128)(2,1)S(1)}, u32[]{:S(2)}) %copy-start) | copy-done | bytes 3145752
  10.6 0.5 collective-permute-start
  11.1 5.2 %own_project.1.own_ref = bf16[2,6,512,256]{3,2,1,0:T(8,128)(2,1)S(1)} custom-call(s32[1]{0:T(128)} %bitcast.index_ref, s32[1]{0:T(128)S(6)} %copy.26.depth_ref, bf16[4,512,768]{2,1,0:T(8,128)(2,1)} %copy-done, bf16[768,2304]{1,0:T(8,128)(2,1)} %w_ref.1, bf16[768,2304]{1,0:T(8,128)(2,1)} %w_ref.1), custom_call_target="tpu_custom_call" | custom-call | flops 2415919104 | bytes 7471104 | tf_op jit(solution)/shard_map/own_project/pallas_call | solution.py:181
  16.3 0.3 collective-permute-done.other_ref
  16.6 3.4 %scores.1 = f32[8,6,64,512]{3,2,1,0:T(8,128)S(1)} custom-call(s32[1]{0:T(128)} %bitcast.index_ref, s32[16]{0:T(128)S(1)} %copy-done.1, s32[1]{0:T(128)S(6)} %copy.26.depth_ref, bf16[2,6,512,256]{3,2,1,0:T(8,128)(2,1)S(1)} %own_project.1.own_ref, bf16[2,6,512,256]{3,2,1,0:T(8,128)(2,1)S(1)} %collective-permute-done.other_ref), custom_call_target="tpu_custom_call" | custom-call | flops 1610612736 | bytes 12582912 | tf_op jit(solution)/shard_map/scores/pallas_call | solution.py:226
  20.0 0.7 convert.6
  20.7 0.2 slice_bitcast_fusion.12
  20.9 2.9 %collective-permute-start.1 = (f16[6,32,512]{2,1,0:T(8,128)(2,1)S(1)}, f16[6,32,512]{2,1,0:T(8,128)(2,1)S(1)}, u32[]{:S(2)}, u32[]{:S(2)}) collective-permute-start(f16[6,32,512]{2,1,0:T(8,128)(2,1)S(1)} %get-tuple-element.63), channel_id=1, source_target_pairs={{0,2},{1,3},{2,6},{3,7},{6,10},{7,11},{10,14},{11,15},{14,12},{15,... | collective-permute-start | bytes 589832 | tf_op jit(solution)/shard_map/ppermute | solution.py:282
  24.0 5.1 %collective-permute-done.1 = f16[6,32,512]{2,1,0:T(8,128)(2,1)S(1)} collective-permute-done((f16[6,32,512]{2,1,0:T(8,128)(2,1)S(1)}, f16[6,32,512]{2,1,0:T(8,128)(2,1)S(1)}, u32[]{:S(2)}, u32[]{:S(2)}) %collective-permute-start.1) | collective-permute-done | bytes 196640 | tf_op jit(solution)/shard_map/ppermute | solution.py:282
  29.1 1.4 %collective-permute-done.2 = f16[6,32,512]{2,1,0:T(8,128)(2,1)S(1)} collective-permute-done((f16[6,32,512]{2,1,0:T(8,128)(2,1)S(1)}, f16[6,32,512]{2,1,0:T(8,128)(2,1)S(1)}, u32[]{:S(2)}, u32[]{:S(2)}) %collective-permute-start.2) | collective-permute-done | bytes 196640 | tf_op jit(solution)/shard_map/ppermute | solution.py:282
  30.5 0.1 fusion.26
  30.7 1.6 %collective-permute-start.3 = (f16[6,32,512]{2,1,0:T(8,128)(2,1)S(1)}, f16[6,32,512]{2,1,0:T(8,128)(2,1)S(1)}, u32[]{:S(2)}, u32[]{:S(2)}) collective-permute-start(f16[6,32,512]{2,1,0:T(8,128)(2,1)S(1)} %get-tuple-element.59), channel_id=1, source_target_pairs={{0,2},{1,3},{2,6},{3,7},{6,10},{7,11},{10,14},{11,15},{14,12},{15,... | collective-permute-start | bytes 589832 | tf_op jit(solution)/shard_map/ppermute | solution.py:282
  32.3 0.5 collective-permute-start.4
  32.8 1.6 %collective-permute-start.7 = (f16[6,32,512]{2,1,0:T(8,128)(2,1)S(1)}, f16[6,32,512]{2,1,0:T(8,128)(2,1)S(1)}, u32[]{:S(2)}, u32[]{:S(2)}) collective-permute-start(f16[6,32,512]{2,1,0:T(8,128)(2,1)S(1)} %get-tuple-element.61), channel_id=1, source_target_pairs={{0,2},{1,3},{2,6},{3,7},{6,10},{7,11},{10,14},{11,15},{14,12},{15,... | collective-permute-start | bytes 589832 | tf_op jit(solution)/shard_map/ppermute | solution.py:282
  34.4 0.5 collective-permute-start.8
  34.8 3.8 %collective-permute-done.3 = f16[6,32,512]{2,1,0:T(8,128)(2,1)S(1)} collective-permute-done((f16[6,32,512]{2,1,0:T(8,128)(2,1)S(1)}, f16[6,32,512]{2,1,0:T(8,128)(2,1)S(1)}, u32[]{:S(2)}, u32[]{:S(2)}) %collective-permute-start.3) | collective-permute-done | bytes 196640 | tf_op jit(solution)/shard_map/ppermute | solution.py:282
  38.6 1.3 collective-permute-done.4
  39.9 0.1 fusion.22
  40.1 1.6 %collective-permute-start.5 = (f16[6,32,512]{2,1,0:T(8,128)(2,1)S(1)}, f16[6,32,512]{2,1,0:T(8,128)(2,1)S(1)}, u32[]{:S(2)}, u32[]{:S(2)}) collective-permute-start(f16[6,32,512]{2,1,0:T(8,128)(2,1)S(1)} %get-tuple-element.57), channel_id=1, source_target_pairs={{0,2},{1,3},{2,6},{3,7},{6,10},{7,11},{10,14},{11,15},{14,12},{15,... | collective-permute-start | bytes 589832 | tf_op jit(solution)/shard_map/ppermute | solution.py:282
  41.7 0.4 collective-permute-start.6
  42.2 0.7 collective-permute-done.7
  42.8 1.3 collective-permute-done.8
  44.1 0.1 fusion.18
  44.3 1.6 %collective-permute-start.10 = (f16[6,32,512]{2,1,0:T(8,128)(2,1)S(1)}, f16[6,32,512]{2,1,0:T(8,128)(2,1)S(1)}, u32[]{:S(2)}, u32[]{:S(2)}) collective-permute-start(f16[6,32,512]{2,1,0:T(8,128)(2,1)S(1)} %get-tuple-element.55), channel_id=1, source_target_pairs={{0,2},{1,3},{2,6},{3,7},{6,10},{7,11},{10,14},{11,15},{14,12},{15,... | collective-permute-start | bytes 589832 | tf_op jit(solution)/shard_map/ppermute | solution.py:282
  45.9 0.5 collective-permute-start.11
  46.3 0.8 collective-permute-done.5
  47.1 1.3 collective-permute-done.6
  48.5 1.5 %collective-permute-done.10 = f16[6,32,512]{2,1,0:T(8,128)(2,1)S(1)} collective-permute-done((f16[6,32,512]{2,1,0:T(8,128)(2,1)S(1)}, f16[6,32,512]{2,1,0:T(8,128)(2,1)S(1)}, u32[]{:S(2)}, u32[]{:S(2)}) %collective-permute-start.10) | collective-permute-done | bytes 196640 | tf_op jit(solution)/shard_map/ppermute | solution.py:282
  50.0 3.1 %collective-permute-done.11 = f16[6,32,512]{2,1,0:T(8,128)(2,1)S(1)} collective-permute-done((f16[6,32,512]{2,1,0:T(8,128)(2,1)S(1)}, f16[6,32,512]{2,1,0:T(8,128)(2,1)S(1)}, u32[]{:S(2)}, u32[]{:S(2)}) %collective-permute-start.11) | collective-permute-done | bytes 196640 | tf_op jit(solution)/shard_map/ppermute | solution.py:282
  53.2 0.5 collective-permute-start.12
  53.7 1.6 %collective-permute-start.9 = (f16[6,32,512]{2,1,0:T(8,128)(2,1)S(1)}, f16[6,32,512]{2,1,0:T(8,128)(2,1)S(1)}, u32[]{:S(2)}, u32[]{:S(2)}) collective-permute-start(f16[6,32,512]{2,1,0:T(8,128)(2,1)S(1)} %get-tuple-element.52), channel_id=1, source_target_pairs={{0,2},{1,3},{2,6},{3,7},{6,10},{7,11},{10,14},{11,15},{14,12},{15,... | collective-permute-start | bytes 589832 | tf_op jit(solution)/shard_map/ppermute | solution.py:282
  55.3 0.4 collective-permute-start.14
  55.7 3.2 %collective-permute-done.12 = f16[6,32,512]{2,1,0:T(8,128)(2,1)S(1)} collective-permute-done((f16[6,32,512]{2,1,0:T(8,128)(2,1)S(1)}, f16[6,32,512]{2,1,0:T(8,128)(2,1)S(1)}, u32[]{:S(2)}, u32[]{:S(2)}) %collective-permute-start.12) | collective-permute-done | bytes 196640 | tf_op jit(solution)/shard_map/ppermute | solution.py:282
  58.9 1.6 %collective-permute-done.9 = f16[6,32,512]{2,1,0:T(8,128)(2,1)S(1)} collective-permute-done((f16[6,32,512]{2,1,0:T(8,128)(2,1)S(1)}, f16[6,32,512]{2,1,0:T(8,128)(2,1)S(1)}, u32[]{:S(2)}, u32[]{:S(2)}) %collective-permute-start.9) | collective-permute-done | bytes 196640 | tf_op jit(solution)/shard_map/ppermute | solution.py:282
  60.5 0.2 fusion.30
  60.7 1.9 %collective-permute-start.13 = (f16[6,32,512]{2,1,0:T(8,128)(2,1)S(1)}, f16[6,32,512]{2,1,0:T(8,128)(2,1)S(1)}, u32[]{:S(2)}, u32[]{:S(2)}) collective-permute-start(f16[6,32,512]{2,1,0:T(8,128)(2,1)S(1)} %get-tuple-element.51), channel_id=1, source_target_pairs={{0,2},{1,3},{2,6},{3,7},{6,10},{7,11},{10,14},{11,15},{14,12},{15,... | collective-permute-start | bytes 589832 | tf_op jit(solution)/shard_map/ppermute | solution.py:282
  62.6 3.8 %collective-permute-done.13 = f16[6,32,512]{2,1,0:T(8,128)(2,1)S(1)} collective-permute-done((f16[6,32,512]{2,1,0:T(8,128)(2,1)S(1)}, f16[6,32,512]{2,1,0:T(8,128)(2,1)S(1)}, u32[]{:S(2)}, u32[]{:S(2)}) %collective-permute-start.13) | collective-permute-done | bytes 196640 | tf_op jit(solution)/shard_map/ppermute | solution.py:282
  66.5 0.3 fusion.5
  66.9 1.9 %collective-permute-start.16 = (bf16[6,64,512]{2,1,0:T(8,128)(2,1)S(1)}, bf16[6,64,512]{2,1,0:T(8,128)(2,1)S(1)}, u32[]{:S(2)}, u32[]{:S(2)}) collective-permute-start(bf16[6,64,512]{2,1,0:T(8,128)(2,1)S(1)} %fusion.5), channel_id=1, source_target_pairs={{0,2},{1,3},{2,6},{3,7},{6,10},{7,11},{10,14},{11,15},{14,12},{15,... | collective-permute-start | bytes 1179656 | tf_op jit(solution)/shard_map/ppermute | solution.py:282
  68.8 0.2 collective-permute-start.18
  69.2 1.0 copy.9
  70.3 2.9 %spread_taps.1 = (bf16[2,3,384,256]{3,2,1,0:T(8,128)(2,1)}, bf16[2,3,512,256]{3,2,1,0:T(8,128)(2,1)}) custom-call(bf16[36,64,64]{2,1,0:T(8,128)(2,1)} %bitcast.115), custom_call_target="tpu_custom_call" | custom-call | bytes 6291456 | tf_op jit(solution)/shard_map/spread_taps/pallas_call | solution.py:471
  73.2 0.8 dynamic_update_slice.48
  74.0 5.2 %value_project.1.v_ref = bf16[12,512,256]{2,1,0:T(8,128)(2,1)S(1)} custom-call(bf16[4,512,768]{2,1,0:T(8,128)(2,1)} %copy-done, bf16[768,2304]{1,0:T(8,128)(2,1)} %w_ref.1), custom_call_target="tpu_custom_call" | custom-call | flops 2415919104 | bytes 7471104 | tf_op jit(solution)/shard_map/value_project/pallas_call | solution.py:206
  79.2 0.8 collective-permute-done.18
  80.0 1.1 collective-permute-start.20
  81.1 0.9 collective-permute-start.22
  82.0 0.5 collective-permute-start.19
  82.6 7.7 %collective-permute-done.20 = bf16[6,64,512]{2,1,0:T(8,128)(2,1)S(1)} collective-permute-done((bf16[6,64,512]{2,1,0:T(8,128)(2,1)S(1)}, bf16[6,64,512]{2,1,0:T(8,128)(2,1)S(1)}, u32[]{:S(2)}, u32[]{:S(2)}) %collective-permute-start.20) | collective-permute-done | bytes 393248 | tf_op jit(solution)/shard_map/ppermute | solution.py:282
  90.3 1.4 %collective-permute-done.22 = bf16[6,64,512]{2,1,0:T(8,128)(2,1)S(1)} collective-permute-done((bf16[6,64,512]{2,1,0:T(8,128)(2,1)S(1)}, bf16[6,64,512]{2,1,0:T(8,128)(2,1)S(1)}, u32[]{:S(2)}, u32[]{:S(2)}) %collective-permute-start.22) | collective-permute-done | bytes 393248 | tf_op jit(solution)/shard_map/ppermute | solution.py:282
  91.7 0.7 collective-permute-start.24
  92.4 1.3 collective-permute-start.26
  93.8 0.5 collective-permute-start.23
  94.4 7.0 %collective-permute-done.24 = bf16[6,64,512]{2,1,0:T(8,128)(2,1)S(1)} collective-permute-done((bf16[6,64,512]{2,1,0:T(8,128)(2,1)S(1)}, bf16[6,64,512]{2,1,0:T(8,128)(2,1)S(1)}, u32[]{:S(2)}, u32[]{:S(2)}) %collective-permute-start.24) | collective-permute-done | bytes 393248 | tf_op jit(solution)/shard_map/ppermute | solution.py:282
  101.5 0.8 collective-permute-start.28
  102.2 1.6 %collective-permute-start.29 = (bf16[6,32,512]{2,1,0:T(8,128)(2,1)S(1)}, bf16[6,32,512]{2,1,0:T(8,128)(2,1)S(1)}, u32[]{:S(2)}, u32[]{:S(2)}) collective-permute-start(bf16[6,32,512]{2,1,0:T(8,128)(2,1)S(1)} %slice.93), channel_id=1, source_target_pairs={{0,4},{1,5},{2,0},{3,1},{6,2},{7,3},{10,6},{11,7},{14,10},{15,11},... | collective-permute-start | bytes 589832 | tf_op jit(solution)/shard_map/ppermute | solution.py:282
  103.8 0.5 collective-permute-start.27
  104.5 2.7 %collective-permute-done.28 = bf16[6,32,512]{2,1,0:T(8,128)(2,1)S(1)} collective-permute-done((bf16[6,32,512]{2,1,0:T(8,128)(2,1)S(1)}, bf16[6,32,512]{2,1,0:T(8,128)(2,1)S(1)}, u32[]{:S(2)}, u32[]{:S(2)}) %collective-permute-start.28) | collective-permute-done | bytes 196640 | tf_op jit(solution)/shard_map/ppermute | solution.py:282
  107.2 0.9 collective-permute-done.29
  108.4 1.5 %collective-permute-done.30 = bf16[6,64,512]{2,1,0:T(8,128)(2,1)S(1)} collective-permute-done((bf16[6,64,512]{2,1,0:T(8,128)(2,1)S(1)}, bf16[6,64,512]{2,1,0:T(8,128)(2,1)S(1)}, u32[]{:S(2)}, u32[]{:S(2)}) %collective-permute-start.30) | collective-permute-done | bytes 393248 | tf_op jit(solution)/shard_map/ppermute | solution.py:285
  110.0 3.7 %pair_window.1.pf_ref = bf16[12,48,512]{2,1,0:T(8,128)(2,1)S(1)} custom-call(s32[1]{0:T(128)} %bitcast.index_ref, s32[16]{0:T(128)S(1)} %copy-done.1, bf16[2,8,6,64,512]{4,3,2,1,0:T(8,128)(2,1)S(1)} %bitcast_dynamic-update-slice_fusion.p_ref), custom_call_target="tpu_custom_call" | custom-call | flops 2717908992 | bytes 6291456 | tf_op jit(solution)/shard_map/pair_window/pallas_call | solution.py:550
  113.7 5.2 %row_mix.1 = bf16[4,512,768]{2,1,0:T(8,128)(2,1)} custom-call(s32[1]{0:T(128)} %bitcast.index_ref, s32[16]{0:T(128)S(1)} %copy-done.1, bf16[2,8,6,64,512]{4,3,2,1,0:T(8,128)(2,1)S(1)} %bitcast_dynamic-update-slice_fusion.p_ref, bf16[12,512,256]{2,1,0:T(8,128)(2,1)S(1)} %value_project.1.v_ref), custom_call_target="tpu_custom_call" | custom-call | flops 1610612736 | bytes 12582912 | tf_op jit(solution)/shard_map/row_mix/pallas_call | solution.py:251
  118.9 19.6 %contact_head.1 = f32[32,512]{1,0:T(8,128)} custom-call(s32[1]{0:T(128)} %bitcast.index_ref, bf16[12,48,512]{2,1,0:T(8,128)(2,1)S(1)} %pair_window.1.pf_ref, bf16[48,256]{1,0:T(8,128)(2,1)S(1)} %mul.28.pair_ref, bf16[2,3,384,256]{3,2,1,0:T(8,128)(2,1)S(1)} %copy-done.3, bf16[2,3,512,256]{3,2,1,0:T(8,128)(2,1)S(1)} %copy-done.2, ...), custom_call_target="tpu_custom_call" | custom-call | flops 5469372416 | bytes 4194304 | tf_op jit(solution)/shard_map/contact_head/pallas_call | solution.py:575
  (56 shorter events, 1.3 us)
Async XLA Ops:
  9.0 1.6 %copy-start = (bf16[4,512,768]{2,1,0:T(8,128)(2,1)}, bf16[4,512,768]{2,1,0:T(8,128)(2,1)S(1)}, u32[]{:S(2)}) copy-start(bf16[4,512,768]{2,1,0:T(8,128)(2,1)S(1)} %get-tuple-element.39.normed_ref) | copy-start | bytes 9437188
  10.6 6.0 %collective-permute-start = (bf16[2,6,512,256]{3,2,1,0:T(8,128)(2,1)}, bf16[2,6,512,256]{3,2,1,0:T(8,128)(2,1)S(1)}, u32[]{:S(2)}, u32[]{:S(2)}) collective-permute-start(bf16[2,6,512,256]{3,2,1,0:T(8,128)(2,1)} %get-tuple-element.27), channel_id=1, source_target_pairs={{0,1},{1,0},{2,3},{3,2},{4,5},{5,4},{6,7},{7,6},{8,9},{9,8},{10,11... | collective-permute-start | bytes 9437192 | tf_op jit(solution)/shard_map/ppermute | solution.py:285
  11.1 5.5 %copy-start.1 = (s32[16]{0:T(128)S(1)}, s32[16]{0:T(128)}, u32[]{:S(2)}) copy-start(s32[16]{0:T(128)} %constant.13.clone.table_ref) | copy-start | bytes 196
  20.9 8.2 %collective-permute-start.1 = (f16[6,32,512]{2,1,0:T(8,128)(2,1)S(1)}, f16[6,32,512]{2,1,0:T(8,128)(2,1)S(1)}, u32[]{:S(2)}, u32[]{:S(2)}) collective-permute-start(f16[6,32,512]{2,1,0:T(8,128)(2,1)S(1)} %get-tuple-element.63), channel_id=1, source_target_pairs={{0,2},{1,3},{2,6},{3,7},{6,10},{7,11},{10,14},{11,15},{14,12},{15,... | collective-permute-start | bytes 589832 | tf_op jit(solution)/shard_map/ppermute | solution.py:282
  23.9 6.7 %collective-permute-start.2 = (f16[6,32,512]{2,1,0:T(8,128)(2,1)S(1)}, f16[6,32,512]{2,1,0:T(8,128)(2,1)S(1)}, u32[]{:S(2)}, u32[]{:S(2)}) collective-permute-start(f16[6,32,512]{2,1,0:T(8,128)(2,1)S(1)} %get-tuple-element.62), channel_id=1, source_target_pairs={{0,4},{1,5},{2,0},{3,1},{6,2},{7,3},{10,6},{11,7},{14,10},{15,11},... | collective-permute-start | bytes 589832 | tf_op jit(solution)/shard_map/ppermute | solution.py:282
  30.7 38.3 %copy-start.5 = (bf16[64,12]{0,1:T(8,128)(2,1)S(1)}, bf16[64,12]{0,1:T(8,128)(2,1)}, u32[]{:S(2)}) copy-start(bf16[64,12]{0,1:T(8,128)(2,1)} %param.10) | copy-start | bytes 4612
  30.7 38.5 %copy-start.6 = (f32[64]{0:T(128)S(1)}, f32[64]{0:T(128)}, u32[]{:S(2)}) copy-start(f32[64]{0:T(128)} %param.12) | copy-start | bytes 772
  30.7 38.5 %copy-start.4 = (bf16[4,9,64,64]{3,2,1,0:T(8,128)(2,1)S(1)}, bf16[4,9,64,64]{3,2,1,0:T(8,128)(2,1)}, u32[]{:S(2)}) copy-start(bf16[4,9,64,64]{3,2,1,0:T(8,128)(2,1)} %param.11) | copy-start | bytes 884740
  30.7 7.9 %collective-permute-start.3 = (f16[6,32,512]{2,1,0:T(8,128)(2,1)S(1)}, f16[6,32,512]{2,1,0:T(8,128)(2,1)S(1)}, u32[]{:S(2)}, u32[]{:S(2)}) collective-permute-start(f16[6,32,512]{2,1,0:T(8,128)(2,1)S(1)} %get-tuple-element.59), channel_id=1, source_target_pairs={{0,2},{1,3},{2,6},{3,7},{6,10},{7,11},{10,14},{11,15},{14,12},{15,... | collective-permute-start | bytes 589832 | tf_op jit(solution)/shard_map/ppermute | solution.py:282
  32.3 7.6 %collective-permute-start.4 = (f16[6,32,512]{2,1,0:T(8,128)(2,1)S(1)}, f16[6,32,512]{2,1,0:T(8,128)(2,1)S(1)}, u32[]{:S(2)}, u32[]{:S(2)}) collective-permute-start(f16[6,32,512]{2,1,0:T(8,128)(2,1)S(1)} %get-tuple-element.58), channel_id=1, source_target_pairs={{0,4},{1,5},{2,0},{3,1},{6,2},{7,3},{10,6},{11,7},{14,10},{15,11},... | collective-permute-start | bytes 589832 | tf_op jit(solution)/shard_map/ppermute | solution.py:282
  32.8 10.0 %collective-permute-start.7 = (f16[6,32,512]{2,1,0:T(8,128)(2,1)S(1)}, f16[6,32,512]{2,1,0:T(8,128)(2,1)S(1)}, u32[]{:S(2)}, u32[]{:S(2)}) collective-permute-start(f16[6,32,512]{2,1,0:T(8,128)(2,1)S(1)} %get-tuple-element.61), channel_id=1, source_target_pairs={{0,2},{1,3},{2,6},{3,7},{6,10},{7,11},{10,14},{11,15},{14,12},{15,... | collective-permute-start | bytes 589832 | tf_op jit(solution)/shard_map/ppermute | solution.py:282
  34.4 9.8 %collective-permute-start.8 = (f16[6,32,512]{2,1,0:T(8,128)(2,1)S(1)}, f16[6,32,512]{2,1,0:T(8,128)(2,1)S(1)}, u32[]{:S(2)}, u32[]{:S(2)}) collective-permute-start(f16[6,32,512]{2,1,0:T(8,128)(2,1)S(1)} %get-tuple-element.60), channel_id=1, source_target_pairs={{0,4},{1,5},{2,0},{3,1},{6,2},{7,3},{10,6},{11,7},{14,10},{15,11},... | collective-permute-start | bytes 589832 | tf_op jit(solution)/shard_map/ppermute | solution.py:282
  40.1 7.0 %collective-permute-start.5 = (f16[6,32,512]{2,1,0:T(8,128)(2,1)S(1)}, f16[6,32,512]{2,1,0:T(8,128)(2,1)S(1)}, u32[]{:S(2)}, u32[]{:S(2)}) collective-permute-start(f16[6,32,512]{2,1,0:T(8,128)(2,1)S(1)} %get-tuple-element.57), channel_id=1, source_target_pairs={{0,2},{1,3},{2,6},{3,7},{6,10},{7,11},{10,14},{11,15},{14,12},{15,... | collective-permute-start | bytes 589832 | tf_op jit(solution)/shard_map/ppermute | solution.py:282
  41.7 6.7 %collective-permute-start.6 = (f16[6,32,512]{2,1,0:T(8,128)(2,1)S(1)}, f16[6,32,512]{2,1,0:T(8,128)(2,1)S(1)}, u32[]{:S(2)}, u32[]{:S(2)}) collective-permute-start(f16[6,32,512]{2,1,0:T(8,128)(2,1)S(1)} %get-tuple-element.56), channel_id=1, source_target_pairs={{0,4},{1,5},{2,0},{3,1},{6,2},{7,3},{10,6},{11,7},{14,10},{15,11},... | collective-permute-start | bytes 589832 | tf_op jit(solution)/shard_map/ppermute | solution.py:282
  44.3 5.7 %collective-permute-start.10 = (f16[6,32,512]{2,1,0:T(8,128)(2,1)S(1)}, f16[6,32,512]{2,1,0:T(8,128)(2,1)S(1)}, u32[]{:S(2)}, u32[]{:S(2)}) collective-permute-start(f16[6,32,512]{2,1,0:T(8,128)(2,1)S(1)} %get-tuple-element.55), channel_id=1, source_target_pairs={{0,2},{1,3},{2,6},{3,7},{6,10},{7,11},{10,14},{11,15},{14,12},{15,... | collective-permute-start | bytes 589832 | tf_op jit(solution)/shard_map/ppermute | solution.py:282
  45.9 7.2 %collective-permute-start.11 = (f16[6,32,512]{2,1,0:T(8,128)(2,1)S(1)}, f16[6,32,512]{2,1,0:T(8,128)(2,1)S(1)}, u32[]{:S(2)}, u32[]{:S(2)}) collective-permute-start(f16[6,32,512]{2,1,0:T(8,128)(2,1)S(1)} %get-tuple-element.54), channel_id=1, source_target_pairs={{0,4},{1,5},{2,0},{3,1},{6,2},{7,3},{10,6},{11,7},{14,10},{15,11},... | collective-permute-start | bytes 589832 | tf_op jit(solution)/shard_map/ppermute | solution.py:282
  53.2 5.7 %collective-permute-start.12 = (f16[6,32,512]{2,1,0:T(8,128)(2,1)S(1)}, f16[6,32,512]{2,1,0:T(8,128)(2,1)S(1)}, u32[]{:S(2)}, u32[]{:S(2)}) collective-permute-start(f16[6,32,512]{2,1,0:T(8,128)(2,1)S(1)} %fusion.12), channel_id=1, source_target_pairs={{0,4},{1,5},{2,0},{3,1},{6,2},{7,3},{10,6},{11,7},{14,10},{15,11},... | collective-permute-start | bytes 589832 | tf_op jit(solution)/shard_map/ppermute | solution.py:282
  53.7 6.8 %collective-permute-start.9 = (f16[6,32,512]{2,1,0:T(8,128)(2,1)S(1)}, f16[6,32,512]{2,1,0:T(8,128)(2,1)S(1)}, u32[]{:S(2)}, u32[]{:S(2)}) collective-permute-start(f16[6,32,512]{2,1,0:T(8,128)(2,1)S(1)} %get-tuple-element.52), channel_id=1, source_target_pairs={{0,2},{1,3},{2,6},{3,7},{6,10},{7,11},{10,14},{11,15},{14,12},{15,... | collective-permute-start | bytes 589832 | tf_op jit(solution)/shard_map/ppermute | solution.py:282
  55.3 7.3 %collective-permute-start.14 = (f16[6,32,512]{2,1,0:T(8,128)(2,1)S(1)}, f16[6,32,512]{2,1,0:T(8,128)(2,1)S(1)}, u32[]{:S(2)}, u32[]{:S(2)}) collective-permute-start(f16[6,32,512]{2,1,0:T(8,128)(2,1)S(1)} %get-tuple-element.53), channel_id=1, source_target_pairs={{0,4},{1,5},{2,0},{3,1},{6,2},{7,3},{10,6},{11,7},{14,10},{15,11},... | collective-permute-start | bytes 589832 | tf_op jit(solution)/shard_map/ppermute | solution.py:282
  60.7 5.7 %collective-permute-start.13 = (f16[6,32,512]{2,1,0:T(8,128)(2,1)S(1)}, f16[6,32,512]{2,1,0:T(8,128)(2,1)S(1)}, u32[]{:S(2)}, u32[]{:S(2)}) collective-permute-start(f16[6,32,512]{2,1,0:T(8,128)(2,1)S(1)} %get-tuple-element.51), channel_id=1, source_target_pairs={{0,2},{1,3},{2,6},{3,7},{6,10},{7,11},{10,14},{11,15},{14,12},{15,... | collective-permute-start | bytes 589832 | tf_op jit(solution)/shard_map/ppermute | solution.py:282
  66.8 15.7 %collective-permute-start.15 = (bf16[6,64,512]{2,1,0:T(8,128)(2,1)S(1)}, bf16[6,64,512]{2,1,0:T(8,128)(2,1)S(1)}, u32[]{:S(2)}, u32[]{:S(2)}) collective-permute-start(bf16[6,64,512]{2,1,0:T(8,128)(2,1)S(1)} %fusion.5), channel_id=1, source_target_pairs={{0,1},{1,0},{2,3},{3,2},{4,5},{5,4},{6,7},{7,6},{8,9},{9,8},{10,11... | collective-permute-start | bytes 1179656 | tf_op jit(solution)/shard_map/ppermute | solution.py:285
  66.9 12.3 %collective-permute-start.16 = (bf16[6,64,512]{2,1,0:T(8,128)(2,1)S(1)}, bf16[6,64,512]{2,1,0:T(8,128)(2,1)S(1)}, u32[]{:S(2)}, u32[]{:S(2)}) collective-permute-start(bf16[6,64,512]{2,1,0:T(8,128)(2,1)S(1)} %fusion.5), channel_id=1, source_target_pairs={{0,2},{1,3},{2,6},{3,7},{6,10},{7,11},{10,14},{11,15},{14,12},{15,... | collective-permute-start | bytes 1179656 | tf_op jit(solution)/shard_map/ppermute | solution.py:282
  68.8 11.2 %collective-permute-start.18 = (bf16[6,64,512]{2,1,0:T(8,128)(2,1)S(1)}, bf16[6,64,512]{2,1,0:T(8,128)(2,1)S(1)}, u32[]{:S(2)}, u32[]{:S(2)}) collective-permute-start(bf16[6,64,512]{2,1,0:T(8,128)(2,1)S(1)} %fusion.5), channel_id=1, source_target_pairs={{0,4},{1,5},{2,0},{3,1},{6,2},{7,3},{10,6},{11,7},{14,10},{15,11},... | collective-permute-start | bytes 1179656 | tf_op jit(solution)/shard_map/ppermute | solution.py:282
  80.0 10.4 %collective-permute-start.20 = (bf16[6,64,512]{2,1,0:T(8,128)(2,1)S(1)}, bf16[6,64,512]{2,1,0:T(8,128)(2,1)S(1)}, u32[]{:S(2)}, u32[]{:S(2)}) collective-permute-start(bf16[6,64,512]{2,1,0:T(8,128)(2,1)S(1)} %collective-permute-done.16), channel_id=1, source_target_pairs={{0,2},{1,3},{2,6},{3,7},{6,10},{7,11},{10,14},{11,15},{14,12},{15,... | collective-permute-start | bytes 1179656 | tf_op jit(solution)/shard_map/ppermute | solution.py:282
  81.1 10.6 %collective-permute-start.22 = (bf16[6,64,512]{2,1,0:T(8,128)(2,1)S(1)}, bf16[6,64,512]{2,1,0:T(8,128)(2,1)S(1)}, u32[]{:S(2)}, u32[]{:S(2)}) collective-permute-start(bf16[6,64,512]{2,1,0:T(8,128)(2,1)S(1)} %collective-permute-done.18), channel_id=1, source_target_pairs={{0,4},{1,5},{2,0},{3,1},{6,2},{7,3},{10,6},{11,7},{14,10},{15,11},... | collective-permute-start | bytes 1179656 | tf_op jit(solution)/shard_map/ppermute | solution.py:282
  82.0 11.8 %collective-permute-start.17 = (bf16[6,64,512]{2,1,0:T(8,128)(2,1)S(1)}, bf16[6,64,512]{2,1,0:T(8,128)(2,1)S(1)}, u32[]{:S(2)}, u32[]{:S(2)}) collective-permute-start(bf16[6,64,512]{2,1,0:T(8,128)(2,1)S(1)} %collective-permute-done.16), channel_id=1, source_target_pairs={{0,1},{1,0},{2,3},{3,2},{4,5},{5,4},{6,7},{7,6},{8,9},{9,8},{10,11... | collective-permute-start | bytes 1179656 | tf_op jit(solution)/shard_map/ppermute | solution.py:285
  82.0 12.3 %collective-permute-start.19 = (bf16[6,64,512]{2,1,0:T(8,128)(2,1)S(1)}, bf16[6,64,512]{2,1,0:T(8,128)(2,1)S(1)}, u32[]{:S(2)}, u32[]{:S(2)}) collective-permute-start(bf16[6,64,512]{2,1,0:T(8,128)(2,1)S(1)} %collective-permute-done.18), channel_id=1, source_target_pairs={{0,1},{1,0},{2,3},{3,2},{4,5},{5,4},{6,7},{7,6},{8,9},{9,8},{10,11... | collective-permute-start | bytes 1179656 | tf_op jit(solution)/shard_map/ppermute | solution.py:285
  91.7 9.7 %collective-permute-start.24 = (bf16[6,64,512]{2,1,0:T(8,128)(2,1)S(1)}, bf16[6,64,512]{2,1,0:T(8,128)(2,1)S(1)}, u32[]{:S(2)}, u32[]{:S(2)}) collective-permute-start(bf16[6,64,512]{2,1,0:T(8,128)(2,1)S(1)} %collective-permute-done.20), channel_id=1, source_target_pairs={{0,2},{1,3},{2,6},{3,7},{6,10},{7,11},{10,14},{11,15},{14,12},{15,... | collective-permute-start | bytes 1179656 | tf_op jit(solution)/shard_map/ppermute | solution.py:282
  92.4 9.8 %collective-permute-start.26 = (bf16[6,64,512]{2,1,0:T(8,128)(2,1)S(1)}, bf16[6,64,512]{2,1,0:T(8,128)(2,1)S(1)}, u32[]{:S(2)}, u32[]{:S(2)}) collective-permute-start(bf16[6,64,512]{2,1,0:T(8,128)(2,1)S(1)} %collective-permute-done.22), channel_id=1, source_target_pairs={{0,4},{1,5},{2,0},{3,1},{6,2},{7,3},{10,6},{11,7},{14,10},{15,11},... | collective-permute-start | bytes 1179656 | tf_op jit(solution)/shard_map/ppermute | solution.py:282
  93.7 10.0 %collective-permute-start.21 = (bf16[6,64,512]{2,1,0:T(8,128)(2,1)S(1)}, bf16[6,64,512]{2,1,0:T(8,128)(2,1)S(1)}, u32[]{:S(2)}, u32[]{:S(2)}) collective-permute-start(bf16[6,64,512]{2,1,0:T(8,128)(2,1)S(1)} %collective-permute-done.20), channel_id=1, source_target_pairs={{0,1},{1,0},{2,3},{3,2},{4,5},{5,4},{6,7},{7,6},{8,9},{9,8},{10,11... | collective-permute-start | bytes 1179656 | tf_op jit(solution)/shard_map/ppermute | solution.py:285
  93.8 10.6 %collective-permute-start.23 = (bf16[6,64,512]{2,1,0:T(8,128)(2,1)S(1)}, bf16[6,64,512]{2,1,0:T(8,128)(2,1)S(1)}, u32[]{:S(2)}, u32[]{:S(2)}) collective-permute-start(bf16[6,64,512]{2,1,0:T(8,128)(2,1)S(1)} %collective-permute-done.22), channel_id=1, source_target_pairs={{0,1},{1,0},{2,3},{3,2},{4,5},{5,4},{6,7},{7,6},{8,9},{9,8},{10,11... | collective-permute-start | bytes 1179656 | tf_op jit(solution)/shard_map/ppermute | solution.py:285
  101.5 5.7 %collective-permute-start.28 = (bf16[6,32,512]{2,1,0:T(8,128)(2,1)S(1)}, bf16[6,32,512]{2,1,0:T(8,128)(2,1)S(1)}, u32[]{:S(2)}, u32[]{:S(2)}) collective-permute-start(bf16[6,32,512]{2,1,0:T(8,128)(2,1)S(1)} %slice.92), channel_id=1, source_target_pairs={{0,2},{1,3},{2,6},{3,7},{6,10},{7,11},{10,14},{11,15},{14,12},{15,... | collective-permute-start | bytes 589832 | tf_op jit(solution)/shard_map/ppermute | solution.py:282
  102.2 5.9 %collective-permute-start.29 = (bf16[6,32,512]{2,1,0:T(8,128)(2,1)S(1)}, bf16[6,32,512]{2,1,0:T(8,128)(2,1)S(1)}, u32[]{:S(2)}, u32[]{:S(2)}) collective-permute-start(bf16[6,32,512]{2,1,0:T(8,128)(2,1)S(1)} %slice.93), channel_id=1, source_target_pairs={{0,4},{1,5},{2,0},{3,1},{6,2},{7,3},{10,6},{11,7},{14,10},{15,11},... | collective-permute-start | bytes 589832 | tf_op jit(solution)/shard_map/ppermute | solution.py:282
  103.8 4.4 %collective-permute-start.25 = (bf16[6,64,512]{2,1,0:T(8,128)(2,1)S(1)}, bf16[6,64,512]{2,1,0:T(8,128)(2,1)S(1)}, u32[]{:S(2)}, u32[]{:S(2)}) collective-permute-start(bf16[6,64,512]{2,1,0:T(8,128)(2,1)S(1)} %collective-permute-done.24), channel_id=1, source_target_pairs={{0,1},{1,0},{2,3},{3,2},{4,5},{5,4},{6,7},{7,6},{8,9},{9,8},{10,11... | collective-permute-start | bytes 1179656 | tf_op jit(solution)/shard_map/ppermute | solution.py:285
  103.8 4.5 %collective-permute-start.27 = (bf16[6,64,512]{2,1,0:T(8,128)(2,1)S(1)}, bf16[6,64,512]{2,1,0:T(8,128)(2,1)S(1)}, u32[]{:S(2)}, u32[]{:S(2)}) collective-permute-start(bf16[6,64,512]{2,1,0:T(8,128)(2,1)S(1)} %collective-permute-done.26), channel_id=1, source_target_pairs={{0,1},{1,0},{2,3},{3,2},{4,5},{5,4},{6,7},{7,6},{8,9},{9,8},{10,11... | collective-permute-start | bytes 1179656 | tf_op jit(solution)/shard_map/ppermute | solution.py:285
  108.2 1.8 %collective-permute-start.30 = (bf16[6,64,512]{2,1,0:T(8,128)(2,1)S(1)}, bf16[6,64,512]{2,1,0:T(8,128)(2,1)S(1)}, u32[]{:S(2)}, u32[]{:S(2)}) collective-permute-start(bf16[6,64,512]{2,1,0:T(8,128)(2,1)S(1)} %constant_dynamic-update-slice_fusion), channel_id=1, source_target_pairs={{0,1},{1,0},{2,3},{3,2},{4,5},{5,4},{6,7},{7,6},{8,9},{9,8},{10,11... | collective-permute-start | bytes 1179656 | tf_op jit(solution)/shard_map/ppermute | solution.py:285
  113.7 5.3 %copy-start.2 = (bf16[2,3,512,256]{3,2,1,0:T(8,128)(2,1)S(1)}, bf16[2,3,512,256]{3,2,1,0:T(8,128)(2,1)}, u32[]{:S(2)}) copy-start(bf16[2,3,512,256]{3,2,1,0:T(8,128)(2,1)} %get-tuple-element.49.far_ref) | copy-start | bytes 4718596
  113.7 5.3 %copy-start.3 = (bf16[2,3,384,256]{3,2,1,0:T(8,128)(2,1)S(1)}, bf16[2,3,384,256]{3,2,1,0:T(8,128)(2,1)}, u32[]{:S(2)}) copy-start(bf16[2,3,384,256]{3,2,1,0:T(8,128)(2,1)} %get-tuple-element.48.near_ref) | copy-start | bytes 3538948

commit v6 on v5

--- a/solution.py
+++ b/solution.py
@@ -179,11 +179,11 @@
         name="norm_send",
     )(index, depth_count, alignment, qkv_weight, qkv_weight)
     own = pl.pallas_call(
-        functools.partial(own_kernel, rows),
+        functools.partial(own_kernel, residues),
         out_shape=qk_shape,
         grid_spec=pltpu.PrefetchScalarGridSpec(
             num_scalar_prefetch=2,
-            grid=(steps,),
+            grid=(1,),
             in_specs=[vmem] + weight_specs(lambda half: half),
             out_specs=vmem,
         ),
@@ -197,7 +197,7 @@
 def value_projection(normed, qkv_weight, head_count):
     seqs, residues, features = normed.shape
     size = features // head_count
-    rows = 256 if residues % 256 == 0 else residues
+    rows = residues
     steps = residues // rows
     flops = 2 * seqs * residues * features * features
     moved = 2 * (2 * seqs * residues * features + features * features)

time: 139 us -> 138 us (level)
  transfers between devices with their start and end apart: 31 -> 31, of which waited for: 21 -> 21; matrix products, arithmetic and copies ran while one was open for 2% -> 2% of each run, Pallas kernels for 10% -> 9%
where the time goes in v6:
time: 138 us
  Pallas kernels  52.5 us (38%)
  waiting for transfers between devices  51.5 us (37%)
  starting transfers between devices  26.1 us (19%)
  local copies, waits for them, and re-layouts  4.31 us (3%)
  other arithmetic  1.93 us (1%)
  between operations  1.64 us (1%)
    ppermute x22, waiting for transfers between devices, send(): return lax.ppermute(value, 'seq', pairs)  49.4 us
    ppermute x22, starting transfers between devices, send(): return lax.ppermute(value, 'seq', pairs)  24 us
    pallas_call x1, Pallas kernels, contact_call(): pl.pallas_call(contact_kernel, out_shape=jax.ShapeDtypeStruct((own_rows,...  19.6 us
    pallas_call x1, Pallas kernels, projections(): pl.pallas_call(norm_send_kernel, out_shape=(jax.ShapeDtypeStruct(alignmen...  7.74 us
    pallas_call x1, Pallas kernels, row_mix_of(): pl.pallas_call(mix_kernel, out_shape=jax.ShapeDtypeStruct((seqs, residues...  5.25 us
    pallas_call x1, Pallas kernels, value_projection(): pl.pallas_call(functools.partial(value_kernel, rows), out_shape=jax.Shape...  4.97 us
    pallas_call x1, Pallas kernels, projections(): pl.pallas_call(functools.partial(own_kernel, residues), out_shape=qk_shap...  4.97 us
    pallas_call x1, Pallas kernels, contact_head(): pl.pallas_call(window_kernel, out_shape=jax.ShapeDtypeStruct((blocks, ROW...  3.68 us
  transfers between devices with their start and end apart: 31, of which 21 were waited for; matrix products, arithmetic and copies ran while one was open for 2% of the time, Pallas kernels for 9%

profile of v6, /device:TPU:0, one launch (start us, length us, event | category | flops | bytes accessed | tf_op | source)
XLA Modules:
  0.0 138.1 jit_solution(3305767844157417984)
XLA Ops:
  1.3 7.7 %norm_send.1 = (bf16[4,512,768]{2,1,0:T(8,128)(2,1)S(1)}, bf16[2,6,512,256]{3,2,1,0:T(8,128)(2,1)}) custom-call(s32[1]{0:T(128)} %bitcast.index_ref, s32[1]{0:T(128)S(6)} %copy.26.depth_ref, bf16[4,512,768]{2,1,0:T(8,128)(2,1)} %x_ref.1, bf16[768,2304]{1,0:T(8,128)(2,1)} %w_ref.1, bf16[768,2304]{1,0:T(8,128)(2,1)} %w_ref.1), custom_call_target="tpu_custom_call" | custom-call | flops 2415919104 | bytes 10616832 | tf_op jit(solution)/shard_map/norm_send/pallas_call | solution.py:168
  9.0 1.6 %copy-done = bf16[4,512,768]{2,1,0:T(8,128)(2,1)} copy-done((bf16[4,512,768]{2,1,0:T(8,128)(2,1)}, bf16[4,512,768]{2,1,0:T(8,128)(2,1)S(1)}, u32[]{:S(2)}) %copy-start) | copy-done | bytes 3145752
  10.6 0.5 collective-permute-start
  11.1 5.0 %own_project.1.own_ref = bf16[2,6,512,256]{3,2,1,0:T(8,128)(2,1)S(1)} custom-call(s32[1]{0:T(128)} %bitcast.index_ref, s32[1]{0:T(128)S(6)} %copy.26.depth_ref, bf16[4,512,768]{2,1,0:T(8,128)(2,1)} %copy-done, bf16[768,2304]{1,0:T(8,128)(2,1)} %w_ref.1, bf16[768,2304]{1,0:T(8,128)(2,1)} %w_ref.1), custom_call_target="tpu_custom_call" | custom-call | flops 2415919104 | bytes 7471104 | tf_op jit(solution)/shard_map/own_project/pallas_call | solution.py:181
  16.1 0.5 collective-permute-done.other_ref
  16.6 3.4 %scores.1 = f32[8,6,64,512]{3,2,1,0:T(8,128)S(1)} custom-call(s32[1]{0:T(128)} %bitcast.index_ref, s32[16]{0:T(128)S(1)} %copy-done.1, s32[1]{0:T(128)S(6)} %copy.26.depth_ref, bf16[2,6,512,256]{3,2,1,0:T(8,128)(2,1)S(1)} %own_project.1.own_ref, bf16[2,6,512,256]{3,2,1,0:T(8,128)(2,1)S(1)} %collective-permute-done.other_ref), custom_call_target="tpu_custom_call" | custom-call | flops 1610612736 | bytes 12582912 | tf_op jit(solution)/shard_map/scores/pallas_call | solution.py:226
  20.0 0.7 convert.6
  20.7 0.2 slice_bitcast_fusion.12
  20.9 2.9 %collective-permute-start.1 = (f16[6,32,512]{2,1,0:T(8,128)(2,1)S(1)}, f16[6,32,512]{2,1,0:T(8,128)(2,1)S(1)}, u32[]{:S(2)}, u32[]{:S(2)}) collective-permute-start(f16[6,32,512]{2,1,0:T(8,128)(2,1)S(1)} %get-tuple-element.63), channel_id=1, source_target_pairs={{0,2},{1,3},{2,6},{3,7},{6,10},{7,11},{10,14},{11,15},{14,12},{15,... | collective-permute-start | bytes 589832 | tf_op jit(solution)/shard_map/ppermute | solution.py:282
  24.0 5.1 %collective-permute-done.1 = f16[6,32,512]{2,1,0:T(8,128)(2,1)S(1)} collective-permute-done((f16[6,32,512]{2,1,0:T(8,128)(2,1)S(1)}, f16[6,32,512]{2,1,0:T(8,128)(2,1)S(1)}, u32[]{:S(2)}, u32[]{:S(2)}) %collective-permute-start.1) | collective-permute-done | bytes 196640 | tf_op jit(solution)/shard_map/ppermute | solution.py:282
  29.1 1.4 %collective-permute-done.2 = f16[6,32,512]{2,1,0:T(8,128)(2,1)S(1)} collective-permute-done((f16[6,32,512]{2,1,0:T(8,128)(2,1)S(1)}, f16[6,32,512]{2,1,0:T(8,128)(2,1)S(1)}, u32[]{:S(2)}, u32[]{:S(2)}) %collective-permute-start.2) | collective-permute-done | bytes 196640 | tf_op jit(solution)/shard_map/ppermute | solution.py:282
  30.5 0.1 fusion.26
  30.7 1.6 %collective-permute-start.3 = (f16[6,32,512]{2,1,0:T(8,128)(2,1)S(1)}, f16[6,32,512]{2,1,0:T(8,128)(2,1)S(1)}, u32[]{:S(2)}, u32[]{:S(2)}) collective-permute-start(f16[6,32,512]{2,1,0:T(8,128)(2,1)S(1)} %get-tuple-element.59), channel_id=1, source_target_pairs={{0,2},{1,3},{2,6},{3,7},{6,10},{7,11},{10,14},{11,15},{14,12},{15,... | collective-permute-start | bytes 589832 | tf_op jit(solution)/shard_map/ppermute | solution.py:282
  32.3 0.5 collective-permute-start.4
  32.8 1.6 %collective-permute-start.7 = (f16[6,32,512]{2,1,0:T(8,128)(2,1)S(1)}, f16[6,32,512]{2,1,0:T(8,128)(2,1)S(1)}, u32[]{:S(2)}, u32[]{:S(2)}) collective-permute-start(f16[6,32,512]{2,1,0:T(8,128)(2,1)S(1)} %get-tuple-element.61), channel_id=1, source_target_pairs={{0,2},{1,3},{2,6},{3,7},{6,10},{7,11},{10,14},{11,15},{14,12},{15,... | collective-permute-start | bytes 589832 | tf_op jit(solution)/shard_map/ppermute | solution.py:282
  34.4 0.5 collective-permute-start.8
  34.8 3.8 %collective-permute-done.3 = f16[6,32,512]{2,1,0:T(8,128)(2,1)S(1)} collective-permute-done((f16[6,32,512]{2,1,0:T(8,128)(2,1)S(1)}, f16[6,32,512]{2,1,0:T(8,128)(2,1)S(1)}, u32[]{:S(2)}, u32[]{:S(2)}) %collective-permute-start.3) | collective-permute-done | bytes 196640 | tf_op jit(solution)/shard_map/ppermute | solution.py:282
  38.6 1.3 collective-permute-done.4
  39.9 0.1 fusion.22
  40.1 1.6 %collective-permute-start.5 = (f16[6,32,512]{2,1,0:T(8,128)(2,1)S(1)}, f16[6,32,512]{2,1,0:T(8,128)(2,1)S(1)}, u32[]{:S(2)}, u32[]{:S(2)}) collective-permute-start(f16[6,32,512]{2,1,0:T(8,128)(2,1)S(1)} %get-tuple-element.57), channel_id=1, source_target_pairs={{0,2},{1,3},{2,6},{3,7},{6,10},{7,11},{10,14},{11,15},{14,12},{15,... | collective-permute-start | bytes 589832 | tf_op jit(solution)/shard_map/ppermute | solution.py:282
  41.7 0.4 collective-permute-start.6
  42.2 0.7 collective-permute-done.7
  42.8 1.3 collective-permute-done.8
  44.1 0.1 fusion.18
  44.3 1.6 %collective-permute-start.10 = (f16[6,32,512]{2,1,0:T(8,128)(2,1)S(1)}, f16[6,32,512]{2,1,0:T(8,128)(2,1)S(1)}, u32[]{:S(2)}, u32[]{:S(2)}) collective-permute-start(f16[6,32,512]{2,1,0:T(8,128)(2,1)S(1)} %get-tuple-element.55), channel_id=1, source_target_pairs={{0,2},{1,3},{2,6},{3,7},{6,10},{7,11},{10,14},{11,15},{14,12},{15,... | collective-permute-start | bytes 589832 | tf_op jit(solution)/shard_map/ppermute | solution.py:282
  45.9 0.5 collective-permute-start.11
  46.3 0.8 collective-permute-done.5
  47.1 1.3 collective-permute-done.6
  48.5 1.5 %collective-permute-done.10 = f16[6,32,512]{2,1,0:T(8,128)(2,1)S(1)} collective-permute-done((f16[6,32,512]{2,1,0:T(8,128)(2,1)S(1)}, f16[6,32,512]{2,1,0:T(8,128)(2,1)S(1)}, u32[]{:S(2)}, u32[]{:S(2)}) %collective-permute-start.10) | collective-permute-done | bytes 196640 | tf_op jit(solution)/shard_map/ppermute | solution.py:282
  50.0 3.1 %collective-permute-done.11 = f16[6,32,512]{2,1,0:T(8,128)(2,1)S(1)} collective-permute-done((f16[6,32,512]{2,1,0:T(8,128)(2,1)S(1)}, f16[6,32,512]{2,1,0:T(8,128)(2,1)S(1)}, u32[]{:S(2)}, u32[]{:S(2)}) %collective-permute-start.11) | collective-permute-done | bytes 196640 | tf_op jit(solution)/shard_map/ppermute | solution.py:282
  53.2 0.5 collective-permute-start.12
  53.7 1.6 %collective-permute-start.9 = (f16[6,32,512]{2,1,0:T(8,128)(2,1)S(1)}, f16[6,32,512]{2,1,0:T(8,128)(2,1)S(1)}, u32[]{:S(2)}, u32[]{:S(2)}) collective-permute-start(f16[6,32,512]{2,1,0:T(8,128)(2,1)S(1)} %get-tuple-element.52), channel_id=1, source_target_pairs={{0,2},{1,3},{2,6},{3,7},{6,10},{7,11},{10,14},{11,15},{14,12},{15,... | collective-permute-start | bytes 589832 | tf_op jit(solution)/shard_map/ppermute | solution.py:282
  55.3 0.4 collective-permute-start.14
  55.7 3.2 %collective-permute-done.12 = f16[6,32,512]{2,1,0:T(8,128)(2,1)S(1)} collective-permute-done((f16[6,32,512]{2,1,0:T(8,128)(2,1)S(1)}, f16[6,32,512]{2,1,0:T(8,128)(2,1)S(1)}, u32[]{:S(2)}, u32[]{:S(2)}) %collective-permute-start.12) | collective-permute-done | bytes 196640 | tf_op jit(solution)/shard_map/ppermute | solution.py:282
  58.9 1.6 %collective-permute-done.9 = f16[6,32,512]{2,1,0:T(8,128)(2,1)S(1)} collective-permute-done((f16[6,32,512]{2,1,0:T(8,128)(2,1)S(1)}, f16[6,32,512]{2,1,0:T(8,128)(2,1)S(1)}, u32[]{:S(2)}, u32[]{:S(2)}) %collective-permute-start.9) | collective-permute-done | bytes 196640 | tf_op jit(solution)/shard_map/ppermute | solution.py:282
  60.5 0.2 fusion.30
  60.7 1.9 %collective-permute-start.13 = (f16[6,32,512]{2,1,0:T(8,128)(2,1)S(1)}, f16[6,32,512]{2,1,0:T(8,128)(2,1)S(1)}, u32[]{:S(2)}, u32[]{:S(2)}) collective-permute-start(f16[6,32,512]{2,1,0:T(8,128)(2,1)S(1)} %get-tuple-element.51), channel_id=1, source_target_pairs={{0,2},{1,3},{2,6},{3,7},{6,10},{7,11},{10,14},{11,15},{14,12},{15,... | collective-permute-start | bytes 589832 | tf_op jit(solution)/shard_map/ppermute | solution.py:282
  62.6 3.8 %collective-permute-done.13 = f16[6,32,512]{2,1,0:T(8,128)(2,1)S(1)} collective-permute-done((f16[6,32,512]{2,1,0:T(8,128)(2,1)S(1)}, f16[6,32,512]{2,1,0:T(8,128)(2,1)S(1)}, u32[]{:S(2)}, u32[]{:S(2)}) %collective-permute-start.13) | collective-permute-done | bytes 196640 | tf_op jit(solution)/shard_map/ppermute | solution.py:282
  66.5 0.3 fusion.5
  66.9 1.9 %collective-permute-start.16 = (bf16[6,64,512]{2,1,0:T(8,128)(2,1)S(1)}, bf16[6,64,512]{2,1,0:T(8,128)(2,1)S(1)}, u32[]{:S(2)}, u32[]{:S(2)}) collective-permute-start(bf16[6,64,512]{2,1,0:T(8,128)(2,1)S(1)} %fusion.5), channel_id=1, source_target_pairs={{0,2},{1,3},{2,6},{3,7},{6,10},{7,11},{10,14},{11,15},{14,12},{15,... | collective-permute-start | bytes 1179656 | tf_op jit(solution)/shard_map/ppermute | solution.py:282
  68.8 0.2 collective-permute-start.18
  69.2 1.0 copy.9
  70.3 2.9 %spread_taps.1 = (bf16[2,3,384,256]{3,2,1,0:T(8,128)(2,1)}, bf16[2,3,512,256]{3,2,1,0:T(8,128)(2,1)}) custom-call(bf16[36,64,64]{2,1,0:T(8,128)(2,1)} %bitcast.115), custom_call_target="tpu_custom_call" | custom-call | bytes 6291456 | tf_op jit(solution)/shard_map/spread_taps/pallas_call | solution.py:471
  73.2 0.8 dynamic_update_slice.48
  74.0 5.0 %value_project.1.v_ref = bf16[12,512,256]{2,1,0:T(8,128)(2,1)S(1)} custom-call(bf16[4,512,768]{2,1,0:T(8,128)(2,1)} %copy-done, bf16[768,2304]{1,0:T(8,128)(2,1)} %w_ref.1), custom_call_target="tpu_custom_call" | custom-call | flops 2415919104 | bytes 7471104 | tf_op jit(solution)/shard_map/value_project/pallas_call | solution.py:206
  79.0 1.0 collective-permute-done.18
  80.0 0.9 collective-permute-start.20
  80.9 1.1 collective-permute-start.22
  82.0 0.5 collective-permute-start.19
  82.6 7.7 %collective-permute-done.20 = bf16[6,64,512]{2,1,0:T(8,128)(2,1)S(1)} collective-permute-done((bf16[6,64,512]{2,1,0:T(8,128)(2,1)S(1)}, bf16[6,64,512]{2,1,0:T(8,128)(2,1)S(1)}, u32[]{:S(2)}, u32[]{:S(2)}) %collective-permute-start.20) | collective-permute-done | bytes 393248 | tf_op jit(solution)/shard_map/ppermute | solution.py:282
  90.3 1.2 collective-permute-done.22
  91.5 0.7 collective-permute-start.24
  92.2 1.3 collective-permute-start.26
  93.5 0.5 collective-permute-start.23
  94.2 7.0 %collective-permute-done.24 = bf16[6,64,512]{2,1,0:T(8,128)(2,1)S(1)} collective-permute-done((bf16[6,64,512]{2,1,0:T(8,128)(2,1)S(1)}, bf16[6,64,512]{2,1,0:T(8,128)(2,1)S(1)}, u32[]{:S(2)}, u32[]{:S(2)}) %collective-permute-start.24) | collective-permute-done | bytes 393248 | tf_op jit(solution)/shard_map/ppermute | solution.py:282
  101.2 0.7 collective-permute-start.28
  101.9 1.5 %collective-permute-start.29 = (bf16[6,32,512]{2,1,0:T(8,128)(2,1)S(1)}, bf16[6,32,512]{2,1,0:T(8,128)(2,1)S(1)}, u32[]{:S(2)}, u32[]{:S(2)}) collective-permute-start(bf16[6,32,512]{2,1,0:T(8,128)(2,1)S(1)} %slice.93), channel_id=1, source_target_pairs={{0,4},{1,5},{2,0},{3,1},{6,2},{7,3},{10,6},{11,7},{14,10},{15,11},... | collective-permute-start | bytes 589832 | tf_op jit(solution)/shard_map/ppermute | solution.py:282
  103.4 0.5 collective-permute-start.27
  104.1 2.9 %collective-permute-done.28 = bf16[6,32,512]{2,1,0:T(8,128)(2,1)S(1)} collective-permute-done((bf16[6,32,512]{2,1,0:T(8,128)(2,1)S(1)}, bf16[6,32,512]{2,1,0:T(8,128)(2,1)S(1)}, u32[]{:S(2)}, u32[]{:S(2)}) %collective-permute-start.28) | collective-permute-done | bytes 196640 | tf_op jit(solution)/shard_map/ppermute | solution.py:282
  107.0 0.7 collective-permute-done.29
  107.9 1.5 %collective-permute-done.30 = bf16[6,64,512]{2,1,0:T(8,128)(2,1)S(1)} collective-permute-done((bf16[6,64,512]{2,1,0:T(8,128)(2,1)S(1)}, bf16[6,64,512]{2,1,0:T(8,128)(2,1)S(1)}, u32[]{:S(2)}, u32[]{:S(2)}) %collective-permute-start.30) | collective-permute-done | bytes 393248 | tf_op jit(solution)/shard_map/ppermute | solution.py:285
  109.5 3.7 %pair_window.1.pf_ref = bf16[12,48,512]{2,1,0:T(8,128)(2,1)S(1)} custom-call(s32[1]{0:T(128)} %bitcast.index_ref, s32[16]{0:T(128)S(1)} %copy-done.1, bf16[2,8,6,64,512]{4,3,2,1,0:T(8,128)(2,1)S(1)} %bitcast_dynamic-update-slice_fusion.p_ref), custom_call_target="tpu_custom_call" | custom-call | flops 2717908992 | bytes 6291456 | tf_op jit(solution)/shard_map/pair_window/pallas_call | solution.py:550
  113.2 5.2 %row_mix.1 = bf16[4,512,768]{2,1,0:T(8,128)(2,1)} custom-call(s32[1]{0:T(128)} %bitcast.index_ref, s32[16]{0:T(128)S(1)} %copy-done.1, bf16[2,8,6,64,512]{4,3,2,1,0:T(8,128)(2,1)S(1)} %bitcast_dynamic-update-slice_fusion.p_ref, bf16[12,512,256]{2,1,0:T(8,128)(2,1)S(1)} %value_project.1.v_ref), custom_call_target="tpu_custom_call" | custom-call | flops 1610612736 | bytes 12582912 | tf_op jit(solution)/shard_map/row_mix/pallas_call | solution.py:251
  118.4 19.6 %contact_head.1 = f32[32,512]{1,0:T(8,128)} custom-call(s32[1]{0:T(128)} %bitcast.index_ref, bf16[12,48,512]{2,1,0:T(8,128)(2,1)S(1)} %pair_window.1.pf_ref, bf16[48,256]{1,0:T(8,128)(2,1)S(1)} %mul.28.pair_ref, bf16[2,3,384,256]{3,2,1,0:T(8,128)(2,1)S(1)} %copy-done.3, bf16[2,3,512,256]{3,2,1,0:T(8,128)(2,1)S(1)} %copy-done.2, ...), custom_call_target="tpu_custom_call" | custom-call | flops 5469372416 | bytes 4194304 | tf_op jit(solution)/shard_map/contact_head/pallas_call | solution.py:575
  (56 shorter events, 1.3 us)
Async XLA Ops:
  9.0 1.6 %copy-start = (bf16[4,512,768]{2,1,0:T(8,128)(2,1)}, bf16[4,512,768]{2,1,0:T(8,128)(2,1)S(1)}, u32[]{:S(2)}) copy-start(bf16[4,512,768]{2,1,0:T(8,128)(2,1)S(1)} %get-tuple-element.39.normed_ref) | copy-start | bytes 9437188
  10.6 6.0 %collective-permute-start = (bf16[2,6,512,256]{3,2,1,0:T(8,128)(2,1)}, bf16[2,6,512,256]{3,2,1,0:T(8,128)(2,1)S(1)}, u32[]{:S(2)}, u32[]{:S(2)}) collective-permute-start(bf16[2,6,512,256]{3,2,1,0:T(8,128)(2,1)} %get-tuple-element.27), channel_id=1, source_target_pairs={{0,1},{1,0},{2,3},{3,2},{4,5},{5,4},{6,7},{7,6},{8,9},{9,8},{10,11... | collective-permute-start | bytes 9437192 | tf_op jit(solution)/shard_map/ppermute | solution.py:285
  11.1 5.5 %copy-start.1 = (s32[16]{0:T(128)S(1)}, s32[16]{0:T(128)}, u32[]{:S(2)}) copy-start(s32[16]{0:T(128)} %constant.13.clone.table_ref) | copy-start | bytes 196
  20.9 8.2 %collective-permute-start.1 = (f16[6,32,512]{2,1,0:T(8,128)(2,1)S(1)}, f16[6,32,512]{2,1,0:T(8,128)(2,1)S(1)}, u32[]{:S(2)}, u32[]{:S(2)}) collective-permute-start(f16[6,32,512]{2,1,0:T(8,128)(2,1)S(1)} %get-tuple-element.63), channel_id=1, source_target_pairs={{0,2},{1,3},{2,6},{3,7},{6,10},{7,11},{10,14},{11,15},{14,12},{15,... | collective-permute-start | bytes 589832 | tf_op jit(solution)/shard_map/ppermute | solution.py:282
  23.9 6.7 %collective-permute-start.2 = (f16[6,32,512]{2,1,0:T(8,128)(2,1)S(1)}, f16[6,32,512]{2,1,0:T(8,128)(2,1)S(1)}, u32[]{:S(2)}, u32[]{:S(2)}) collective-permute-start(f16[6,32,512]{2,1,0:T(8,128)(2,1)S(1)} %get-tuple-element.62), channel_id=1, source_target_pairs={{0,4},{1,5},{2,0},{3,1},{6,2},{7,3},{10,6},{11,7},{14,10},{15,11},... | collective-permute-start | bytes 589832 | tf_op jit(solution)/shard_map/ppermute | solution.py:282
  30.7 38.3 %copy-start.5 = (bf16[64,12]{0,1:T(8,128)(2,1)S(1)}, bf16[64,12]{0,1:T(8,128)(2,1)}, u32[]{:S(2)}) copy-start(bf16[64,12]{0,1:T(8,128)(2,1)} %param.10) | copy-start | bytes 4612
  30.7 38.5 %copy-start.6 = (f32[64]{0:T(128)S(1)}, f32[64]{0:T(128)}, u32[]{:S(2)}) copy-start(f32[64]{0:T(128)} %param.12) | copy-start | bytes 772
  30.7 38.5 %copy-start.4 = (bf16[4,9,64,64]{3,2,1,0:T(8,128)(2,1)S(1)}, bf16[4,9,64,64]{3,2,1,0:T(8,128)(2,1)}, u32[]{:S(2)}) copy-start(bf16[4,9,64,64]{3,2,1,0:T(8,128)(2,1)} %param.11) | copy-start | bytes 884740
  30.7 7.9 %collective-permute-start.3 = (f16[6,32,512]{2,1,0:T(8,128)(2,1)S(1)}, f16[6,32,512]{2,1,0:T(8,128)(2,1)S(1)}, u32[]{:S(2)}, u32[]{:S(2)}) collective-permute-start(f16[6,32,512]{2,1,0:T(8,128)(2,1)S(1)} %get-tuple-element.59), channel_id=1, source_target_pairs={{0,2},{1,3},{2,6},{3,7},{6,10},{7,11},{10,14},{11,15},{14,12},{15,... | collective-permute-start | bytes 589832 | tf_op jit(solution)/shard_map/ppermute | solution.py:282
  32.3 7.6 %collective-permute-start.4 = (f16[6,32,512]{2,1,0:T(8,128)(2,1)S(1)}, f16[6,32,512]{2,1,0:T(8,128)(2,1)S(1)}, u32[]{:S(2)}, u32[]{:S(2)}) collective-permute-start(f16[6,32,512]{2,1,0:T(8,128)(2,1)S(1)} %get-tuple-element.58), channel_id=1, source_target_pairs={{0,4},{1,5},{2,0},{3,1},{6,2},{7,3},{10,6},{11,7},{14,10},{15,11},... | collective-permute-start | bytes 589832 | tf_op jit(solution)/shard_map/ppermute | solution.py:282
  32.8 10.0 %collective-permute-start.7 = (f16[6,32,512]{2,1,0:T(8,128)(2,1)S(1)}, f16[6,32,512]{2,1,0:T(8,128)(2,1)S(1)}, u32[]{:S(2)}, u32[]{:S(2)}) collective-permute-start(f16[6,32,512]{2,1,0:T(8,128)(2,1)S(1)} %get-tuple-element.61), channel_id=1, source_target_pairs={{0,2},{1,3},{2,6},{3,7},{6,10},{7,11},{10,14},{11,15},{14,12},{15,... | collective-permute-start | bytes 589832 | tf_op jit(solution)/shard_map/ppermute | solution.py:282
  34.4 9.8 %collective-permute-start.8 = (f16[6,32,512]{2,1,0:T(8,128)(2,1)S(1)}, f16[6,32,512]{2,1,0:T(8,128)(2,1)S(1)}, u32[]{:S(2)}, u32[]{:S(2)}) collective-permute-start(f16[6,32,512]{2,1,0:T(8,128)(2,1)S(1)} %get-tuple-element.60), channel_id=1, source_target_pairs={{0,4},{1,5},{2,0},{3,1},{6,2},{7,3},{10,6},{11,7},{14,10},{15,11},... | collective-permute-start | bytes 589832 | tf_op jit(solution)/shard_map/ppermute | solution.py:282
  40.1 7.0 %collective-permute-start.5 = (f16[6,32,512]{2,1,0:T(8,128)(2,1)S(1)}, f16[6,32,512]{2,1,0:T(8,128)(2,1)S(1)}, u32[]{:S(2)}, u32[]{:S(2)}) collective-permute-start(f16[6,32,512]{2,1,0:T(8,128)(2,1)S(1)} %get-tuple-element.57), channel_id=1, source_target_pairs={{0,2},{1,3},{2,6},{3,7},{6,10},{7,11},{10,14},{11,15},{14,12},{15,... | collective-permute-start | bytes 589832 | tf_op jit(solution)/shard_map/ppermute | solution.py:282
  41.7 6.7 %collective-permute-start.6 = (f16[6,32,512]{2,1,0:T(8,128)(2,1)S(1)}, f16[6,32,512]{2,1,0:T(8,128)(2,1)S(1)}, u32[]{:S(2)}, u32[]{:S(2)}) collective-permute-start(f16[6,32,512]{2,1,0:T(8,128)(2,1)S(1)} %get-tuple-element.56), channel_id=1, source_target_pairs={{0,4},{1,5},{2,0},{3,1},{6,2},{7,3},{10,6},{11,7},{14,10},{15,11},... | collective-permute-start | bytes 589832 | tf_op jit(solution)/shard_map/ppermute | solution.py:282
  44.3 5.7 %collective-permute-start.10 = (f16[6,32,512]{2,1,0:T(8,128)(2,1)S(1)}, f16[6,32,512]{2,1,0:T(8,128)(2,1)S(1)}, u32[]{:S(2)}, u32[]{:S(2)}) collective-permute-start(f16[6,32,512]{2,1,0:T(8,128)(2,1)S(1)} %get-tuple-element.55), channel_id=1, source_target_pairs={{0,2},{1,3},{2,6},{3,7},{6,10},{7,11},{10,14},{11,15},{14,12},{15,... | collective-permute-start | bytes 589832 | tf_op jit(solution)/shard_map/ppermute | solution.py:282
  45.9 7.2 %collective-permute-start.11 = (f16[6,32,512]{2,1,0:T(8,128)(2,1)S(1)}, f16[6,32,512]{2,1,0:T(8,128)(2,1)S(1)}, u32[]{:S(2)}, u32[]{:S(2)}) collective-permute-start(f16[6,32,512]{2,1,0:T(8,128)(2,1)S(1)} %get-tuple-element.54), channel_id=1, source_target_pairs={{0,4},{1,5},{2,0},{3,1},{6,2},{7,3},{10,6},{11,7},{14,10},{15,11},... | collective-permute-start | bytes 589832 | tf_op jit(solution)/shard_map/ppermute | solution.py:282
  53.2 5.7 %collective-permute-start.12 = (f16[6,32,512]{2,1,0:T(8,128)(2,1)S(1)}, f16[6,32,512]{2,1,0:T(8,128)(2,1)S(1)}, u32[]{:S(2)}, u32[]{:S(2)}) collective-permute-start(f16[6,32,512]{2,1,0:T(8,128)(2,1)S(1)} %fusion.12), channel_id=1, source_target_pairs={{0,4},{1,5},{2,0},{3,1},{6,2},{7,3},{10,6},{11,7},{14,10},{15,11},... | collective-permute-start | bytes 589832 | tf_op jit(solution)/shard_map/ppermute | solution.py:282
  53.7 6.8 %collective-permute-start.9 = (f16[6,32,512]{2,1,0:T(8,128)(2,1)S(1)}, f16[6,32,512]{2,1,0:T(8,128)(2,1)S(1)}, u32[]{:S(2)}, u32[]{:S(2)}) collective-permute-start(f16[6,32,512]{2,1,0:T(8,128)(2,1)S(1)} %get-tuple-element.52), channel_id=1, source_target_pairs={{0,2},{1,3},{2,6},{3,7},{6,10},{7,11},{10,14},{11,15},{14,12},{15,... | collective-permute-start | bytes 589832 | tf_op jit(solution)/shard_map/ppermute | solution.py:282
  55.3 7.3 %collective-permute-start.14 = (f16[6,32,512]{2,1,0:T(8,128)(2,1)S(1)}, f16[6,32,512]{2,1,0:T(8,128)(2,1)S(1)}, u32[]{:S(2)}, u32[]{:S(2)}) collective-permute-start(f16[6,32,512]{2,1,0:T(8,128)(2,1)S(1)} %get-tuple-element.53), channel_id=1, source_target_pairs={{0,4},{1,5},{2,0},{3,1},{6,2},{7,3},{10,6},{11,7},{14,10},{15,11},... | collective-permute-start | bytes 589832 | tf_op jit(solution)/shard_map/ppermute | solution.py:282
  60.7 5.7 %collective-permute-start.13 = (f16[6,32,512]{2,1,0:T(8,128)(2,1)S(1)}, f16[6,32,512]{2,1,0:T(8,128)(2,1)S(1)}, u32[]{:S(2)}, u32[]{:S(2)}) collective-permute-start(f16[6,32,512]{2,1,0:T(8,128)(2,1)S(1)} %get-tuple-element.51), channel_id=1, source_target_pairs={{0,2},{1,3},{2,6},{3,7},{6,10},{7,11},{10,14},{11,15},{14,12},{15,... | collective-permute-start | bytes 589832 | tf_op jit(solution)/shard_map/ppermute | solution.py:282
  66.8 15.7 %collective-permute-start.15 = (bf16[6,64,512]{2,1,0:T(8,128)(2,1)S(1)}, bf16[6,64,512]{2,1,0:T(8,128)(2,1)S(1)}, u32[]{:S(2)}, u32[]{:S(2)}) collective-permute-start(bf16[6,64,512]{2,1,0:T(8,128)(2,1)S(1)} %fusion.5), channel_id=1, source_target_pairs={{0,1},{1,0},{2,3},{3,2},{4,5},{5,4},{6,7},{7,6},{8,9},{9,8},{10,11... | collective-permute-start | bytes 1179656 | tf_op jit(solution)/shard_map/ppermute | solution.py:285
  66.9 12.1 %collective-permute-start.16 = (bf16[6,64,512]{2,1,0:T(8,128)(2,1)S(1)}, bf16[6,64,512]{2,1,0:T(8,128)(2,1)S(1)}, u32[]{:S(2)}, u32[]{:S(2)}) collective-permute-start(bf16[6,64,512]{2,1,0:T(8,128)(2,1)S(1)} %fusion.5), channel_id=1, source_target_pairs={{0,2},{1,3},{2,6},{3,7},{6,10},{7,11},{10,14},{11,15},{14,12},{15,... | collective-permute-start | bytes 1179656 | tf_op jit(solution)/shard_map/ppermute | solution.py:282
  68.8 11.2 %collective-permute-start.18 = (bf16[6,64,512]{2,1,0:T(8,128)(2,1)S(1)}, bf16[6,64,512]{2,1,0:T(8,128)(2,1)S(1)}, u32[]{:S(2)}, u32[]{:S(2)}) collective-permute-start(bf16[6,64,512]{2,1,0:T(8,128)(2,1)S(1)} %fusion.5), channel_id=1, source_target_pairs={{0,4},{1,5},{2,0},{3,1},{6,2},{7,3},{10,6},{11,7},{14,10},{15,11},... | collective-permute-start | bytes 1179656 | tf_op jit(solution)/shard_map/ppermute | solution.py:282
  80.0 10.4 %collective-permute-start.20 = (bf16[6,64,512]{2,1,0:T(8,128)(2,1)S(1)}, bf16[6,64,512]{2,1,0:T(8,128)(2,1)S(1)}, u32[]{:S(2)}, u32[]{:S(2)}) collective-permute-start(bf16[6,64,512]{2,1,0:T(8,128)(2,1)S(1)} %collective-permute-done.16), channel_id=1, source_target_pairs={{0,2},{1,3},{2,6},{3,7},{6,10},{7,11},{10,14},{11,15},{14,12},{15,... | collective-permute-start | bytes 1179656 | tf_op jit(solution)/shard_map/ppermute | solution.py:282
  80.9 10.6 %collective-permute-start.22 = (bf16[6,64,512]{2,1,0:T(8,128)(2,1)S(1)}, bf16[6,64,512]{2,1,0:T(8,128)(2,1)S(1)}, u32[]{:S(2)}, u32[]{:S(2)}) collective-permute-start(bf16[6,64,512]{2,1,0:T(8,128)(2,1)S(1)} %collective-permute-done.18), channel_id=1, source_target_pairs={{0,4},{1,5},{2,0},{3,1},{6,2},{7,3},{10,6},{11,7},{14,10},{15,11},... | collective-permute-start | bytes 1179656 | tf_op jit(solution)/shard_map/ppermute | solution.py:282
  82.0 11.6 %collective-permute-start.17 = (bf16[6,64,512]{2,1,0:T(8,128)(2,1)S(1)}, bf16[6,64,512]{2,1,0:T(8,128)(2,1)S(1)}, u32[]{:S(2)}, u32[]{:S(2)}) collective-permute-start(bf16[6,64,512]{2,1,0:T(8,128)(2,1)S(1)} %collective-permute-done.16), channel_id=1, source_target_pairs={{0,1},{1,0},{2,3},{3,2},{4,5},{5,4},{6,7},{7,6},{8,9},{9,8},{10,11... | collective-permute-start | bytes 1179656 | tf_op jit(solution)/shard_map/ppermute | solution.py:285
  82.0 12.1 %collective-permute-start.19 = (bf16[6,64,512]{2,1,0:T(8,128)(2,1)S(1)}, bf16[6,64,512]{2,1,0:T(8,128)(2,1)S(1)}, u32[]{:S(2)}, u32[]{:S(2)}) collective-permute-start(bf16[6,64,512]{2,1,0:T(8,128)(2,1)S(1)} %collective-permute-done.18), channel_id=1, source_target_pairs={{0,1},{1,0},{2,3},{3,2},{4,5},{5,4},{6,7},{7,6},{8,9},{9,8},{10,11... | collective-permute-start | bytes 1179656 | tf_op jit(solution)/shard_map/ppermute | solution.py:285
  91.5 9.7 %collective-permute-start.24 = (bf16[6,64,512]{2,1,0:T(8,128)(2,1)S(1)}, bf16[6,64,512]{2,1,0:T(8,128)(2,1)S(1)}, u32[]{:S(2)}, u32[]{:S(2)}) collective-permute-start(bf16[6,64,512]{2,1,0:T(8,128)(2,1)S(1)} %collective-permute-done.20), channel_id=1, source_target_pairs={{0,2},{1,3},{2,6},{3,7},{6,10},{7,11},{10,14},{11,15},{14,12},{15,... | collective-permute-start | bytes 1179656 | tf_op jit(solution)/shard_map/ppermute | solution.py:282
  92.2 9.7 %collective-permute-start.26 = (bf16[6,64,512]{2,1,0:T(8,128)(2,1)S(1)}, bf16[6,64,512]{2,1,0:T(8,128)(2,1)S(1)}, u32[]{:S(2)}, u32[]{:S(2)}) collective-permute-start(bf16[6,64,512]{2,1,0:T(8,128)(2,1)S(1)} %collective-permute-done.22), channel_id=1, source_target_pairs={{0,4},{1,5},{2,0},{3,1},{6,2},{7,3},{10,6},{11,7},{14,10},{15,11},... | collective-permute-start | bytes 1179656 | tf_op jit(solution)/shard_map/ppermute | solution.py:282
  93.5 9.9 %collective-permute-start.21 = (bf16[6,64,512]{2,1,0:T(8,128)(2,1)S(1)}, bf16[6,64,512]{2,1,0:T(8,128)(2,1)S(1)}, u32[]{:S(2)}, u32[]{:S(2)}) collective-permute-start(bf16[6,64,512]{2,1,0:T(8,128)(2,1)S(1)} %collective-permute-done.20), channel_id=1, source_target_pairs={{0,1},{1,0},{2,3},{3,2},{4,5},{5,4},{6,7},{7,6},{8,9},{9,8},{10,11... | collective-permute-start | bytes 1179656 | tf_op jit(solution)/shard_map/ppermute | solution.py:285
  93.5 10.4 %collective-permute-start.23 = (bf16[6,64,512]{2,1,0:T(8,128)(2,1)S(1)}, bf16[6,64,512]{2,1,0:T(8,128)(2,1)S(1)}, u32[]{:S(2)}, u32[]{:S(2)}) collective-permute-start(bf16[6,64,512]{2,1,0:T(8,128)(2,1)S(1)} %collective-permute-done.22), channel_id=1, source_target_pairs={{0,1},{1,0},{2,3},{3,2},{4,5},{5,4},{6,7},{7,6},{8,9},{9,8},{10,11... | collective-permute-start | bytes 1179656 | tf_op jit(solution)/shard_map/ppermute | solution.py:285
  101.2 5.7 %collective-permute-start.28 = (bf16[6,32,512]{2,1,0:T(8,128)(2,1)S(1)}, bf16[6,32,512]{2,1,0:T(8,128)(2,1)S(1)}, u32[]{:S(2)}, u32[]{:S(2)}) collective-permute-start(bf16[6,32,512]{2,1,0:T(8,128)(2,1)S(1)} %slice.92), channel_id=1, source_target_pairs={{0,2},{1,3},{2,6},{3,7},{6,10},{7,11},{10,14},{11,15},{14,12},{15,... | collective-permute-start | bytes 589832 | tf_op jit(solution)/shard_map/ppermute | solution.py:282
  101.9 5.7 %collective-permute-start.29 = (bf16[6,32,512]{2,1,0:T(8,128)(2,1)S(1)}, bf16[6,32,512]{2,1,0:T(8,128)(2,1)S(1)}, u32[]{:S(2)}, u32[]{:S(2)}) collective-permute-start(bf16[6,32,512]{2,1,0:T(8,128)(2,1)S(1)} %slice.93), channel_id=1, source_target_pairs={{0,4},{1,5},{2,0},{3,1},{6,2},{7,3},{10,6},{11,7},{14,10},{15,11},... | collective-permute-start | bytes 589832 | tf_op jit(solution)/shard_map/ppermute | solution.py:282
  103.4 4.3 %collective-permute-start.25 = (bf16[6,64,512]{2,1,0:T(8,128)(2,1)S(1)}, bf16[6,64,512]{2,1,0:T(8,128)(2,1)S(1)}, u32[]{:S(2)}, u32[]{:S(2)}) collective-permute-start(bf16[6,64,512]{2,1,0:T(8,128)(2,1)S(1)} %collective-permute-done.24), channel_id=1, source_target_pairs={{0,1},{1,0},{2,3},{3,2},{4,5},{5,4},{6,7},{7,6},{8,9},{9,8},{10,11... | collective-permute-start | bytes 1179656 | tf_op jit(solution)/shard_map/ppermute | solution.py:285
  103.4 4.4 %collective-permute-start.27 = (bf16[6,64,512]{2,1,0:T(8,128)(2,1)S(1)}, bf16[6,64,512]{2,1,0:T(8,128)(2,1)S(1)}, u32[]{:S(2)}, u32[]{:S(2)}) collective-permute-start(bf16[6,64,512]{2,1,0:T(8,128)(2,1)S(1)} %collective-permute-done.26), channel_id=1, source_target_pairs={{0,1},{1,0},{2,3},{3,2},{4,5},{5,4},{6,7},{7,6},{8,9},{9,8},{10,11... | collective-permute-start | bytes 1179656 | tf_op jit(solution)/shard_map/ppermute | solution.py:285
  107.7 1.8 %collective-permute-start.30 = (bf16[6,64,512]{2,1,0:T(8,128)(2,1)S(1)}, bf16[6,64,512]{2,1,0:T(8,128)(2,1)S(1)}, u32[]{:S(2)}, u32[]{:S(2)}) collective-permute-start(bf16[6,64,512]{2,1,0:T(8,128)(2,1)S(1)} %constant_dynamic-update-slice_fusion), channel_id=1, source_target_pairs={{0,1},{1,0},{2,3},{3,2},{4,5},{5,4},{6,7},{7,6},{8,9},{9,8},{10,11... | collective-permute-start | bytes 1179656 | tf_op jit(solution)/shard_map/ppermute | solution.py:285
  113.2 5.3 %copy-start.2 = (bf16[2,3,512,256]{3,2,1,0:T(8,128)(2,1)S(1)}, bf16[2,3,512,256]{3,2,1,0:T(8,128)(2,1)}, u32[]{:S(2)}) copy-start(bf16[2,3,512,256]{3,2,1,0:T(8,128)(2,1)} %get-tuple-element.49.far_ref) | copy-start | bytes 4718596
  113.2 5.3 %copy-start.3 = (bf16[2,3,384,256]{3,2,1,0:T(8,128)(2,1)S(1)}, bf16[2,3,384,256]{3,2,1,0:T(8,128)(2,1)}, u32[]{:S(2)}) copy-start(bf16[2,3,384,256]{3,2,1,0:T(8,128)(2,1)} %get-tuple-element.48.near_ref) | copy-start | bytes 3538948
